TPU v7x, 32 devices: a whole 2x2x4 slice. The times are simulated.
32 devices in a mesh: ctx: 16 (over z, y, x), width: 2 (over core).
Axes of the slice: x: 2, y: 2, z: 4, core: 2. Of those that a mesh axis runs over, the one named last changes fastest.
Arguments:
- query_proj: bfloat16 [4096, 8192], P('ctx', 'width'), may hold values from -6 to 6
- key_proj: bfloat16 [4096, 8192], P('ctx', 'width'), may hold values from -6 to 6
- value_proj: bfloat16 [4096, 8192], P('ctx', 'width'), may hold values from -6 to 6
- short_kernel: float32 [3, 3, 8192], P(None, None, 'width'), may hold values from -3 to 3
- explicit_taps: bfloat16 [64, 512], P('width'), may hold values from -0.25 to 0.25
- decay_rate: float32 [64, 16], P('width'), may hold values from 0 to 1, as said below
- residues: float32 [64, 16], P('width'), may hold values from -3 to 3
- residual: bfloat16 [4096, 8192], P('ctx', 'width')
- norm_gain: float32 [8192], P('width'), may hold values from 0.5 to 1.5
Outputs:
- block_out: bfloat16 [4096, 8192], P('ctx', 'width')
- normed: bfloat16 [4096, 8192], P('ctx', 'width')
Inputs may be any that keep to these rules, and one draw needn't show every extreme that they name: `decay_rate`: every decay rate is positive.
All inputs are finite; a program needn't handle non-finite values.
Results may differ from a plain program's by a relative error of at most 0.008.
Values may be sent and summed in bfloat16 or wider, within the bound.
No kernel may reach another device: no remote copies, remote signals or barrier semaphores. Data moves between devices by JAX's collectives and lax.ppermute only.
A program may use at most 128 MiB of HBM per device.

v0:
```python
import math

import jax
import jax.numpy as jnp
from jax import lax
from jax.sharding import PartitionSpec as P

HIGHEST = lax.Precision.HIGHEST


def passed_along(array, axis, by):
    length = lax.axis_size(axis)
    pairs = [(i, i + by) for i in range(length) if 0 <= i + by < length]
    return lax.ppermute(array, axis, pairs)


def shorten(rows, tail_rows, kern):
    joined = jnp.concatenate([tail_rows, rows], axis=0).astype(jnp.float32)
    return kern[0] * joined[2:] + kern[1] * joined[1:-1] + kern[2] * joined[:-2]


def toeplitz(padded, offset, length):
    window = lax.slice_in_dim(padded, offset * length + 1, offset * length + 1 + 2 * length, axis=1)
    rolled = jnp.roll(window[:, ::-1], -length, axis=1)
    flattened = jnp.tile(rolled, (1, length))[:, : length * (2 * length - 1)]
    return flattened.reshape(padded.shape[0], length, 2 * length - 1)[:, :, :length]


def split_parts(table):
    upper = table.astype(jnp.bfloat16)
    lower = (table - upper.astype(jnp.float32)).astype(jnp.bfloat16)
    return (upper, lower)


def two_pass(form, table, data):
    upper, lower = split_parts(table)
    first = jnp.einsum(form, upper, data, preferred_element_type=jnp.float32)
    return first + jnp.einsum(form, lower, data, preferred_element_type=jnp.float32)


def body(
    query_proj,
    key_proj,
    value_proj,
    short_kernel,
    explicit_taps,
    decay_rate,
    residues,
    residual,
    norm_gain,
):
    length = query_proj.shape[0]
    channels = query_proj.shape[1]
    group_count = explicit_taps.shape[0]
    group_size = channels // group_count
    span_count = explicit_taps.shape[1] // length
    mode_count = decay_rate.shape[1]
    tails = passed_along(
        (query_proj[length - 2 :], key_proj[length - 2 :], value_proj[length - 2 :]), "ctx", 1
    )
    query_f = shorten(query_proj, tails[0], short_kernel[0])
    key_f = shorten(key_proj, tails[1], short_kernel[1])
    value_f = shorten(value_proj, tails[2], short_kernel[2])
    mixer_input = (key_f * value_f).astype(jnp.bfloat16)
    padded_taps = jnp.pad(explicit_taps, ((0, 0), (length, length + 1)))

    def near_term(source, offset):
        matrix = toeplitz(padded_taps, offset, length)
        return jnp.einsum(
            "gts,sgc->tgc",
            matrix,
            source.reshape(length, group_count, group_size),
            preferred_element_type=jnp.float32,
        )

    explicit_part = near_term(mixer_input, 0)
    for offset in range(1, span_count + 1):
        source = passed_along(mixer_input, "ctx", offset)
        explicit_part = explicit_part + near_term(source, offset)
    weight = residues * jnp.sqrt(-jnp.expm1(-2.0 * decay_rate))
    block_len = math.gcd(length, 128)
    block_count = length // block_len
    positions = jnp.arange(block_len).astype(jnp.float32)
    lag_grid = positions[:, None] - positions[None, :]
    causal = lag_grid >= 0.0
    decay_grid = jnp.exp(-decay_rate[:, :, None, None] * jnp.maximum(lag_grid, 0.0)[None, None])
    inner_taps = jnp.where(
        causal[None], jnp.einsum("gm,gmts->gts", weight, decay_grid, precision=HIGHEST), 0.0
    )
    blocked = mixer_input.reshape(block_count, block_len, group_count, group_size)
    near_modal = two_pass("gts,jsgc->jtgc", inner_taps, blocked)
    to_end = jnp.exp(-decay_rate[:, :, None] * (block_len - 1.0 - positions)[None, None, :])
    summary = two_pass("gms,jsgc->jmgc", to_end, blocked)
    per_block = jnp.transpose(jnp.exp(-decay_rate * block_len))[:, :, None]

    def advance(carried, summary_row):
        return (per_block * carried + summary_row, carried)

    final_state, before = lax.scan(
        advance, jnp.zeros((mode_count, group_count, group_size), jnp.float32), summary
    )
    per_device = jnp.transpose(jnp.exp(-decay_rate * length))[:, :, None]

    def relay(step_index, state_pair):
        incoming_state = passed_along(state_pair[1], "ctx", 1)
        return (incoming_state, per_device * incoming_state + final_state)

    incoming, unused_state = lax.fori_loop(
        0, lax.axis_size("ctx") - 1, relay, (jnp.zeros_like(final_state), final_state)
    )
    starts = jnp.arange(block_count).astype(jnp.float32) * block_len
    lead_decay = jnp.exp(-jnp.transpose(decay_rate)[None, :, :, None] * starts[:, None, None, None])
    entering = lead_decay * incoming[None] + before
    out_decay = weight[None] * jnp.exp(-decay_rate[None] * (positions + 1.0)[:, None, None])
    far_modal = jnp.einsum("tgm,jmgc->jtgc", out_decay, entering, precision=HIGHEST)
    modal_part = (near_modal + far_modal).reshape(length, group_count, group_size)
    filtered = (explicit_part + modal_part).reshape(length, channels)
    block_out = (residual.astype(jnp.float32) + query_f * filtered).astype(jnp.bfloat16)
    out_values = block_out.astype(jnp.float32)
    squares_total = lax.psum(jnp.sum(out_values * out_values, axis=1), "width")
    mean_sq = squares_total / (channels * lax.axis_size("width"))
    normed = (out_values * lax.rsqrt(mean_sq + 1e-05)[:, None] * norm_gain[None, :]).astype(
        jnp.bfloat16
    )
    return (block_out, normed)


def solution(mesh):
    return jax.shard_map(
        body,
        mesh=mesh,
        in_specs=(
            P("ctx", "width"),
            P("ctx", "width"),
            P("ctx", "width"),
            P(None, None, "width"),
            P("width", None),
            P("width", None),
            P("width", None),
            P("ctx", "width"),
            P("width"),
        ),
        out_specs=(P("ctx", "width"), P("ctx", "width")),
        check_vma=False,
    )
```

profile of v0, /device:TPU:25, one launch (start us, length us, event | category | flops | bytes accessed | tf_op | source)
XLA Modules:
  0.0 560.2 jit_solution(13094485573281547618)
XLA Ops:
  17.0 11.4 %multiply_exponential_fusion = f32[32,16,128,128]{3,2,1,0:T(8,128)} fusion(f32[128,128]{1,0:T(8,128)S(1)} %subtract_maximum_fusion, f32[32,16]{1,0:T(8,128)S(1)} %copy.29), kind=kLoop, calls=%fused_computation.7 | loop fusion | flops 8388608 | bytes 33622016 | tf_op jit(solution)/shard_map/exp | solution.py:86
  28.5 46.1 %fusion.1 = f32[32,1,128,128]{3,1,2,0:T(1,128)} fusion(f32[32,16,1,1]{1,2,3,0:T(1,128)S(1)} %copy.41, f32[32,16,128,128]{3,2,1,0:T(8,128)} %multiply_exponential_fusion), kind=kOutput, calls=%fused_computation.5 | convolution fusion | flops 100663296 | bytes 35653632 | tf_op jit(solution)/shard_map/gm,gmts->gts/dot_general | solution.py:88
  79.0 11.4 %copy.53 = bf16[4,8,256,512]{3,1,2,0:T(8,128)(2,1)} copy(bf16[4,8,256,512]{3,2,1,0:T(8,128)(2,1)} %bitcast.91) | data formatting | bytes 16777216
  90.5 7.1 %slice.183 = bf16[32,130816]{1,0:T(8,128)(2,1)} slice(bf16[32,131072]{1,0:T(8,128)(2,1)} %bitcast.94), slice={[0:32], [0:130816]} | slice | bytes 16744448 | tf_op jit(solution)/shard_map/slice | solution.py:25
  97.6 19.9 %reshape.163 = bf16[32,256,511]{2,1,0:T(8,128)(2,1)} reshape(bf16[32,130816]{1,0:T(8,128)(2,1)} %slice.183) | data formatting | bytes 16744448 | tf_op jit(solution)/shard_map/reshape | solution.py:26
  121.4 11.4 %copy.52 = bf16[4,8,256,512]{3,1,2,0:T(8,128)(2,1)} copy(bf16[4,8,256,512]{3,2,1,0:T(8,128)(2,1)} %bitcast.92) | data formatting | bytes 16777216
  132.8 7.1 %slice.181 = bf16[32,130816]{1,0:T(8,128)(2,1)} slice(bf16[32,131072]{1,0:T(8,128)(2,1)} %bitcast.95), slice={[0:32], [0:130816]} | slice | bytes 16744448 | tf_op jit(solution)/shard_map/slice | solution.py:25
  140.0 19.7 %reshape.161 = bf16[32,256,511]{2,1,0:T(8,128)(2,1)} reshape(bf16[32,130816]{1,0:T(8,128)(2,1)} %slice.181) | data formatting | bytes 16744448 | tf_op jit(solution)/shard_map/reshape | solution.py:26
  163.6 11.4 %copy.54 = bf16[4,8,256,512]{3,1,2,0:T(8,128)(2,1)} copy(bf16[4,8,256,512]{3,2,1,0:T(8,128)(2,1)} %bitcast.93) | data formatting | bytes 16777216
  175.0 7.1 %slice.185 = bf16[32,130816]{1,0:T(8,128)(2,1)} slice(bf16[32,131072]{1,0:T(8,128)(2,1)} %bitcast.96), slice={[0:32], [0:130816]} | slice | bytes 16744448 | tf_op jit(solution)/shard_map/slice | solution.py:25
  182.1 19.6 %reshape.165 = bf16[32,256,511]{2,1,0:T(8,128)(2,1)} reshape(bf16[32,130816]{1,0:T(8,128)(2,1)} %slice.185) | data formatting | bytes 16744448 | tf_op jit(solution)/shard_map/reshape | solution.py:26
  221.1 259.2 %while.25 = (s32[]{:T(128)}, f32[16,32,128]{2,1,0:T(8,128)}, f32[16,32,128]{2,1,0:T(8,128)S(1)}, f32[16,32,1]{1,0,2:T(8,128)S(1)}, f32[16,32,128]{2,1,0:T(8,128)S(1)}, /*index=5*/s32[]{:T(128)}) while((s32[]{:T(128)}, f32[16,32,128]{2,1,0:T(8,128)}, f32[16,32,128]{2,1,0:T(8,128)S(1)}, f32[16,32,1]{1,0,2:T(8,128)S(1)}, ...), condition=%wide.region_3.4_spmd, body=%wide.region_2.3_spmd.sunk | while | flops 131074 | bytes 2885769 | solution.py:108
  223.0 113.6 %collective-permute-done = f32[16,32,128]{2,1,0:T(8,128)S(1)} collective-permute-done((f32[16,32,128]{2,1,0:T(8,128)S(1)}, f32[16,32,128]{2,1,0:T(8,128)S(1)}, u32[]{:S(2)}, u32[]{:S(2)}) %collective-permute-start) | collective-permute-done | bytes 262176 | tf_op jit(solution)/shard_map/while/body/eval_jaxpr/ppermute | solution.py:14
  339.2 7.0 %collective-permute-done = f32[16,32,128]{2,1,0:T(8,128)S(1)} collective-permute-done((f32[16,32,128]{2,1,0:T(8,128)S(1)}, f32[16,32,128]{2,1,0:T(8,128)S(1)}, u32[]{:S(2)}, u32[]{:S(2)}) %collective-permute-start) | collective-permute-done | bytes 262176 | tf_op jit(solution)/shard_map/while/body/eval_jaxpr/ppermute | solution.py:14
  348.8 7.0 %collective-permute-done = f32[16,32,128]{2,1,0:T(8,128)S(1)} collective-permute-done((f32[16,32,128]{2,1,0:T(8,128)S(1)}, f32[16,32,128]{2,1,0:T(8,128)S(1)}, u32[]{:S(2)}, u32[]{:S(2)}) %collective-permute-start) | collective-permute-done | bytes 262176 | tf_op jit(solution)/shard_map/while/body/eval_jaxpr/ppermute | solution.py:14
  358.4 7.0 %collective-permute-done = f32[16,32,128]{2,1,0:T(8,128)S(1)} collective-permute-done((f32[16,32,128]{2,1,0:T(8,128)S(1)}, f32[16,32,128]{2,1,0:T(8,128)S(1)}, u32[]{:S(2)}, u32[]{:S(2)}) %collective-permute-start) | collective-permute-done | bytes 262176 | tf_op jit(solution)/shard_map/while/body/eval_jaxpr/ppermute | solution.py:14
  368.0 7.0 %collective-permute-done = f32[16,32,128]{2,1,0:T(8,128)S(1)} collective-permute-done((f32[16,32,128]{2,1,0:T(8,128)S(1)}, f32[16,32,128]{2,1,0:T(8,128)S(1)}, u32[]{:S(2)}, u32[]{:S(2)}) %collective-permute-start) | collective-permute-done | bytes 262176 | tf_op jit(solution)/shard_map/while/body/eval_jaxpr/ppermute | solution.py:14
  377.6 7.0 %collective-permute-done = f32[16,32,128]{2,1,0:T(8,128)S(1)} collective-permute-done((f32[16,32,128]{2,1,0:T(8,128)S(1)}, f32[16,32,128]{2,1,0:T(8,128)S(1)}, u32[]{:S(2)}, u32[]{:S(2)}) %collective-permute-start) | collective-permute-done | bytes 262176 | tf_op jit(solution)/shard_map/while/body/eval_jaxpr/ppermute | solution.py:14
  387.2 7.7 %collective-permute-done = f32[16,32,128]{2,1,0:T(8,128)S(1)} collective-permute-done((f32[16,32,128]{2,1,0:T(8,128)S(1)}, f32[16,32,128]{2,1,0:T(8,128)S(1)}, u32[]{:S(2)}, u32[]{:S(2)}) %collective-permute-start) | collective-permute-done | bytes 262176 | tf_op jit(solution)/shard_map/while/body/eval_jaxpr/ppermute | solution.py:14
  397.5 8.8 %collective-permute-done = f32[16,32,128]{2,1,0:T(8,128)S(1)} collective-permute-done((f32[16,32,128]{2,1,0:T(8,128)S(1)}, f32[16,32,128]{2,1,0:T(8,128)S(1)}, u32[]{:S(2)}, u32[]{:S(2)}) %collective-permute-start) | collective-permute-done | bytes 262176 | tf_op jit(solution)/shard_map/while/body/eval_jaxpr/ppermute | solution.py:14
  408.9 10.0 %collective-permute-done = f32[16,32,128]{2,1,0:T(8,128)S(1)} collective-permute-done((f32[16,32,128]{2,1,0:T(8,128)S(1)}, f32[16,32,128]{2,1,0:T(8,128)S(1)}, u32[]{:S(2)}, u32[]{:S(2)}) %collective-permute-start) | collective-permute-done | bytes 262176 | tf_op jit(solution)/shard_map/while/body/eval_jaxpr/ppermute | solution.py:14
  421.4 9.1 %collective-permute-done = f32[16,32,128]{2,1,0:T(8,128)S(1)} collective-permute-done((f32[16,32,128]{2,1,0:T(8,128)S(1)}, f32[16,32,128]{2,1,0:T(8,128)S(1)}, u32[]{:S(2)}, u32[]{:S(2)}) %collective-permute-start) | collective-permute-done | bytes 262176 | tf_op jit(solution)/shard_map/while/body/eval_jaxpr/ppermute | solution.py:14
  433.1 8.2 %collective-permute-done = f32[16,32,128]{2,1,0:T(8,128)S(1)} collective-permute-done((f32[16,32,128]{2,1,0:T(8,128)S(1)}, f32[16,32,128]{2,1,0:T(8,128)S(1)}, u32[]{:S(2)}, u32[]{:S(2)}) %collective-permute-start) | collective-permute-done | bytes 262176 | tf_op jit(solution)/shard_map/while/body/eval_jaxpr/ppermute | solution.py:14
  443.9 7.0 %collective-permute-done = f32[16,32,128]{2,1,0:T(8,128)S(1)} collective-permute-done((f32[16,32,128]{2,1,0:T(8,128)S(1)}, f32[16,32,128]{2,1,0:T(8,128)S(1)}, u32[]{:S(2)}, u32[]{:S(2)}) %collective-permute-start) | collective-permute-done | bytes 262176 | tf_op jit(solution)/shard_map/while/body/eval_jaxpr/ppermute | solution.py:14
  453.5 7.0 %collective-permute-done = f32[16,32,128]{2,1,0:T(8,128)S(1)} collective-permute-done((f32[16,32,128]{2,1,0:T(8,128)S(1)}, f32[16,32,128]{2,1,0:T(8,128)S(1)}, u32[]{:S(2)}, u32[]{:S(2)}) %collective-permute-start) | collective-permute-done | bytes 262176 | tf_op jit(solution)/shard_map/while/body/eval_jaxpr/ppermute | solution.py:14
  463.1 7.0 %collective-permute-done = f32[16,32,128]{2,1,0:T(8,128)S(1)} collective-permute-done((f32[16,32,128]{2,1,0:T(8,128)S(1)}, f32[16,32,128]{2,1,0:T(8,128)S(1)}, u32[]{:S(2)}, u32[]{:S(2)}) %collective-permute-start) | collective-permute-done | bytes 262176 | tf_op jit(solution)/shard_map/while/body/eval_jaxpr/ppermute | solution.py:14
  472.7 7.0 %collective-permute-done = f32[16,32,128]{2,1,0:T(8,128)S(1)} collective-permute-done((f32[16,32,128]{2,1,0:T(8,128)S(1)}, f32[16,32,128]{2,1,0:T(8,128)S(1)}, u32[]{:S(2)}, u32[]{:S(2)}) %collective-permute-start) | collective-permute-done | bytes 262176 | tf_op jit(solution)/shard_map/while/body/eval_jaxpr/ppermute | solution.py:14
  494.5 5.8 %copy.50 = f32[256,32,128]{0,2,1:T(8,128)} copy(f32[256,32,128]{2,0,1:T(8,128)} %bitcast.101) | data formatting | bytes 8388608 | tf_op jit(solution)/shard_map/reshape | solution.py:116
  515.1 9.4 %bitcast_add_fusion = f32[256,32,128]{0,2,1:T(8,128)} fusion(f32[256,32,128]{0,2,1:T(8,128)} %copy.50, f32[32,128,256]{2,1,0:T(8,128)} %fusion.10, f32[32,128,256]{2,1,0:T(8,128)} %fusion.8, bf16[256,32,128]{0,2,1:T(8,128)(2,1)S(1)} %bitcast.105, bf16[32,256,511]{2,1,0:T(8,128)(2,1)} %reshape.165), kind=kOutput, calls=%fused_computation.39 | convolution fusion | flops 540016640 | bytes 23068672 | tf_op jit(solution)/shard_map/gts,sgc->tgc/dot_general | solution.py:69
  524.5 5.6 %copy.40 = f32[256,4096]{1,0:T(8,128)} copy(f32[256,4096]{0,1:T(8,128)} %bitcast.102) | data formatting | bytes 8388608 | tf_op jit(solution)/shard_map/reshape | solution.py:117
  530.2 7.9 %fusion.3 = (f32[256]{0:T(256)S(1)}, bf16[256,4096]{1,0:T(8,128)(2,1)S(1)}) fusion(f32[256,4096]{1,0:T(8,128)} %copy.40, f32[258,4096]{1,0:T(8,128)} %maximum_convert_fusion, f32[4096]{0:T(1024)S(1)} %bitcast.110, f32[4096]{0:T(1024)S(1)} %bitcast.111, f32[4096]{0:T(1024)S(1)} %bitcast.109, bf16[256,4096]{1,0:T(8,128)(2,1)} %param.20), kind=kLoop, calls=%fused_computation.10 | loop fusion | flops 12582656 | bytes 21021696 | tf_op jit(solution)/shard_map/reduce_sum | solution.py:120
  538.0 19.8 %psum.7 = f32[256]{0:T(256)S(1)} all-reduce(f32[256]{0:T(256)S(1)} %get-tuple-element.107), channel_id=1, replica_groups=mesh['ctx'=16,'width'=2] {'width'}, use_global_device_ids=true, to_apply=%region_5.6 | all-reduce | flops 256 | bytes 2048 | tf_op jit(solution)/shard_map/psum | solution.py:120
  (145 shorter events, 118.1 us)
Async XLA Ops:
  1.5 200.2 %collective-permute-start.2 = (bf16[2,4096]{1,0:T(2,128)(2,1)S(1)}, bf16[2,4096]{1,0:T(2,128)(2,1)S(1)}, u32[]{:S(2)}, u32[]{:S(2)}) collective-permute-start(bf16[2,4096]{1,0:T(2,128)(2,1)S(1)} %slice.147), channel_id=1, source_target_pairs={{0,2},{2,4},{4,6},{6,8},{8,10},{10,12},{12,14},{14,16},{16,18},{18... | collective-permute-start | bytes 49160 | tf_op jit(solution)/shard_map/ppermute | solution.py:14
  5.5 196.9 %collective-permute-start.3 = (bf16[2,4096]{1,0:T(2,128)(2,1)S(1)}, bf16[2,4096]{1,0:T(2,128)(2,1)S(1)}, u32[]{:S(2)}, u32[]{:S(2)}) collective-permute-start(bf16[2,4096]{1,0:T(2,128)(2,1)S(1)} %slice.154), channel_id=1, source_target_pairs={{0,2},{2,4},{4,6},{6,8},{8,10},{10,12},{12,14},{14,16},{16,18},{18... | collective-permute-start | bytes 49160 | tf_op jit(solution)/shard_map/ppermute | solution.py:14
  10.1 490.2 %collective-permute-start.1 = (bf16[2,4096]{1,0:T(2,128)(2,1)}, bf16[2,4096]{1,0:T(2,128)(2,1)S(1)}, u32[]{:S(2)}, u32[]{:S(2)}) collective-permute-start(bf16[2,4096]{1,0:T(2,128)(2,1)} %slice.140), channel_id=1, source_target_pairs={{0,2},{2,4},{4,6},{6,8},{8,10},{10,12},{12,14},{14,16},{16,18},{18... | collective-permute-start | bytes 49160 | tf_op jit(solution)/shard_map/ppermute | solution.py:14
  13.2 204.4 %copy-start.8 = (f32[128]{0:T(128)}, f32[128]{0:T(128)S(1)}, u32[]{:S(2)}) copy-start(f32[128]{0:T(128)S(1)} %broadcast_subtract_fusion) | copy-start | bytes 1540
  182.1 19.6 %copy-start.4 = (bf16[256,4096]{1,0:T(8,128)(2,1)S(1)}, bf16[256,4096]{1,0:T(8,128)(2,1)}, u32[]{:S(2)}) copy-start(bf16[256,4096]{1,0:T(8,128)(2,1)} %param.14) | copy-start | bytes 6291460
  201.7 1.6 copy-start.5
  207.6 295.3 %collective-permute-start.4 = (bf16[256,4096]{1,0:T(8,128)(2,1)}, bf16[256,4096]{1,0:T(8,128)(2,1)}, u32[]{:S(2)}, u32[]{:S(2)}) collective-permute-start(bf16[256,4096]{1,0:T(8,128)(2,1)} %fusion.14), channel_id=1, source_target_pairs={{0,2},{2,4},{4,6},{6,8},{8,10},{10,12},{12,14},{14,16},{16,18},{18... | collective-permute-start | bytes 6291464 | tf_op jit(solution)/shard_map/ppermute | solution.py:14
  213.6 298.2 %collective-permute-start.5 = (bf16[256,4096]{1,0:T(8,128)(2,1)}, bf16[256,4096]{1,0:T(8,128)(2,1)}, u32[]{:S(2)}, u32[]{:S(2)}) collective-permute-start(bf16[256,4096]{1,0:T(8,128)(2,1)} %fusion.14), channel_id=1, source_target_pairs={{0,4},{2,6},{4,8},{6,10},{8,12},{10,14},{12,16},{14,18},{16,20},{1... | collective-permute-start | bytes 6291464 | tf_op jit(solution)/shard_map/ppermute | solution.py:14
  221.1 260.6 %copy-start.9 = (f32[128]{0:T(128)S(1)}, f32[128]{0:T(128)}, u32[]{:S(2)}) copy-start(f32[128]{0:T(128)} %broadcast_add_fusion) | copy-start | bytes 1540
  221.1 115.5 %collective-permute-start = (f32[16,32,128]{2,1,0:T(8,128)S(1)}, f32[16,32,128]{2,1,0:T(8,128)S(1)}, u32[]{:S(2)}, u32[]{:S(2)}) collective-permute-start(f32[16,32,128]{2,1,0:T(8,128)S(1)} %get-tuple-element.218), channel_id=1, source_target_pairs={{0,2},{2,4},{4,6},{6,8},{8,10},{10,12},{12,14},{14,16},{16,18},{18... | collective-permute-start | bytes 786440 | tf_op jit(solution)/shard_map/while/body/eval_jaxpr/ppermute | solution.py:14
  336.6 0.7 copy-start.1
  337.3 8.9 %collective-permute-start = (f32[16,32,128]{2,1,0:T(8,128)S(1)}, f32[16,32,128]{2,1,0:T(8,128)S(1)}, u32[]{:S(2)}, u32[]{:S(2)}) collective-permute-start(f32[16,32,128]{2,1,0:T(8,128)S(1)} %get-tuple-element.218), channel_id=1, source_target_pairs={{0,2},{2,4},{4,6},{6,8},{8,10},{10,12},{12,14},{14,16},{16,18},{18... | collective-permute-start | bytes 786440 | tf_op jit(solution)/shard_map/while/body/eval_jaxpr/ppermute | solution.py:14
  346.9 8.9 %collective-permute-start = (f32[16,32,128]{2,1,0:T(8,128)S(1)}, f32[16,32,128]{2,1,0:T(8,128)S(1)}, u32[]{:S(2)}, u32[]{:S(2)}) collective-permute-start(f32[16,32,128]{2,1,0:T(8,128)S(1)} %get-tuple-element.218), channel_id=1, source_target_pairs={{0,2},{2,4},{4,6},{6,8},{8,10},{10,12},{12,14},{14,16},{16,18},{18... | collective-permute-start | bytes 786440 | tf_op jit(solution)/shard_map/while/body/eval_jaxpr/ppermute | solution.py:14
  356.5 8.9 %collective-permute-start = (f32[16,32,128]{2,1,0:T(8,128)S(1)}, f32[16,32,128]{2,1,0:T(8,128)S(1)}, u32[]{:S(2)}, u32[]{:S(2)}) collective-permute-start(f32[16,32,128]{2,1,0:T(8,128)S(1)} %get-tuple-element.218), channel_id=1, source_target_pairs={{0,2},{2,4},{4,6},{6,8},{8,10},{10,12},{12,14},{14,16},{16,18},{18... | collective-permute-start | bytes 786440 | tf_op jit(solution)/shard_map/while/body/eval_jaxpr/ppermute | solution.py:14
  366.1 8.9 %collective-permute-start = (f32[16,32,128]{2,1,0:T(8,128)S(1)}, f32[16,32,128]{2,1,0:T(8,128)S(1)}, u32[]{:S(2)}, u32[]{:S(2)}) collective-permute-start(f32[16,32,128]{2,1,0:T(8,128)S(1)} %get-tuple-element.218), channel_id=1, source_target_pairs={{0,2},{2,4},{4,6},{6,8},{8,10},{10,12},{12,14},{14,16},{16,18},{18... | collective-permute-start | bytes 786440 | tf_op jit(solution)/shard_map/while/body/eval_jaxpr/ppermute | solution.py:14
  375.7 8.9 %collective-permute-start = (f32[16,32,128]{2,1,0:T(8,128)S(1)}, f32[16,32,128]{2,1,0:T(8,128)S(1)}, u32[]{:S(2)}, u32[]{:S(2)}) collective-permute-start(f32[16,32,128]{2,1,0:T(8,128)S(1)} %get-tuple-element.218), channel_id=1, source_target_pairs={{0,2},{2,4},{4,6},{6,8},{8,10},{10,12},{12,14},{14,16},{16,18},{18... | collective-permute-start | bytes 786440 | tf_op jit(solution)/shard_map/while/body/eval_jaxpr/ppermute | solution.py:14
  385.2 9.6 %collective-permute-start = (f32[16,32,128]{2,1,0:T(8,128)S(1)}, f32[16,32,128]{2,1,0:T(8,128)S(1)}, u32[]{:S(2)}, u32[]{:S(2)}) collective-permute-start(f32[16,32,128]{2,1,0:T(8,128)S(1)} %get-tuple-element.218), channel_id=1, source_target_pairs={{0,2},{2,4},{4,6},{6,8},{8,10},{10,12},{12,14},{14,16},{16,18},{18... | collective-permute-start | bytes 786440 | tf_op jit(solution)/shard_map/while/body/eval_jaxpr/ppermute | solution.py:14
  395.6 10.7 %collective-permute-start = (f32[16,32,128]{2,1,0:T(8,128)S(1)}, f32[16,32,128]{2,1,0:T(8,128)S(1)}, u32[]{:S(2)}, u32[]{:S(2)}) collective-permute-start(f32[16,32,128]{2,1,0:T(8,128)S(1)} %get-tuple-element.218), channel_id=1, source_target_pairs={{0,2},{2,4},{4,6},{6,8},{8,10},{10,12},{12,14},{14,16},{16,18},{18... | collective-permute-start | bytes 786440 | tf_op jit(solution)/shard_map/while/body/eval_jaxpr/ppermute | solution.py:14
  406.9 11.9 %collective-permute-start = (f32[16,32,128]{2,1,0:T(8,128)S(1)}, f32[16,32,128]{2,1,0:T(8,128)S(1)}, u32[]{:S(2)}, u32[]{:S(2)}) collective-permute-start(f32[16,32,128]{2,1,0:T(8,128)S(1)} %get-tuple-element.218), channel_id=1, source_target_pairs={{0,2},{2,4},{4,6},{6,8},{8,10},{10,12},{12,14},{14,16},{16,18},{18... | collective-permute-start | bytes 786440 | tf_op jit(solution)/shard_map/while/body/eval_jaxpr/ppermute | solution.py:14
  419.5 11.0 %collective-permute-start = (f32[16,32,128]{2,1,0:T(8,128)S(1)}, f32[16,32,128]{2,1,0:T(8,128)S(1)}, u32[]{:S(2)}, u32[]{:S(2)}) collective-permute-start(f32[16,32,128]{2,1,0:T(8,128)S(1)} %get-tuple-element.218), channel_id=1, source_target_pairs={{0,2},{2,4},{4,6},{6,8},{8,10},{10,12},{12,14},{14,16},{16,18},{18... | collective-permute-start | bytes 786440 | tf_op jit(solution)/shard_map/while/body/eval_jaxpr/ppermute | solution.py:14
  431.2 10.1 %collective-permute-start = (f32[16,32,128]{2,1,0:T(8,128)S(1)}, f32[16,32,128]{2,1,0:T(8,128)S(1)}, u32[]{:S(2)}, u32[]{:S(2)}) collective-permute-start(f32[16,32,128]{2,1,0:T(8,128)S(1)} %get-tuple-element.218), channel_id=1, source_target_pairs={{0,2},{2,4},{4,6},{6,8},{8,10},{10,12},{12,14},{14,16},{16,18},{18... | collective-permute-start | bytes 786440 | tf_op jit(solution)/shard_map/while/body/eval_jaxpr/ppermute | solution.py:14
  442.0 8.9 %collective-permute-start = (f32[16,32,128]{2,1,0:T(8,128)S(1)}, f32[16,32,128]{2,1,0:T(8,128)S(1)}, u32[]{:S(2)}, u32[]{:S(2)}) collective-permute-start(f32[16,32,128]{2,1,0:T(8,128)S(1)} %get-tuple-element.218), channel_id=1, source_target_pairs={{0,2},{2,4},{4,6},{6,8},{8,10},{10,12},{12,14},{14,16},{16,18},{18... | collective-permute-start | bytes 786440 | tf_op jit(solution)/shard_map/while/body/eval_jaxpr/ppermute | solution.py:14
  451.6 8.9 %collective-permute-start = (f32[16,32,128]{2,1,0:T(8,128)S(1)}, f32[16,32,128]{2,1,0:T(8,128)S(1)}, u32[]{:S(2)}, u32[]{:S(2)}) collective-permute-start(f32[16,32,128]{2,1,0:T(8,128)S(1)} %get-tuple-element.218), channel_id=1, source_target_pairs={{0,2},{2,4},{4,6},{6,8},{8,10},{10,12},{12,14},{14,16},{16,18},{18... | collective-permute-start | bytes 786440 | tf_op jit(solution)/shard_map/while/body/eval_jaxpr/ppermute | solution.py:14
  461.1 8.9 %collective-permute-start = (f32[16,32,128]{2,1,0:T(8,128)S(1)}, f32[16,32,128]{2,1,0:T(8,128)S(1)}, u32[]{:S(2)}, u32[]{:S(2)}) collective-permute-start(f32[16,32,128]{2,1,0:T(8,128)S(1)} %get-tuple-element.218), channel_id=1, source_target_pairs={{0,2},{2,4},{4,6},{6,8},{8,10},{10,12},{12,14},{14,16},{16,18},{18... | collective-permute-start | bytes 786440 | tf_op jit(solution)/shard_map/while/body/eval_jaxpr/ppermute | solution.py:14
  470.7 8.9 %collective-permute-start = (f32[16,32,128]{2,1,0:T(8,128)S(1)}, f32[16,32,128]{2,1,0:T(8,128)S(1)}, u32[]{:S(2)}, u32[]{:S(2)}) collective-permute-start(f32[16,32,128]{2,1,0:T(8,128)S(1)} %get-tuple-element.218), channel_id=1, source_target_pairs={{0,2},{2,4},{4,6},{6,8},{8,10},{10,12},{12,14},{14,16},{16,18},{18... | collective-permute-start | bytes 786440 | tf_op jit(solution)/shard_map/while/body/eval_jaxpr/ppermute | solution.py:14
  480.3 5.1 copy-start
  485.4 5.6 slice-start
  486.9 4.1 slice-start.1
  486.9 4.1 copy-start.3
  494.5 5.8 %copy-start.6 = (bf16[256,4096]{1,0:T(8,128)(2,1)S(1)}, bf16[256,4096]{1,0:T(8,128)(2,1)}, u32[]{:S(2)}) copy-start(bf16[256,4096]{1,0:T(8,128)(2,1)} %param.13) | copy-start | bytes 6291460
  530.2 27.7 %copy-start.7 = (f32[4096]{0:T(1024)S(1)}, f32[4096]{0:T(1024)}, u32[]{:S(2)}) copy-start(f32[4096]{0:T(1024)} %param.21) | copy-start | bytes 49156
  538.0 21.8 %copy-start.2 = (bf16[256,4096]{1,0:T(8,128)(2,1)}, bf16[256,4096]{1,0:T(8,128)(2,1)S(1)}, u32[]{:S(2)}) copy-start(bf16[256,4096]{1,0:T(8,128)(2,1)S(1)} %get-tuple-element.108) | copy-start | bytes 6291460
  (14 other events, 9.6 us)
where the time goes:
time: 570 us; the launch traced here: 560 us
  waiting for transfers between devices  220 us (39%)
  local copies, waits for them, and re-layouts  166 us (29%)
  matrix products  76.6 us (13%)
  starting transfers between devices  41.8 us (7%)
  other arithmetic  34 us (6%)
  blocking collectives  19.8 us (3%)
    ppermute x20, waiting for transfers between devices, passed_along(): return lax.ppermute(array, axis, pairs)  220 us
    reshape x3, local copies, waits for them, and re-layouts, toeplitz(): flattened.reshape(padded.shape[0], length, 2 * length - 1)[:, :, :length]  59.2 us
    dot_general x1, matrix products, body(): jnp.einsum('gm,gmts->gts', weight, decay_grid, precision=HIGHEST)  46.1 us
    ppermute x20, starting transfers between devices, passed_along(): return lax.ppermute(array, axis, pairs)  41.8 us
    unnamed x27, local copies, waits for them, and re-layouts  37.3 us
    slice x3, local copies, waits for them, and re-layouts, toeplitz(): flattened = jnp.tile(rolled, (1, length))[:, :length * (2 * length - 1)]  21.4 us
    psum x1, blocking collectives, body(): squares_total = lax.psum(jnp.sum(out_values * out_values, axis=1), 'width')  19.8 us
    dot_general x3, matrix products, near_term(): jnp.einsum('gts,sgc->tgc', matrix, source.reshape(length, group_count, gr...  18.5 us
  transfers between devices with their start and end apart: 20, of which 15 were waited for; matrix products, arithmetic and copies ran while one was open for 43% of the time, Pallas kernels for 0%

commit v1 on v0

v1 whole, which is shorter than its diff:
```python
import jax
import jax.numpy as jnp
from jax import lax
from jax.experimental import pallas as pl
from jax.experimental.pallas import tpu as pltpu
from jax.sharding import PartitionSpec as P

F32 = jnp.float32
BF16 = jnp.bfloat16
LANES = 128


def shifted_pairs(length, by):
    return [(i, i + by) for i in range(length) if i + by < length]


def swap_pairs(length):
    return [(i, i ^ 1) for i in range(length)]


def dot(a, b):
    return jnp.dot(a, b, preferred_element_type=F32)


def split(x):
    hi = x.astype(BF16)
    return hi, (x - hi.astype(F32)).astype(BF16)


def short_filter(ref, tail, kern, lanes):
    rows = ref[:, lanes].astype(F32)
    return (
        kern[0] * rows
        + kern[1] * pltpu.roll(rows, 1, 0)
        + kern[2] * pltpu.roll(rows, 2, 0)
    )


def short_filter_top(ref, tail, kern, lanes):
    rows = ref[0:16, lanes].astype(F32)
    before, last = tail
    place = lax.broadcasted_iota(jnp.int32, rows.shape, 0)
    one = jnp.where(place == 0, last, pltpu.roll(rows, 1, 0))
    two = jnp.where(place == 0, before, jnp.where(place == 1, last, pltpu.roll(rows, 2, 0)))
    return kern[0] * rows + kern[1] * one + kern[2] * two


def mix_kernel(groups, k_ref, v_ref, tail_ref, sk_ref, rate_ref, x_ref, f_ref):
    length = k_ref.shape[0]
    for g in range(groups):
        lanes = slice(g * LANES, (g + 1) * LANES)
        k_kern = [sk_ref[1, j : j + 1, lanes] for j in range(3)]
        v_kern = [sk_ref[2, j : j + 1, lanes] for j in range(3)]
        k_tail = [tail_ref[j : j + 1, lanes] for j in (2, 3)]
        v_tail = [tail_ref[j : j + 1, lanes] for j in (4, 5)]
        x_ref[:, lanes] = (
            short_filter(k_ref, k_tail, k_kern, lanes) * short_filter(v_ref, v_tail, v_kern, lanes)
        ).astype(BF16)
        x_ref[0:16, lanes] = (
            short_filter_top(k_ref, k_tail, k_kern, lanes)
            * short_filter_top(v_ref, v_tail, v_kern, lanes)
        ).astype(BF16)
        rate = rate_ref[:, lanes]
        total = None
        for part in range(length // LANES):
            place = lax.broadcasted_iota(jnp.int32, rate.shape, 1) + part * LANES
            hi, lo = split(jnp.exp(-rate * (length - 1 - place).astype(F32)))
            data = x_ref[part * LANES : (part + 1) * LANES, lanes]
            term = dot(jnp.concatenate([hi, lo], axis=0), data)
            total = term if total is None else total + term
        modes = rate.shape[0]
        f_ref[:, lanes] = total[:modes] + total[modes:]


def table_kernel(
    groups, first_blocks, source_ref, rate_ref, weight_ref, xa_ref, xb_ref, tb_ref, fa_ref, fb_ref
):
    length = xa_ref.shape[0]
    width = source_ref.shape[-1]
    taps = width - LANES
    for g in range(groups):
        lanes = slice(g * LANES, (g + 1) * LANES)
        row = jnp.broadcast_to(source_ref[0, g : g + 1, :], (LANES, width))
        band = pltpu.roll(row, 0, 1, stride=1, stride_axis=0)
        tb_ref[g] = band[:, :taps].astype(BF16)
        rate = rate_ref[:, lanes]
        weight = weight_ref[:, lanes]
        pieces = []
        for part in range(3):
            place = lax.broadcasted_iota(jnp.int32, rate.shape, 1) + part * LANES
            lag = jnp.where(place <= LANES, LANES - place, 4 * LANES - place)
            inside = (place <= LANES) | (place > 2 * LANES)
            value = weight * jnp.exp(-rate * jnp.maximum(lag, 0).astype(F32))
            pieces.append(jnp.sum(jnp.where(inside, value, 0.0), axis=0, keepdims=True))
        modal = jnp.broadcast_to(jnp.concatenate(pieces, axis=1), (LANES, 3 * LANES))
        modal = pltpu.roll(modal, 0, 1, stride=1, stride_axis=0)
        near = band[:, taps - LANES :] + modal[:, : 2 * LANES]
        hi, lo = split(near)

        def apply(x_ref, out_ref):
            top = x_ref[0:LANES, lanes]
            both = x_ref[:, lanes]
            out_ref[0:LANES, lanes] = dot(hi[:, LANES:], top) + dot(lo[:, LANES:], top)
            out_ref[LANES:, lanes] = dot(hi, both) + dot(lo, both)

        @pl.when(pl.program_id(0) < first_blocks)
        def _():
            apply(xa_ref, fa_ref)

        @pl.when(pl.program_id(0) >= first_blocks)
        def _():
            apply(xb_ref, fb_ref)


def lag_one(tb, x):
    top = dot(tb[:, 256:512], x)
    low = dot(tb[:, 128:384], x)
    return top, low


def lag_two(tb, x):
    top = dot(tb[:, 0:256], x)
    low = dot(tb[:, 0:128], x[128:])
    return top, low


def merge_kernel(groups, odd_ref, tb_ref, near_ref, own_ref, fa_ref, send_ref, keep_ref):
    odd = odd_ref[0]

    @pl.when(odd == 1)
    def _():
        send_ref[...] = own_ref[...]
        for g in range(groups):
            lanes = slice(g * LANES, (g + 1) * LANES)
            top, low = lag_one(tb_ref[g], near_ref[:, lanes])
            keep_ref[0:LANES, lanes] = fa_ref[0:LANES, lanes] + top
            keep_ref[LANES:, lanes] = fa_ref[LANES:, lanes] + low

    @pl.when(odd == 0)
    def _():
        keep_ref[...] = fa_ref[...]
        for g in range(groups):
            lanes = slice(g * LANES, (g + 1) * LANES)
            top, low = lag_one(tb_ref[g], near_ref[:, lanes])
            top2, low2 = lag_two(tb_ref[g], own_ref[:, lanes])
            send_ref[0:LANES, lanes] = (top + top2).astype(BF16)
            send_ref[LANES:, lanes] = (low + low2).astype(BF16)


def late_kernel(
    groups,
    first_blocks,
    odd_ref,
    tb_ref,
    keep_ref,
    fb_ref,
    got_ref,
    near_ref,
    far_ref,
    state_ref,
    rate_ref,
    weight_ref,
    q_ref,
    tail_ref,
    sk_ref,
    residual_ref,
    out_ref,
    square_ref,
    acc_ref,
):
    odd = odd_ref[0]
    step = pl.program_id(0)
    length = q_ref.shape[0]

    @pl.when(step == 0)
    def _():
        square_ref[...] = jnp.zeros_like(square_ref)

    for g in range(groups):
        lanes = slice(g * LANES, (g + 1) * LANES)
        tb = tb_ref[g]
        rate = rate_ref[:, lanes]
        weight = weight_ref[:, lanes]
        s_hi, s_lo = split(state_ref[:, lanes])
        state = jnp.concatenate([s_hi, s_lo, s_hi], axis=0)
        for part in range(length // LANES):
            place = lax.broadcasted_iota(jnp.int32, rate.shape, 1) + part * LANES
            o_hi, o_lo = split(weight * jnp.exp(-rate * (place + 1).astype(F32)))
            table = jnp.concatenate([o_hi, o_hi, o_lo], axis=0)
            acc_ref[part * LANES : (part + 1) * LANES, :] = lax.dot_general(
                table, state, (((0,), (0,)), ((), ())), preferred_element_type=F32
            )

        @pl.when((step < first_blocks) & (odd == 1))
        def _():
            top, low = lag_two(tb, got_ref[:, lanes])
            acc_ref[0:LANES] += keep_ref[0:LANES, lanes] + top
            acc_ref[LANES:] += keep_ref[LANES:, lanes] + low

        @pl.when((step < first_blocks) & (odd == 0))
        def _():
            acc_ref[...] += keep_ref[:, lanes] + got_ref[:, lanes].astype(F32)

        @pl.when(step >= first_blocks)
        def _():
            top, low = lag_one(tb, near_ref[:, lanes])
            top2, low2 = lag_two(tb, far_ref[:, lanes])
            acc_ref[0:LANES] += fb_ref[0:LANES, lanes] + top + top2
            acc_ref[LANES:] += fb_ref[LANES:, lanes] + low + low2

        q_kern = [sk_ref[0, j : j + 1, lanes] for j in range(3)]
        tails = [tail_ref[j : j + 1, lanes] for j in (0, 1)]
        query = short_filter(q_ref, tails, q_kern, lanes)
        out = residual_ref[:, lanes].astype(F32) + query * acc_ref[...]
        out_ref[:, lanes] = out.astype(BF16)
        query_top = short_filter_top(q_ref, tails, q_kern, lanes)
        out_top = residual_ref[0:16, lanes].astype(F32) + query_top * acc_ref[0:16]
        out_ref[0:16, lanes] = out_top.astype(BF16)
        rounded = out_ref[:, lanes].astype(F32)
        square_ref[...] += rounded * rounded


def norm_kernel(scale_ref, gain_ref, x_ref, o_ref):
    o_ref[...] = (x_ref[...].astype(F32) * scale_ref[...] * gain_ref[...]).astype(BF16)


def cost(flops, moved):
    return pl.CostEstimate(flops=int(flops), bytes_accessed=int(moved), transcendentals=0)


def body(
    query_proj,
    key_proj,
    value_proj,
    short_kernel,
    explicit_taps,
    decay_rate,
    residues,
    residual,
    norm_gain,
):
    length, channels = query_proj.shape
    group_count, taps = explicit_taps.shape
    modes = decay_rate.shape[1]
    devices = lax.axis_size("ctx")
    per = max(group_count // 8, 1)
    steps = group_count // per
    first = (steps * 3) // 8
    second = steps - first
    lanes = per * LANES
    wide_a = first * lanes
    wide_b = second * lanes
    odd = (lax.axis_index("ctx") % 2).astype(jnp.int32).reshape(1)

    own_tail = jnp.concatenate(
        [query_proj[length - 2 :], key_proj[length - 2 :], value_proj[length - 2 :]], axis=0
    )
    tail = lax.ppermute(own_tail, "ctx", shifted_pairs(devices, 1)).astype(F32)

    weight = residues * jnp.sqrt(-jnp.expm1(-2.0 * decay_rate))
    spread = lambda t: jnp.repeat(t.T, LANES, axis=1)
    rate_c = spread(decay_rate)
    weight_c = spread(weight)
    source = jnp.pad(jnp.flip(explicit_taps, axis=1).astype(F32), ((0, 0), (1, LANES - 1)))
    source = source.reshape(steps, per, taps + LANES)

    smem = pl.BlockSpec(memory_space=pltpu.SMEM)

    def mix(offset, count):
        return pl.pallas_call(
            lambda *refs: mix_kernel(per, *refs),
            grid=(count,),
            in_specs=[
                pl.BlockSpec((length, lanes), lambda s: (0, s + offset)),
                pl.BlockSpec((length, lanes), lambda s: (0, s + offset)),
                pl.BlockSpec((6, lanes), lambda s: (0, s + offset)),
                pl.BlockSpec((3, 3, lanes), lambda s: (0, 0, s + offset)),
                pl.BlockSpec((modes, lanes), lambda s: (0, s + offset)),
            ],
            out_specs=[
                pl.BlockSpec((length, lanes), lambda s: (0, s)),
                pl.BlockSpec((modes, lanes), lambda s: (0, s)),
            ],
            out_shape=[
                jax.ShapeDtypeStruct((length, count * lanes), BF16),
                jax.ShapeDtypeStruct((modes, count * lanes), F32),
            ],
            cost_estimate=cost(0, count * lanes * length * 6),
            name="mix",
        )(key_proj, value_proj, tail, short_kernel, rate_c)

    xb, sum_b = mix(first, second)
    far = lax.ppermute(xb, "ctx", shifted_pairs(devices, 2))
    xa, sum_a = mix(0, first)
    near_a = lax.ppermute(xa, "ctx", swap_pairs(devices))

    window = jnp.concatenate([sum_a, sum_b], axis=1)
    state = jnp.zeros_like(window)
    hop = 1
    while hop < devices:
        got = lax.ppermute(window, "ctx", shifted_pairs(devices, hop))
        state = state + jnp.exp(-rate_c * (length * (hop - 1))) * got
        window = window + jnp.exp(-rate_c * (length * hop)) * got
        hop *= 2

    clamp_a = lambda s: (0, jnp.minimum(s, first - 1))
    clamp_b = lambda s: (0, jnp.maximum(s - first, 0))
    block_a = pl.BlockSpec((length, lanes), clamp_a)
    block_b = pl.BlockSpec((length, lanes), clamp_b)
    block = pl.BlockSpec((length, lanes), lambda s: (0, s))
    mode_block = pl.BlockSpec((modes, lanes), lambda s: (0, s))
    tb_block = pl.BlockSpec((per, LANES, taps), lambda s: (s, 0, 0))

    table, part_a, part_b = pl.pallas_call(
        lambda *refs: table_kernel(per, first, *refs),
        grid=(steps,),
        in_specs=[
            pl.BlockSpec((1, per, taps + LANES), lambda s: (s, 0, 0)),
            mode_block,
            mode_block,
            block_a,
            block_b,
        ],
        out_specs=[tb_block, block_a, block_b],
        out_shape=[
            jax.ShapeDtypeStruct((group_count, LANES, taps), BF16),
            jax.ShapeDtypeStruct((length, wide_a), F32),
            jax.ShapeDtypeStruct((length, wide_b), F32),
        ],
        cost_estimate=cost(0, 40e6),
        name="table",
    )(source, rate_c, weight_c, xa, xb)

    send_a, keep_a = pl.pallas_call(
        lambda *refs: merge_kernel(per, *refs),
        grid=(first,),
        in_specs=[smem, tb_block, block, block, block],
        out_specs=[block, block],
        out_shape=[
            jax.ShapeDtypeStruct((length, wide_a), BF16),
            jax.ShapeDtypeStruct((length, wide_a), F32),
        ],
        cost_estimate=cost(0, 8e6),
        name="merge",
    )(odd, table, near_a, xa, part_a)
    got_a = lax.ppermute(send_a, "ctx", shifted_pairs(devices, 2))

    send_b = jnp.where(odd[0] == 1, far, xb)
    near_b = lax.ppermute(send_b, "ctx", swap_pairs(devices))

    block_out, squares = pl.pallas_call(
        lambda *refs: late_kernel(per, first, *refs),
        grid=(steps,),
        in_specs=[
            smem,
            tb_block,
            block_a,
            block_b,
            block_a,
            block_b,
            block_b,
            mode_block,
            mode_block,
            mode_block,
            block,
            pl.BlockSpec((6, lanes), lambda s: (0, s)),
            pl.BlockSpec((3, 3, lanes), lambda s: (0, 0, s)),
            block,
        ],
        out_specs=[block, pl.BlockSpec((length, LANES), lambda s: (0, 0))],
        out_shape=[
            jax.ShapeDtypeStruct((length, channels), BF16),
            jax.ShapeDtypeStruct((length, LANES), F32),
        ],
        scratch_shapes=[pltpu.VMEM((length, LANES), F32)],
        cost_estimate=cost(0, 20e6),
        name="late",
    )(
        odd,
        table,
        keep_a,
        part_b,
        got_a,
        near_b,
        far,
        state,
        rate_c,
        weight_c,
        query_proj,
        tail,
        short_kernel,
        residual,
    )
    total = lax.psum(jnp.sum(squares, axis=1), "width")
    mean_sq = total / (channels * lax.axis_size("width"))
    scale = lax.rsqrt(mean_sq + 1e-05)[:, None]
    normed = pl.pallas_call(
        norm_kernel,
        grid=(steps,),
        in_specs=[
            pl.BlockSpec((length, 1), lambda s: (0, 0)),
            pl.BlockSpec((1, lanes), lambda s: (0, s)),
            block,
        ],
        out_specs=block,
        out_shape=jax.ShapeDtypeStruct((length, channels), BF16),
        cost_estimate=cost(0, 4e6),
        name="norm",
    )(scale, norm_gain[None, :], block_out)
    return (block_out, normed)


def solution(mesh):
    return jax.shard_map(
        body,
        mesh=mesh,
        in_specs=(
            P("ctx", "width"),
            P("ctx", "width"),
            P("ctx", "width"),
            P(None, None, "width"),
            P("width", None),
            P("width", None),
            P("width", None),
            P("ctx", "width"),
            P("width"),
        ),
        out_specs=(P("ctx", "width"), P("ctx", "width")),
        check_vma=False,
    )
```

time: 570 us -> 154 us (0.27)
  the two profiles are of different devices: /device:TPU:25 before, /device:TPU:0 now
where the time goes in v1:
time: 154 us; the launch traced here: 153 us
  Pallas kernels  52.2 us (34%)
  waiting for transfers between devices  43.2 us (28%)
  starting transfers between devices  37.6 us (24%)
  local copies, waits for them, and re-layouts  9.52 us (6%)
  other arithmetic  7.17 us (5%)
  blocking collectives  2.47 us (2%)
    ppermute x4, waiting for transfers between devices, body(): got = lax.ppermute(window, 'ctx', shifted_pairs(devices, hop))  27.9 us
    ppermute x4, starting transfers between devices, body(): got = lax.ppermute(window, 'ctx', shifted_pairs(devices, hop))  22.2 us
    pallas_call x1, Pallas kernels, body(): pl.pallas_call(lambda *refs: late_kernel(per, first, *refs), grid=(steps,...  15.8 us
    pallas_call x1, Pallas kernels, body(): pl.pallas_call(lambda *refs: table_kernel(per, first, *refs), grid=(steps...  15.1 us
    ppermute x1, waiting for transfers between devices, body(): got_a = lax.ppermute(send_a, 'ctx', shifted_pairs(devices, 2))  15.1 us
    pallas_call x2, Pallas kernels, mix(): pl.pallas_call(lambda *refs: mix_kernel(per, *refs), grid=(count,), in_sp...  9.83 us
    pallas_call x1, Pallas kernels, body(): pl.pallas_call(norm_kernel, grid=(steps,), in_specs=[pl.BlockSpec((length...  6.17 us
    pallas_call x1, Pallas kernels, body(): pl.pallas_call(lambda *refs: merge_kernel(per, *refs), grid=(first,), in_...  5.23 us
  transfers between devices with their start and end apart: 9, of which 5 were waited for; matrix products, arithmetic and copies ran while one was open for 6% of the time, Pallas kernels for 13%

profile of v1, /device:TPU:0, one launch (start us, length us, event | category | flops | bytes accessed | tf_op | source)
XLA Modules:
  0.0 153.0 jit_solution(7726099779137588077)
XLA Ops:
  0.6 0.9 slice.10
  1.5 0.9 slice.11
  2.4 0.9 slice.9
  3.3 4.8 %collective-permute-start = (bf16[6,4096]{1,0:T(8,128)(2,1)S(1)}, bf16[6,4096]{1,0:T(8,128)(2,1)S(1)}, u32[]{:S(2)}, u32[]{:S(2)}) collective-permute-start(bf16[6,4096]{1,0:T(8,128)(2,1)S(1)} %pad_maximum_fusion), channel_id=1, source_target_pairs={{0,2},{2,4},{4,6},{6,8},{8,10},{10,12},{12,14},{14,16},{16,18},{18... | collective-permute-start | bytes 147464 | tf_op jit(solution)/shard_map/ppermute | solution.py:258
  9.0 0.9 copy.25
  10.7 5.7 %mix.3 = (bf16[256,2560]{1,0:T(8,128)(2,1)}, f32[16,2560]{1,0:T(8,128)}) custom-call(bf16[256,4096]{1,0:T(8,128)(2,1)} %refs_0_.3, bf16[256,4096]{1,0:T(8,128)(2,1)} %refs_1_.3, f32[6,4096]{1,0:T(8,128)} %convert_element_type.6.refs_2_.refs_11_, f32[3,3,4096]{2,1,0:T(4,128)} %refs_12_.1, f32[16,4096]{1,0:T(8,128)} %bitcast.27), custom_call_target="tpu_custom_call" | custom-call | bytes 3932160 | tf_op jit(solution)/shard_map/mix/pallas_call | solution.py:270
  16.4 4.1 %mix.2 = (bf16[256,1536]{1,0:T(8,128)(2,1)}, f32[16,1536]{1,0:T(8,128)}) custom-call(bf16[256,4096]{1,0:T(8,128)(2,1)} %refs_0_.3, bf16[256,4096]{1,0:T(8,128)(2,1)} %refs_1_.3, f32[6,4096]{1,0:T(8,128)} %convert_element_type.6.refs_2_.refs_11_, f32[3,3,4096]{2,1,0:T(4,128)} %refs_12_.1, f32[16,4096]{1,0:T(8,128)} %bitcast.28), custom_call_target="tpu_custom_call" | custom-call | bytes 2359296 | tf_op jit(solution)/shard_map/mix/pallas_call | solution.py:270
  20.5 0.9 constant_dynamic-update-slice_fusion.1
  21.4 4.3 %collective-permute-start.5 = (f32[16,4096]{1,0:T(8,128)S(1)}, f32[16,4096]{1,0:T(8,128)S(1)}, u32[]{:S(2)}, u32[]{:S(2)}) collective-permute-start(f32[16,4096]{1,0:T(8,128)S(1)} %constant_dynamic-update-slice_fusion), channel_id=1, source_target_pairs={{0,2},{2,4},{4,6},{6,8},{8,10},{10,12},{12,14},{14,16},{16,18},{18... | collective-permute-start | bytes 786440 | tf_op jit(solution)/shard_map/ppermute | solution.py:301
  25.7 3.5 %collective-permute-start.3 = (bf16[256,2560]{1,0:T(8,128)(2,1)S(1)}, bf16[256,2560]{1,0:T(8,128)(2,1)S(1)}, u32[]{:S(2)}, u32[]{:S(2)}) collective-permute-start(bf16[256,2560]{1,0:T(8,128)(2,1)S(1)} %copy-done.1), channel_id=1, source_target_pairs={{0,4},{2,6},{4,8},{6,10},{8,12},{10,14},{12,16},{14,18},{16,20},{1... | collective-permute-start | bytes 3932168 | tf_op jit(solution)/shard_map/ppermute | solution.py:293
  29.2 0.9 collective-permute-done.5
  30.1 0.9 multiply_add_fusion.3
  31.0 6.3 %collective-permute-start.6 = (f32[16,4096]{1,0:T(8,128)}, f32[16,4096]{1,0:T(8,128)S(1)}, u32[]{:S(2)}, u32[]{:S(2)}) collective-permute-start(f32[16,4096]{1,0:T(8,128)} %multiply_add_fusion.3), channel_id=1, source_target_pairs={{0,4},{2,6},{4,8},{6,10},{8,12},{10,14},{12,16},{14,18},{16,20},{1... | collective-permute-start | bytes 786440 | tf_op jit(solution)/shard_map/ppermute | solution.py:301
  37.4 3.0 %collective-permute-start.1 = (bf16[256,1536]{1,0:T(8,128)(2,1)}, bf16[256,1536]{1,0:T(8,128)(2,1)}, u32[]{:S(2)}, u32[]{:S(2)}) collective-permute-start(bf16[256,1536]{1,0:T(8,128)(2,1)} %get-tuple-element.13.refs_3_), channel_id=1, source_target_pairs={{0,2},{2,0},{4,6},{6,4},{8,10},{10,8},{12,14},{14,12},{16,18},{18,... | collective-permute-start | bytes 2359304 | tf_op jit(solution)/shard_map/ppermute | solution.py:295
  40.4 25.4 %collective-permute-done.6 = f32[16,4096]{1,0:T(8,128)S(1)} collective-permute-done((f32[16,4096]{1,0:T(8,128)}, f32[16,4096]{1,0:T(8,128)S(1)}, u32[]{:S(2)}, u32[]{:S(2)}) %collective-permute-start.6) | collective-permute-done | bytes 262176 | tf_op jit(solution)/shard_map/ppermute | solution.py:301
  65.7 1.1 multiply_add_fusion.2
  66.9 6.2 %collective-permute-start.7 = (f32[16,4096]{1,0:T(8,128)S(1)}, f32[16,4096]{1,0:T(8,128)S(1)}, u32[]{:S(2)}, u32[]{:S(2)}) collective-permute-start(f32[16,4096]{1,0:T(8,128)S(1)} %multiply_add_fusion.2), channel_id=1, source_target_pairs={{0,8},{2,10},{4,12},{6,14},{8,16},{10,18},{12,20},{14,22},{16,24},... | collective-permute-start | bytes 786440 | tf_op jit(solution)/shard_map/ppermute | solution.py:301
  73.1 1.4 broadcast_select_fusion
  75.4 1.7 %collective-permute-done.7 = f32[16,4096]{1,0:T(8,128)S(1)} collective-permute-done((f32[16,4096]{1,0:T(8,128)S(1)}, f32[16,4096]{1,0:T(8,128)S(1)}, u32[]{:S(2)}, u32[]{:S(2)}) %collective-permute-start.7) | collective-permute-done | bytes 262176 | tf_op jit(solution)/shard_map/ppermute | solution.py:301
  77.1 0.9 multiply_add_fusion.1
  78.0 5.4 %collective-permute-start.8 = (f32[16,4096]{1,0:T(8,128)}, f32[16,4096]{1,0:T(8,128)S(1)}, u32[]{:S(2)}, u32[]{:S(2)}) collective-permute-start(f32[16,4096]{1,0:T(8,128)} %multiply_add_fusion.1), channel_id=1, source_target_pairs={{0,16},{2,18},{4,20},{6,22},{8,24},{10,26},{12,28},{14,30},{1,17},... | collective-permute-start | bytes 786440 | tf_op jit(solution)/shard_map/ppermute | solution.py:301
  83.6 0.9 copy.24
  85.6 15.1 %table.1 = (bf16[32,128,512]{2,1,0:T(8,128)(2,1)}, f32[256,1536]{1,0:T(8,128)}, f32[256,2560]{1,0:T(8,128)}) custom-call(f32[8,4,640]{2,1,0:T(4,128)} %reshape.24.refs_0_, f32[16,4096]{1,0:T(8,128)} %bitcast.29, f32[16,4096]{1,0:T(8,128)} %bitcast.31, bf16[256,1536]{1,0:T(8,128)(2,1)} %get-tuple-element.13.refs_3_, bf16[256,2560]{1,0:T(8,128)(2,1)} %get-tuple-element.14.refs_4_), custom_call_target="tpu_custom_call" | custom-call | bytes 40000000 | tf_op jit(solution)/shard_map/table/pallas_call | solution.py:314
  100.7 5.2 %merge.1 = (bf16[256,1536]{1,0:T(8,128)(2,1)}, f32[256,1536]{1,0:T(8,128)}) custom-call(s32[1]{0:T(128)} %bitcast.refs_0_, bf16[32,128,512]{2,1,0:T(8,128)(2,1)} %get-tuple-element.15.refs_1_, bf16[256,1536]{1,0:T(8,128)(2,1)} %collective-permute-done.1.refs_2_, bf16[256,1536]{1,0:T(8,128)(2,1)} %get-tuple-element.13.refs_3_, ...), custom_call_target="tpu_custom_call" | custom-call | bytes 8000000 | tf_op jit(solution)/shard_map/merge/pallas_call | solution.py:334
  105.9 3.3 %collective-permute-start.2 = (bf16[256,1536]{1,0:T(8,128)(2,1)}, bf16[256,1536]{1,0:T(8,128)(2,1)S(1)}, u32[]{:S(2)}, u32[]{:S(2)}) collective-permute-start(bf16[256,1536]{1,0:T(8,128)(2,1)} %get-tuple-element.19), channel_id=1, source_target_pairs={{0,4},{2,6},{4,8},{6,10},{8,12},{10,14},{12,16},{14,18},{16,20},{1... | collective-permute-start | bytes 2359304 | tf_op jit(solution)/shard_map/ppermute | solution.py:346
  109.3 1.0 multiply_add_fusion.refs_7_
  110.3 15.1 %collective-permute-done.2.refs_4_ = bf16[256,1536]{1,0:T(8,128)(2,1)S(1)} collective-permute-done((bf16[256,1536]{1,0:T(8,128)(2,1)}, bf16[256,1536]{1,0:T(8,128)(2,1)S(1)}, u32[]{:S(2)}, u32[]{:S(2)}) %collective-permute-start.2) | collective-permute-done | bytes 786464 | tf_op jit(solution)/shard_map/ppermute | solution.py:346
  125.4 0.9 copy-done.5
  126.7 15.8 %late.1 = (bf16[256,4096]{1,0:T(8,128)(2,1)}, f32[256,128]{1,0:T(8,128)}) custom-call(s32[1]{0:T(128)} %bitcast.refs_0_, bf16[32,128,512]{2,1,0:T(8,128)(2,1)} %get-tuple-element.15.refs_1_, f32[256,1536]{1,0:T(8,128)} %get-tuple-element.17.refs_2_, f32[256,2560]{1,0:T(8,128)} %get-tuple-element.18.refs_3_, bf16[256,1536]{1,0:T(8,128)(2,1)} %copy-done.5, ...), custom_call_target="tpu_custom_call" | custom-call | bytes 20000000 | tf_op jit(solution)/shard_map/late/pallas_call | solution.py:351
  142.5 1.0 reduce_sum.9
  143.6 2.5 %psum.7 = f32[256]{0:T(256)S(1)} all-reduce(f32[256]{0:T(256)S(1)} %reduce_sum.9), channel_id=1, replica_groups=mesh['ctx'=16,'width'=2] {'width'}, use_global_device_ids=true, to_apply=%region_1.2 | all-reduce | flops 256 | bytes 2048 | tf_op jit(solution)/shard_map/psum | solution.py:394
  146.9 6.2 %norm.1 = bf16[256,4096]{1,0:T(8,128)(2,1)} custom-call(f32[256,1]{1,0:T(8,128)} %copy.11.scale_ref, f32[1,4096]{1,0:T(1,128)} %bitcast.35, bf16[256,4096]{1,0:T(8,128)(2,1)} %get-tuple-element.11.x_ref), custom_call_target="tpu_custom_call" | custom-call | bytes 4000000 | tf_op jit(solution)/shard_map/norm/pallas_call | solution.py:397
  (36 shorter events, 5.2 us)
Async XLA Ops:
  3.3 6.7 %collective-permute-start = (bf16[6,4096]{1,0:T(8,128)(2,1)S(1)}, bf16[6,4096]{1,0:T(8,128)(2,1)S(1)}, u32[]{:S(2)}, u32[]{:S(2)}) collective-permute-start(bf16[6,4096]{1,0:T(8,128)(2,1)S(1)} %pad_maximum_fusion), channel_id=1, source_target_pairs={{0,2},{2,4},{4,6},{6,8},{8,10},{10,12},{12,14},{14,16},{16,18},{18... | collective-permute-start | bytes 147464 | tf_op jit(solution)/shard_map/ppermute | solution.py:258
  16.4 5.0 %copy-start.6 = (f32[16,2560]{1,0:T(8,128)S(1)}, f32[16,2560]{1,0:T(8,128)}, u32[]{:S(2)}) copy-start(f32[16,2560]{1,0:T(8,128)} %get-tuple-element.21) | copy-start | bytes 491524
  16.4 9.4 %copy-start.1 = (bf16[256,2560]{1,0:T(8,128)(2,1)S(1)}, bf16[256,2560]{1,0:T(8,128)(2,1)}, u32[]{:S(2)}) copy-start(bf16[256,2560]{1,0:T(8,128)(2,1)} %get-tuple-element.14.refs_4_) | copy-start | bytes 3932164
  21.4 8.7 %collective-permute-start.5 = (f32[16,4096]{1,0:T(8,128)S(1)}, f32[16,4096]{1,0:T(8,128)S(1)}, u32[]{:S(2)}, u32[]{:S(2)}) collective-permute-start(f32[16,4096]{1,0:T(8,128)S(1)} %constant_dynamic-update-slice_fusion), channel_id=1, source_target_pairs={{0,2},{2,4},{4,6},{6,8},{8,10},{10,12},{12,14},{14,16},{16,18},{18... | collective-permute-start | bytes 786440 | tf_op jit(solution)/shard_map/ppermute | solution.py:301
  25.7 47.3 %collective-permute-start.3 = (bf16[256,2560]{1,0:T(8,128)(2,1)S(1)}, bf16[256,2560]{1,0:T(8,128)(2,1)S(1)}, u32[]{:S(2)}, u32[]{:S(2)}) collective-permute-start(bf16[256,2560]{1,0:T(8,128)(2,1)S(1)} %copy-done.1), channel_id=1, source_target_pairs={{0,4},{2,6},{4,8},{6,10},{8,12},{10,14},{12,16},{14,18},{16,20},{1... | collective-permute-start | bytes 3932168 | tf_op jit(solution)/shard_map/ppermute | solution.py:293
  31.0 34.7 %collective-permute-start.6 = (f32[16,4096]{1,0:T(8,128)}, f32[16,4096]{1,0:T(8,128)S(1)}, u32[]{:S(2)}, u32[]{:S(2)}) collective-permute-start(f32[16,4096]{1,0:T(8,128)} %multiply_add_fusion.3), channel_id=1, source_target_pairs={{0,4},{2,6},{4,8},{6,10},{8,12},{10,14},{12,16},{14,18},{16,20},{1... | collective-permute-start | bytes 786440 | tf_op jit(solution)/shard_map/ppermute | solution.py:301
  37.4 63.3 %collective-permute-start.1 = (bf16[256,1536]{1,0:T(8,128)(2,1)}, bf16[256,1536]{1,0:T(8,128)(2,1)}, u32[]{:S(2)}, u32[]{:S(2)}) collective-permute-start(bf16[256,1536]{1,0:T(8,128)(2,1)} %get-tuple-element.13.refs_3_), channel_id=1, source_target_pairs={{0,2},{2,0},{4,6},{6,4},{8,10},{10,8},{12,14},{14,12},{16,18},{18,... | collective-permute-start | bytes 2359304 | tf_op jit(solution)/shard_map/ppermute | solution.py:295
  66.9 16.6 %copy-start.7 = (f32[32,16]{0,1:T(8,128)S(1)}, f32[32,16]{0,1:T(8,128)}, u32[]{:S(2)}) copy-start(f32[32,16]{0,1:T(8,128)} %param.14) | copy-start | bytes 6148
  66.9 16.6 %copy-start.9 = (f32[32,16]{0,1:T(8,128)S(1)}, f32[32,16]{0,1:T(8,128)}, u32[]{:S(2)}) copy-start(f32[32,16]{0,1:T(8,128)} %param.15) | copy-start | bytes 6148
  66.9 10.2 %collective-permute-start.7 = (f32[16,4096]{1,0:T(8,128)S(1)}, f32[16,4096]{1,0:T(8,128)S(1)}, u32[]{:S(2)}, u32[]{:S(2)}) collective-permute-start(f32[16,4096]{1,0:T(8,128)S(1)} %multiply_add_fusion.2), channel_id=1, source_target_pairs={{0,8},{2,10},{4,12},{6,14},{8,16},{10,18},{12,20},{14,22},{16,24},... | collective-permute-start | bytes 786440 | tf_op jit(solution)/shard_map/ppermute | solution.py:301
  73.1 1.6 %copy-start = (bf16[256,2560]{1,0:T(8,128)(2,1)}, bf16[256,2560]{1,0:T(8,128)(2,1)S(1)}, u32[]{:S(2)}) copy-start(bf16[256,2560]{1,0:T(8,128)(2,1)S(1)} %collective-permute-done.3.refs_6_) | copy-start | bytes 3932164
  74.7 9.8 %copy-start.8 = (bf16[32,512]{1,0:T(8,128)(2,1)S(1)}, bf16[32,512]{1,0:T(8,128)(2,1)}, u32[]{:S(2)}) copy-start(bf16[32,512]{1,0:T(8,128)(2,1)} %param.13) | copy-start | bytes 98308
  74.7 50.7 %collective-permute-start.4 = (bf16[256,2560]{1,0:T(8,128)(2,1)}, bf16[256,2560]{1,0:T(8,128)(2,1)S(1)}, u32[]{:S(2)}, u32[]{:S(2)}) collective-permute-start(bf16[256,2560]{1,0:T(8,128)(2,1)} %broadcast_select_fusion), channel_id=1, source_target_pairs={{0,2},{2,0},{4,6},{6,4},{8,10},{10,8},{12,14},{14,12},{16,18},{18,... | collective-permute-start | bytes 3932168 | tf_op jit(solution)/shard_map/ppermute | solution.py:349
  77.1 6.3 %copy-start.3 = (f32[16,4096]{1,0:T(8,128)}, f32[16,4096]{1,0:T(8,128)S(1)}, u32[]{:S(2)}) copy-start(f32[16,4096]{1,0:T(8,128)S(1)} %collective-permute-done.7) | copy-start | bytes 786436
  78.0 31.3 %collective-permute-start.8 = (f32[16,4096]{1,0:T(8,128)}, f32[16,4096]{1,0:T(8,128)S(1)}, u32[]{:S(2)}, u32[]{:S(2)}) collective-permute-start(f32[16,4096]{1,0:T(8,128)} %multiply_add_fusion.1), channel_id=1, source_target_pairs={{0,16},{2,18},{4,20},{6,22},{8,24},{10,26},{12,28},{14,30},{1,17},... | collective-permute-start | bytes 786440 | tf_op jit(solution)/shard_map/ppermute | solution.py:301
  100.7 8.6 %copy-start.4 = (f32[16,4096]{1,0:T(8,128)S(1)}, f32[16,4096]{1,0:T(8,128)}, u32[]{:S(2)}) copy-start(f32[16,4096]{1,0:T(8,128)} %copy-done.3) | copy-start | bytes 786436
  105.9 19.4 %collective-permute-start.2 = (bf16[256,1536]{1,0:T(8,128)(2,1)}, bf16[256,1536]{1,0:T(8,128)(2,1)S(1)}, u32[]{:S(2)}, u32[]{:S(2)}) collective-permute-start(bf16[256,1536]{1,0:T(8,128)(2,1)} %get-tuple-element.19), channel_id=1, source_target_pairs={{0,4},{2,6},{4,8},{6,10},{8,12},{10,14},{12,16},{14,18},{16,20},{1... | collective-permute-start | bytes 2359304 | tf_op jit(solution)/shard_map/ppermute | solution.py:346
  125.4 0.9 copy-start.5
  125.4 1.3 copy-start.2

commit v2 on v0

v2 whole, which is shorter than its diff:
```python
import jax
import jax.numpy as jnp
from jax import lax
from jax.experimental import pallas as pl
from jax.experimental.pallas import tpu as pltpu
from jax.sharding import PartitionSpec as P

F32 = jnp.float32
BF16 = jnp.bfloat16
LANES = 128


def shifted_pairs(length, by):
    return [(i, i + by) for i in range(length) if i + by < length]


def swap_pairs(length):
    return [(i, i ^ 1) for i in range(length)]


def dot(a, b):
    return jnp.dot(a, b, preferred_element_type=F32)


def split(x):
    hi = x.astype(BF16)
    return hi, (x - hi.astype(F32)).astype(BF16)


def each(count, body, unroll):
    def several(step, carry):
        for j in range(unroll):
            body(step * unroll + j)
        return carry

    lax.fori_loop(0, count // unroll, several, 0)
    for group in range(count - count % unroll, count):
        body(group)


def after(value, *others):
    return lax.optimization_barrier((value, *others))[0]


def at(group):
    if isinstance(group, int):
        return pl.ds(group * LANES, LANES)
    return pl.ds(pl.multiple_of(group * LANES, LANES), LANES)


def column(table, group):
    place = lax.broadcasted_iota(jnp.int32, table.shape, 1)
    picked = jnp.sum(jnp.where(place == group, table, 0.0), axis=1, keepdims=True)
    return jnp.broadcast_to(picked, (table.shape[0], LANES))


def taps_of(sk_ref, which, lanes):
    return [sk_ref[which, j : j + 1, lanes] for j in range(3)]


def tails_of(tail_ref, which, lanes):
    rows = tail_ref[0:8, lanes].astype(F32)
    return [rows[2 * which + j : 2 * which + j + 1] for j in range(2)]


def short_filter(ref, kern, lanes):
    rows = ref[:, lanes].astype(F32)
    return kern[0] * rows + kern[1] * pltpu.roll(rows, 1, 0) + kern[2] * pltpu.roll(rows, 2, 0)


def short_filter_top(ref, tail, kern, lanes):
    rows = ref[0:16, lanes].astype(F32)
    before, last = tail
    place = lax.broadcasted_iota(jnp.int32, rows.shape, 0)
    one = jnp.where(place == 0, last, pltpu.roll(rows, 1, 0))
    two = jnp.where(place == 0, before, jnp.where(place == 1, last, pltpu.roll(rows, 2, 0)))
    return kern[0] * rows + kern[1] * one + kern[2] * two


def tail_kernel(q_ref, k_ref, v_ref, o_ref):
    for which, ref in enumerate((q_ref, k_ref, v_ref)):
        o_ref[2 * which : 2 * which + 2, :] = ref[14:16, :]
    o_ref[6:8, :] = v_ref[14:16, :]


def mix_kernel(sizes, k_ref, v_ref, sk_ref, *x_refs):
    def make(start, x_ref):
        def one(g):
            source = at(g + start)
            x_ref[:, at(g)] = (
                short_filter(k_ref, taps_of(sk_ref, 1, source), source)
                * short_filter(v_ref, taps_of(sk_ref, 2, source), source)
            ).astype(BF16)

        return one

    start = 0
    for size, x_ref in zip(sizes, x_refs):
        each(size, make(start, x_ref), 2)
        start += size


def head_kernel(sizes, *refs):
    k_ref, v_ref, tail_ref, sk_ref, rate_ref, *x_refs, f_ref = refs[len(sizes) :]
    length = k_ref.shape[0]

    def make(start, x_ref):
        def one(g):
            source = at(g + start)
            lanes = at(g)
            x_ref[0:16, lanes] = (
                short_filter_top(
                    k_ref, tails_of(tail_ref, 1, source), taps_of(sk_ref, 1, source), source
                )
                * short_filter_top(
                    v_ref, tails_of(tail_ref, 2, source), taps_of(sk_ref, 2, source), source
                )
            ).astype(BF16)
            rate = column(rate_ref[...], g + start)
            tables = []
            for part in range(length // LANES):
                place = lax.broadcasted_iota(jnp.int32, rate.shape, 1) + part * LANES
                tables.append(jnp.exp(-rate * (length - 1 - place).astype(F32)))
            hi, lo = split(jnp.concatenate(tables, axis=1))
            total = dot(jnp.concatenate([hi, lo], axis=0), x_ref[:, lanes])
            modes = rate.shape[0]
            f_ref[:, source] = total[:modes] + total[modes:]

        return one

    start = 0
    for size, x_ref in zip(sizes, x_refs):
        each(size, make(start, x_ref), 2)
        start += size


def table_kernel(start, pieces, source_ref, rate_ref, weight_ref, *refs):
    *x_refs, tb_ref, f_ref = refs
    done = 0
    for groups, x_ref in zip(pieces, x_refs):
        table_piece(start, done, groups, source_ref, rate_ref, weight_ref, x_ref, tb_ref, f_ref)
        done += groups


def table_piece(start, skip, groups, source_ref, rate_ref, weight_ref, x_ref, tb_ref, f_ref):
    taps = source_ref.shape[-1]
    row_at = lax.broadcasted_iota(jnp.int32, (LANES, LANES), 0)
    col_at = lax.broadcasted_iota(jnp.int32, (LANES, LANES), 1)
    below = col_at <= row_at
    place = lax.broadcasted_iota(jnp.int32, (1, LANES), 1)

    def one(g):
        lanes = at(g)
        taken = source_ref[pl.ds(g + start + skip, 1), :]
        band = pltpu.roll(jnp.broadcast_to(taken, (LANES, taps)), 0, 1, stride=1, stride_axis=0)
        tb_ref[g + skip, :, 0:LANES] = jnp.where(below, 0.0, band[:, 0:LANES]).astype(BF16)
        tb_ref[g + skip, :, LANES:] = band[:, LANES:].astype(BF16)
        rate = column(rate_ref[...], g + start + skip)
        weight = column(weight_ref[...], g + start + skip)

        def modal(lag):
            value = weight * jnp.exp(-rate * lag.astype(F32))
            return jnp.sum(value, axis=0, keepdims=True)

        first = taken[:, taps - LANES :] + modal(LANES - place)
        lag_zero = taken[:, 0:1] + modal(place * 0)[:, 0:1]
        second = taken[:, taps - 2 * LANES : taps - LANES] + modal(2 * LANES - place)
        second = jnp.where(place == 0, lag_zero, second)
        near = jnp.broadcast_to(jnp.concatenate([first, second], axis=1), (LANES, 2 * LANES))
        near = pltpu.roll(near, 0, 1, stride=1, stride_axis=0)
        zero_lag = jnp.where(below, near[:, LANES:], 0.0)
        low = jnp.concatenate([near[:, :LANES], zero_lag], axis=1)
        top = jnp.concatenate([zero_lag, jnp.zeros((LANES, LANES), F32)], axis=1)
        hi, lo = split(jnp.concatenate([top, low], axis=0))
        both = dot(jnp.concatenate([hi, lo], axis=0), x_ref[:, lanes])
        f_ref[:, at(g + skip)] = both[: 2 * LANES] + both[2 * LANES :]

    each(groups, one, 2)


def lag_one(tb_ref, g):
    return jnp.concatenate([tb_ref[g, :, 256:512], tb_ref[g, :, 128:384]], axis=0)


def lag_two(tb_ref, g):
    low = jnp.concatenate([jnp.zeros((LANES, LANES), BF16), tb_ref[g, :, 0:128]], axis=1)
    return jnp.concatenate([tb_ref[g, :, 0:256], low], axis=0)


def merge_kernel(
    first,
    b_parts,
    odd_ref,
    tb_ref,
    near_ref,
    own_ref,
    f_ref,
    far1_ref,
    far2_ref,
    xb1_ref,
    xb2_ref,
    send_a_ref,
    send_b_ref,
    keep_ref,
):
    odd = odd_ref[0]
    middle = b_parts[0] * LANES

    @pl.when(odd == 1)
    def _():
        send_a_ref[...] = own_ref[...]
        send_b_ref[:, :middle] = far1_ref[...]
        send_b_ref[:, middle:] = far2_ref[...]

        def one(g):
            lanes = at(g)
            keep_ref[:, lanes] = f_ref[:, lanes] + dot(lag_one(tb_ref, g), near_ref[:, lanes])

        each(first, one, 2)

    @pl.when(odd == 0)
    def _():
        keep_ref[...] = f_ref[...]
        send_b_ref[:, :middle] = xb1_ref[...]
        send_b_ref[:, middle:] = xb2_ref[...]

        def one(g):
            lanes = at(g)
            send_a_ref[:, lanes] = (
                dot(lag_one(tb_ref, g), near_ref[:, lanes])
                + dot(lag_two(tb_ref, g), own_ref[:, lanes])
            ).astype(BF16)

        each(first, one, 2)


def pre_kernel(
    start, one, two, tb_ref, far1_ref, far2_ref, f_ref, q_ref, tail_ref, sk_ref, acc_ref, query_ref
):
    def filtered(g):
        lanes = at(g)
        kern = taps_of(sk_ref, 0, lanes)
        query_ref[:, lanes] = short_filter(q_ref, kern, lanes)
        query_ref[0:16, lanes] = short_filter_top(q_ref, tails_of(tail_ref, 0, lanes), kern, lanes)

    each(start, filtered, 2)

    def make(skip, far_ref):
        def added(g):
            lanes = at(g + skip)
            filtered(g + skip + start)
            acc_ref[:, lanes] = f_ref[:, lanes] + dot(lag_two(tb_ref, g + skip), far_ref[:, at(g)])

        return added

    each(one, make(0, far1_ref), 2)
    each(two, make(one, far2_ref), 2)


def state_kernel(
    first, second, fa_ref, fb_ref, state_ref, rate_ref, weight_ref, query_ref, res_ref, base_ref
):
    length = fa_ref.shape[0]

    def make(start, ref):
        def one(g):
            lanes = at(g)
            wide = at(g + start)
            rate = column(rate_ref[...], g + start)
            weight = column(weight_ref[...], g + start)
            s_hi, s_lo = split(state_ref[:, wide])
            state = jnp.concatenate([s_hi, s_lo, s_hi], axis=0)
            tables = []
            for part in range(length // LANES):
                place = lax.broadcasted_iota(jnp.int32, rate.shape, 1) + part * LANES
                tables.append(weight * jnp.exp(-rate * (place + 1).astype(F32)))
            o_hi, o_lo = split(jnp.concatenate(tables, axis=1))
            table = jnp.concatenate([o_hi, o_hi, o_lo], axis=0)
            far = lax.dot_general(
                table, state, (((0,), (0,)), ((), ())), preferred_element_type=F32
            )
            base_ref[:, wide] = res_ref[:, wide].astype(F32) + query_ref[:, wide] * (
                ref[:, lanes] + far
            )

        return one

    each(first, make(0, fa_ref), 2)
    each(second, make(first, fb_ref), 2)


def chunks_of(groups):
    return [(c * groups // 8, (c + 1) * groups // 8) for c in range(8)]


def copy_out(source_ref, target_ref, sems, index, low, high):
    span = pl.ds(low * LANES, (high - low) * LANES)
    return pltpu.make_async_copy(source_ref.at[:, span], target_ref.at[:, span], sems.at[index])


def late_kernel(
    first,
    second,
    odd_ref,
    ta_ref,
    tb_ref,
    got_ref,
    near_ref,
    base_ref,
    query_ref,
    target_ref,
    out_ref,
    square_ref,
    sum_ref,
    sems,
):
    odd = odd_ref[0]
    sum_ref[...] = jnp.zeros_like(sum_ref)

    def finish(wide, term):
        rounded = (base_ref[:, wide] + query_ref[:, wide] * term).astype(BF16)
        out_ref[:, wide] = rounded
        back = rounded.astype(F32)
        sum_ref[...] += back * back

    def far(g):
        finish(at(g), dot(lag_two(ta_ref, g), got_ref[:, at(g)]))

    def merged(g):
        finish(at(g), got_ref[:, at(g)].astype(F32))

    def near(g):
        finish(at(g + first), dot(lag_one(tb_ref, g), near_ref[:, at(g)]))

    @pl.when(odd == 1)
    def _():
        each(first, far, 2)

    @pl.when(odd == 0)
    def _():
        each(first, merged, 2)

    copy_a = copy_out(out_ref, target_ref, sems, 0, 0, first)
    copy_a.start()
    each(second, near, 2)
    copy_b = copy_out(out_ref, target_ref, sems, 1, first, first + second)
    copy_b.start()
    turned = jnp.transpose(sum_ref[...])
    square_ref[...] = jnp.broadcast_to(jnp.sum(turned, axis=0, keepdims=True), square_ref.shape)
    copy_a.wait()
    copy_b.wait()


def norm_kernel(count, groups, total_ref, gain_ref, x_ref, target_ref, o_ref, sems):
    scale = jnp.transpose(lax.rsqrt(total_ref[...] * (1.0 / count) + 1e-05))
    wide = jnp.broadcast_to(scale[:, 0:1], (scale.shape[0], LANES))
    copies = []
    for index, (low, high) in enumerate(chunks_of(groups)):
        for g in range(low, high):
            lanes = at(g)
            o_ref[:, lanes] = (x_ref[:, lanes].astype(F32) * wide * gain_ref[:, lanes]).astype(BF16)
        copy = copy_out(o_ref, target_ref, sems, index, low, high)
        copy.start()
        copies.append(copy)
    for copy in copies:
        copy.wait()


def call(kernel, out_shape, name, *args, smem=0, scratch=(), loose=(), alias={}):
    specs = [pl.BlockSpec(memory_space=pltpu.SMEM)] * smem
    specs += [pl.BlockSpec(memory_space=pltpu.VMEM)] * (len(args) - smem)
    outs = [
        pl.BlockSpec(memory_space=pl.ANY if i in loose else pltpu.VMEM)
        for i in range(len(out_shape))
    ]
    return pl.pallas_call(
        kernel,
        in_specs=specs,
        out_specs=outs,
        out_shape=out_shape,
        scratch_shapes=scratch,
        input_output_aliases=alias,
        cost_estimate=pl.CostEstimate(flops=0, bytes_accessed=20000, transcendentals=0),
        compiler_params=pltpu.CompilerParams(vmem_limit_bytes=24 << 20),
        name=name,
    )(*args)


def body(
    query_proj,
    key_proj,
    value_proj,
    short_kernel,
    explicit_taps,
    decay_rate,
    residues,
    residual,
    norm_gain,
):
    length, channels = query_proj.shape
    groups, taps = explicit_taps.shape
    modes = decay_rate.shape[1]
    devices = lax.axis_size("ctx")
    first = groups // 2
    second = groups - first
    b_parts = ((second * 3) // 8, second - (second * 3) // 8)
    sizes = (first, *b_parts)
    wide_a = first * LANES
    wide_b = second * LANES
    odd = (lax.axis_index("ctx") % 2).astype(jnp.int32).reshape(1)
    is_odd = odd[0] == 1
    shape = jax.ShapeDtypeStruct

    last = pl.BlockSpec((16, channels), lambda s: (length // 16 - 1, 0))
    own_tail = pl.pallas_call(
        tail_kernel,
        grid=(1,),
        in_specs=[last, last, last],
        out_specs=pl.BlockSpec((8, channels), lambda s: (0, 0)),
        out_shape=shape((8, channels), BF16),
        name="tail",
    )(query_proj, key_proj, value_proj)
    tail = lax.ppermute(own_tail, "ctx", shifted_pairs(devices, 1))

    rate_t = decay_rate.T
    weight_t = (residues * jnp.sqrt(-jnp.expm1(-2.0 * decay_rate))).T
    flipped = jnp.flip(explicit_taps, axis=1).astype(F32)
    source = jnp.concatenate([flipped[:, taps - 1 :], flipped[:, : taps - 1]], axis=1)

    blocks = [shape((length, size * LANES), BF16) for size in sizes]
    mixed = call(
        lambda *refs: mix_kernel(sizes, *refs), blocks, "mix", key_proj, value_proj, short_kernel
    )
    xa, xb1, xb2, window = call(
        lambda *refs: head_kernel(sizes, *refs),
        [*blocks, shape((modes, channels), F32)],
        "head",
        *mixed, key_proj, value_proj, after(tail, mixed[0]), short_kernel, rate_t,
        alias={i: i for i in range(len(sizes))},
    )
    half = channels // 2
    mine = jnp.where(is_odd, window[:, half:], window[:, :half])
    beside = lax.ppermute(
        jnp.where(is_odd, window[:, :half], window[:, half:]), "ctx", swap_pairs(devices)
    )

    def tables(start, parts, x, source):
        count = sum(parts)
        return call(
            lambda *refs: table_kernel(start, parts, *refs),
            [shape((count, LANES, taps), BF16), shape((length, count * LANES), F32)],
            "table",
            source, rate_t, weight_t, *x,
        )

    wide_rate = jnp.broadcast_to(rate_t[:, :, None], (modes, groups, LANES)).reshape(modes, channels)
    wide_rate = jnp.where(is_odd, wide_rate[:, half:], wide_rate[:, :half])
    decay = lambda blocks: jnp.exp(-wide_rate * (length * blocks))

    ta, part_a = tables(0, (first,), (xa,), source)
    beside = after(beside, part_a)
    pair = decay(1.0) * jnp.where(is_odd, beside, mine) + jnp.where(is_odd, mine, beside)
    far1 = lax.ppermute(xb1, "ctx", shifted_pairs(devices, 2))
    near_a = lax.ppermute(xa, "ctx", swap_pairs(devices))
    got = lax.ppermute(pair, "ctx", shifted_pairs(devices, 2))
    tb, part_b = tables(first, b_parts, (xb1, xb2), after(source, pair))
    before = after(got, part_b)
    pair = pair + decay(2.0) * before
    far1 = after(far1, part_b)
    far2 = lax.ppermute(after(xb2, far1, pair), "ctx", shifted_pairs(devices, 2))
    near_a = after(near_a, part_b)
    hop = 4
    while hop < devices:
        got = lax.ppermute(pair, "ctx", shifted_pairs(devices, hop))
        before = before + decay(float(hop - 2)) * got
        pair = pair + decay(float(hop)) * got
        hop *= 2
        if hop * 2 == devices:
            far2, near_a = after(far2, pair), after(near_a, pair)
    send_a, send_b, keep_a = call(
        lambda *refs: merge_kernel(first, b_parts, *refs),
        [
            shape((length, wide_a), BF16),
            shape((length, wide_b), BF16),
            shape((length, wide_a), F32),
        ],
        "merge",
        odd, ta, near_a, xa, part_a, far1, far2, xb1, xb2,
        smem=1,
    )
    onward = decay(1.0) * before + jnp.where(is_odd, beside, mine)
    other = lax.ppermute(
        after(jnp.where(is_odd, before, onward), keep_a), "ctx", swap_pairs(devices)
    )
    near_b = lax.ppermute(after(send_b, onward), "ctx", swap_pairs(devices))
    got_a = lax.ppermute(send_a, "ctx", shifted_pairs(devices, 2))
    acc_b, query = call(
        lambda *refs: pre_kernel(first, *b_parts, *refs),
        [shape((length, wide_b), F32), shape((length, channels), F32)],
        "pre",
        tb, far1, far2, after(part_b, keep_a), query_proj, tail, short_kernel,
    )
    other = after(other, query)
    state = jnp.where(
        is_odd,
        jnp.concatenate([other, onward], axis=1),
        jnp.concatenate([before, other], axis=1),
    )
    (base,) = call(
        lambda *refs: state_kernel(first, second, *refs),
        [shape((length, channels), F32)],
        "state",
        keep_a, acc_b, state, rate_t, weight_t, query, residual,
    )
    block_out, again, squares = call(
        lambda *refs: late_kernel(first, second, *refs),
        [
            shape((length, channels), BF16),
            shape((length, channels), BF16),
            shape((8, length), F32),
        ],
        "late",
        odd, ta, tb, got_a, near_b, base, query,
        smem=1,
        scratch=[pltpu.VMEM((length, LANES), F32), pltpu.SemaphoreType.DMA((2,))],
        loose=(0,),
    )
    total = lax.psum(squares, "width")
    count = float(channels * lax.axis_size("width"))
    (normed,) = call(
        lambda *refs: norm_kernel(count, groups, *refs),
        [shape((length, channels), BF16)],
        "norm",
        total, norm_gain[None, :], again,
        scratch=[pltpu.VMEM((length, channels), BF16), pltpu.SemaphoreType.DMA((8,))],
        loose=(0,),
    )
    return (block_out, normed)


def solution(mesh):
    return jax.shard_map(
        body,
        mesh=mesh,
        in_specs=(
            P("ctx", "width"),
            P("ctx", "width"),
            P("ctx", "width"),
            P(None, None, "width"),
            P("width", None),
            P("width", None),
            P("width", None),
            P("ctx", "width"),
            P("width"),
        ),
        out_specs=(P("ctx", "width"), P("ctx", "width")),
        check_vma=False,
    )
```

time: 570 us -> 109 us (0.19)
  the two profiles are of different devices: /device:TPU:25 before, /device:TPU:0 now
where the time goes in v2:
time: 109 us
  Pallas kernels  37.4 us (34%)
  starting transfers between devices  31.7 us (29%)
  waiting for transfers between devices  29.7 us (27%)
  local copies, waits for them, and re-layouts  6.11 us (6%)
  blocking collectives  2.5 us (2%)
    pallas_call x9, Pallas kernels, call(): pl.pallas_call(kernel, in_specs=specs, out_specs=outs, out_shape=out_shap...  35.6 us
    ppermute x1, waiting for transfers between devices, body(): lax.ppermute(after(jnp.where(is_odd, before, onward), keep_a), 'ctx', swa...  15.5 us
    ppermute x1, waiting for transfers between devices, body(): near_a = lax.ppermute(xa, 'ctx', swap_pairs(devices))  11.7 us
    ppermute x2, starting transfers between devices, body(): got = lax.ppermute(pair, 'ctx', shifted_pairs(devices, hop))  8.59 us
    ppermute x1, starting transfers between devices, body(): tail = lax.ppermute(own_tail, 'ctx', shifted_pairs(devices, 1))  5.45 us
    unnamed x31, local copies, waits for them, and re-layouts  4.26 us
    ppermute x1, starting transfers between devices, body(): far1 = lax.ppermute(xb1, 'ctx', shifted_pairs(devices, 2))  3.57 us
    ppermute x1, starting transfers between devices, body(): got_a = lax.ppermute(send_a, 'ctx', shifted_pairs(devices, 2))  3.5 us
  transfers between devices with their start and end apart: 11, of which 3 were waited for; matrix products, arithmetic and copies ran while one was open for 2% of the time, Pallas kernels for 20%

profile of v2, /device:TPU:0, one launch (start us, length us, event | category | flops | bytes accessed | tf_op | source)
XLA Modules:
  0.0 108.7 jit_solution(15847544286424703451)
XLA Ops:
  0.6 1.8 %tail.1 = bf16[8,4096]{1,0:T(8,128)(2,1)} custom-call(bf16[256,4096]{1,0:T(8,128)(2,1)} %refs_4_.3, bf16[256,4096]{1,0:T(8,128)(2,1)} %refs_3_.1, bf16[256,4096]{1,0:T(8,128)(2,1)} %refs_4_.2), custom_call_target="tpu_custom_call" | custom-call | tf_op jit(solution)/shard_map/tail/pallas_call | solution.py:415
  2.5 5.5 %collective-permute-start = (bf16[8,4096]{1,0:T(8,128)(2,1)}, bf16[8,4096]{1,0:T(8,128)(2,1)}, u32[]{:S(2)}, u32[]{:S(2)}) collective-permute-start(bf16[8,4096]{1,0:T(8,128)(2,1)} %tail.1), channel_id=1, source_target_pairs={{0,2},{2,4},{4,6},{6,8},{8,10},{10,12},{12,14},{14,16},{16,18},{18... | collective-permute-start | bytes 196616 | tf_op jit(solution)/shard_map/ppermute | solution.py:423
  7.9 1.6 %copy-done.1 = bf16[256,4096]{1,0:T(8,128)(2,1)S(1)} copy-done((bf16[256,4096]{1,0:T(8,128)(2,1)S(1)}, bf16[256,4096]{1,0:T(8,128)(2,1)}, u32[]{:S(2)}) %copy-start.1) | copy-done | bytes 2097176
  9.5 0.9 copy-done.8
  10.5 3.1 %mix.1 = (bf16[256,2048]{1,0:T(8,128)(2,1)S(1)}, bf16[256,768]{1,0:T(8,128)(2,1)S(1)}, bf16[256,1280]{1,0:T(8,128)(2,1)S(1)}) custom-call(bf16[256,4096]{1,0:T(8,128)(2,1)S(1)} %copy-done, bf16[256,4096]{1,0:T(8,128)(2,1)S(1)} %copy-done.1, f32[3,3,4096]{2,1,0:T(4,128)S(1)} %copy-done.8), custom_call_target="tpu_custom_call" | custom-call | bytes 20000 | tf_op jit(solution)/shard_map/mix/pallas_call | solution.py:376
  13.6 4.5 %head.1 = (bf16[256,2048]{1,0:T(8,128)(2,1)S(1)}, bf16[256,768]{1,0:T(8,128)(2,1)S(1)}, bf16[256,1280]{1,0:T(8,128)(2,1)S(1)}, f32[16,4096]{1,0:T(8,128)S(1)}) custom-call(bf16[256,2048]{1,0:T(8,128)(2,1)S(1)} %get-tuple-element.34.refs_0_, ...), custom_call_target="tpu_custom_call", output_to_operand_aliasing={{0}: (0, {}), {1}: (1, {}), {2}: (2, {})} | custom-call | bytes 20000 | tf_op jit(solution)/shard_map/head/pallas_call | solution.py:376
  18.1 0.8 copy-done.3
  18.9 0.7 copy-done.5
  19.7 1.0 collective-permute-start.1
  20.7 1.6 %rev.4 = bf16[32,512]{1,0:T(8,128)(2,1)S(1)} reverse(bf16[32,512]{1,0:T(8,128)(2,1)} %param.13), dimensions={1} | reverse | bytes 65536 | tf_op jit(solution)/shard_map/jit(_flip)/rev | solution.py:427
  22.4 0.1 broadcast_in_dim.4
  22.5 0.2 copy.16
  22.8 4.4 %table.2 = (bf16[16,128,512]{2,1,0:T(8,128)(2,1)S(1)}, f32[256,2048]{1,0:T(8,128)S(1)}) custom-call(f32[32,512]{1,0:T(8,128)S(1)} %pad_maximum_fusion.refs_0_, f32[16,32]{1,0:T(8,128)S(1)} %bitcast.11, f32[16,32]{1,0:T(8,128)S(1)} %multiply_bitcast_fusion.refs_2_.refs_4_, bf16[256,2048]{1,0:T(8,128)(2,1)S(1)} %get-tuple-element.38.refs_3_), custom_call_target="tpu_custom_call" | custom-call | bytes 20000 | tf_op jit(solution)/shard_map/table/pallas_call | solution.py:376
  27.3 3.4 %collective-permute-start.3 = (f32[16,2048]{1,0:T(8,128)S(1)}, f32[16,2048]{1,0:T(8,128)S(1)}, u32[]{:S(2)}, u32[]{:S(2)}) collective-permute-start(f32[16,2048]{1,0:T(8,128)S(1)} %get-tuple-element.69), channel_id=1, source_target_pairs={{0,4},{2,6},{4,8},{6,10},{8,12},{10,14},{12,16},{14,18},{16,20},{1... | collective-permute-start | bytes 393224 | tf_op jit(solution)/shard_map/ppermute | solution.py:465
  30.7 3.6 %collective-permute-start.5 = (bf16[256,768]{1,0:T(8,128)(2,1)S(1)}, bf16[256,768]{1,0:T(8,128)(2,1)S(1)}, u32[]{:S(2)}, u32[]{:S(2)}) collective-permute-start(bf16[256,768]{1,0:T(8,128)(2,1)S(1)} %get-tuple-element.44.refs_3_.refs_7_), channel_id=1, source_target_pairs={{0,4},{2,6},{4,8},{6,10},{8,12},{10,14},{12,16},{14,18},{16,20},{1... | collective-permute-start | bytes 1179656 | tf_op jit(solution)/shard_map/ppermute | solution.py:463
  34.3 4.4 %table.3 = (bf16[16,128,512]{2,1,0:T(8,128)(2,1)S(1)}, f32[256,2048]{1,0:T(8,128)S(1)}) custom-call(f32[32,512]{1,0:T(8,128)S(1)} %pad_maximum_fusion.refs_0_, f32[16,32]{1,0:T(8,128)S(1)} %bitcast.12, f32[16,32]{1,0:T(8,128)S(1)} %multiply_bitcast_fusion.refs_2_.refs_4_, bf16[256,768]{1,0:T(8,128)(2,1)S(1)} %get-tuple-element.44.refs_3_.refs_7_, ...), custom_call_target="tpu_custom_call" | custom-call | bytes 20000 | tf_op jit(solution)/shard_map/table/pallas_call | solution.py:376
  38.8 3.5 %collective-permute-start.4 = (f32[16,2048]{1,0:T(8,128)S(1)}, f32[16,2048]{1,0:T(8,128)S(1)}, u32[]{:S(2)}, u32[]{:S(2)}) collective-permute-start(f32[16,2048]{1,0:T(8,128)S(1)} %multiply_add_fusion.3), channel_id=1, source_target_pairs={{0,8},{2,10},{4,12},{6,14},{8,16},{10,18},{12,20},{14,22},{16,24},... | collective-permute-start | bytes 393224 | tf_op jit(solution)/shard_map/ppermute | solution.py:474
  42.3 0.6 collective-permute-start.2
  42.9 3.4 %collective-permute-start.6 = (bf16[256,1280]{1,0:T(8,128)(2,1)S(1)}, bf16[256,1280]{1,0:T(8,128)(2,1)S(1)}, u32[]{:S(2)}, u32[]{:S(2)}) collective-permute-start(bf16[256,1280]{1,0:T(8,128)(2,1)S(1)} %copy-done.4), channel_id=1, source_target_pairs={{0,4},{2,6},{4,8},{6,10},{8,12},{10,14},{12,16},{14,18},{16,20},{1... | collective-permute-start | bytes 1966088 | tf_op jit(solution)/shard_map/ppermute | solution.py:470
  46.4 5.1 %collective-permute-start.8 = (f32[16,2048]{1,0:T(8,128)S(1)}, f32[16,2048]{1,0:T(8,128)S(1)}, u32[]{:S(2)}, u32[]{:S(2)}) collective-permute-start(f32[16,2048]{1,0:T(8,128)S(1)} %multiply_add_fusion.2), channel_id=1, source_target_pairs={{0,16},{2,18},{4,20},{6,22},{8,24},{10,26},{12,28},{14,30},{1,17},... | collective-permute-start | bytes 393224 | tf_op jit(solution)/shard_map/ppermute | solution.py:474
  51.5 2.5 %collective-permute-done.8 = f32[16,2048]{1,0:T(8,128)S(1)} collective-permute-done((f32[16,2048]{1,0:T(8,128)S(1)}, f32[16,2048]{1,0:T(8,128)S(1)}, u32[]{:S(2)}, u32[]{:S(2)}) %collective-permute-start.8) | collective-permute-done | bytes 131104 | tf_op jit(solution)/shard_map/ppermute | solution.py:474
  54.0 0.1 broadcast_select_fusion
  54.1 11.7 %collective-permute-done.2.refs_2_ = bf16[256,2048]{1,0:T(8,128)(2,1)S(1)} collective-permute-done((bf16[256,2048]{1,0:T(8,128)(2,1)S(1)}, bf16[256,2048]{1,0:T(8,128)(2,1)S(1)}, u32[]{:S(2)}, u32[]{:S(2)}) %collective-permute-start.2) | collective-permute-done | bytes 1048608 | tf_op jit(solution)/shard_map/ppermute | solution.py:464
  65.9 2.7 %merge.1 = (bf16[256,2048]{1,0:T(8,128)(2,1)S(1)}, bf16[256,2048]{1,0:T(8,128)(2,1)S(1)}, f32[256,2048]{1,0:T(8,128)S(1)}) custom-call(s32[1]{0:T(128)} %bitcast.refs_0_, bf16[16,128,512]{2,1,0:T(8,128)(2,1)S(1)} %get-tuple-element.39.refs_1_, bf16[256,2048]{1,0:T(8,128)(2,1)S(1)} %collective-permute-done.2.refs_2_, ...), custom_call_target="tpu_custom_call" | custom-call | bytes 20000 | tf_op jit(solution)/shard_map/merge/pallas_call | solution.py:376
  68.7 3.5 %collective-permute-start.7 = (bf16[256,2048]{1,0:T(8,128)(2,1)S(1)}, bf16[256,2048]{1,0:T(8,128)(2,1)S(1)}, u32[]{:S(2)}, u32[]{:S(2)}) collective-permute-start(bf16[256,2048]{1,0:T(8,128)(2,1)S(1)} %get-tuple-element.54), channel_id=1, source_target_pairs={{0,4},{2,6},{4,8},{6,10},{8,12},{10,14},{12,16},{14,18},{16,20},{1... | collective-permute-start | bytes 3145736 | tf_op jit(solution)/shard_map/ppermute | solution.py:496
  72.2 2.1 %collective-permute-start.10 = (f32[16,2048]{1,0:T(8,128)S(1)}, f32[16,2048]{1,0:T(8,128)S(1)}, u32[]{:S(2)}, u32[]{:S(2)}) collective-permute-start(f32[16,2048]{1,0:T(8,128)S(1)} %get-tuple-element.60), channel_id=1, source_target_pairs={{0,2},{2,0},{4,6},{6,4},{8,10},{10,8},{12,14},{14,12},{16,18},{18,... | collective-permute-start | bytes 393224 | tf_op jit(solution)/shard_map/ppermute | solution.py:492
  74.3 4.3 %pre.1 = (f32[256,2048]{1,0:T(8,128)S(1)}, f32[256,4096]{1,0:T(8,128)S(1)}) custom-call(bf16[16,128,512]{2,1,0:T(8,128)(2,1)S(1)} %get-tuple-element.46.refs_0_.refs_2_, bf16[256,768]{1,0:T(8,128)(2,1)S(1)} %collective-permute-done.5.refs_5_.refs_1_, bf16[256,1280]{1,0:T(8,128)(2,1)S(1)} %collective-permute-done.6.refs_6_.refs_2_, ...), custom_call_target="tpu_custom_call" | custom-call | bytes 20000 | tf_op jit(solution)/shard_map/pre/pallas_call | solution.py:376
  78.6 15.5 %collective-permute-done.10 = f32[16,2048]{1,0:T(8,128)S(1)} collective-permute-done((f32[16,2048]{1,0:T(8,128)S(1)}, f32[16,2048]{1,0:T(8,128)S(1)}, u32[]{:S(2)}, u32[]{:S(2)}) %collective-permute-start.10) | collective-permute-done | bytes 131104 | tf_op jit(solution)/shard_map/ppermute | solution.py:492
  94.1 5.8 %state.1.refs_5_ = f32[256,4096]{1,0:T(8,128)S(1)} custom-call(f32[256,2048]{1,0:T(8,128)S(1)} %get-tuple-element.57.refs_0_, f32[256,2048]{1,0:T(8,128)S(1)} %get-tuple-element.59.refs_1_, f32[16,4096]{1,0:T(8,128)S(1)} %maximum_select_fusion.refs_2_, f32[16,32]{1,0:T(8,128)S(1)} %bitcast.13, f32[16,32]{1,0:T(8,128)S(1)} %multiply_bitcast_fusion.refs_2_.refs_4_, ...), custom_call_target="tpu_custom_call" | custom-call | bytes 20000 | tf_op jit(solution)/shard_map/state/pallas_call | solution.py:376
  100.0 4.3 %late.1 = (bf16[256,4096]{1,0:T(8,128)(2,1)}, bf16[256,4096]{1,0:T(8,128)(2,1)S(1)}, f32[8,256]{1,0:T(8,128)S(1)}) custom-call(s32[1]{0:T(128)} %bitcast.refs_0_, bf16[16,128,512]{2,1,0:T(8,128)(2,1)S(1)} %get-tuple-element.39.refs_1_, bf16[16,128,512]{2,1,0:T(8,128)(2,1)S(1)} %get-tuple-element.46.refs_0_.refs_2_, ...), custom_call_target="tpu_custom_call" | custom-call | bytes 20000 | tf_op jit(solution)/shard_map/late/pallas_call | solution.py:376
  104.2 2.5 %psum.7.refs_0_ = f32[8,256]{1,0:T(8,128)S(1)} all-reduce(f32[8,256]{1,0:T(8,128)S(1)} %get-tuple-element.64), channel_id=1, replica_groups=mesh['ctx'=16,'width'=2] {'width'}, use_global_device_ids=true, to_apply=%region_0.1 | all-reduce | flops 2048 | bytes 16384 | tf_op jit(solution)/shard_map/psum | solution.py:528
  106.7 2.0 %norm.1 = bf16[256,4096]{1,0:T(8,128)(2,1)} custom-call(f32[8,256]{1,0:T(8,128)S(1)} %psum.7.refs_0_, f32[1,4096]{1,0:T(1,128)S(1)} %bitcast.14, bf16[256,4096]{1,0:T(8,128)(2,1)S(1)} %get-tuple-element.65.refs_2_), custom_call_target="tpu_custom_call" | custom-call | bytes 20000 | tf_op jit(solution)/shard_map/norm/pallas_call | solution.py:376
  (44 shorter events, 0.5 us)
Async XLA Ops:
  0.6 7.3 %copy-start = (bf16[256,4096]{1,0:T(8,128)(2,1)S(1)}, bf16[256,4096]{1,0:T(8,128)(2,1)}, u32[]{:S(2)}) copy-start(bf16[256,4096]{1,0:T(8,128)(2,1)} %refs_3_.1) | copy-start | bytes 6291460
  2.5 11.1 %collective-permute-start = (bf16[8,4096]{1,0:T(8,128)(2,1)}, bf16[8,4096]{1,0:T(8,128)(2,1)}, u32[]{:S(2)}, u32[]{:S(2)}) collective-permute-start(bf16[8,4096]{1,0:T(8,128)(2,1)} %tail.1), channel_id=1, source_target_pairs={{0,2},{2,4},{4,6},{6,8},{8,10},{10,12},{12,14},{14,16},{16,18},{18... | collective-permute-start | bytes 196616 | tf_op jit(solution)/shard_map/ppermute | solution.py:423
  7.9 1.6 %copy-start.1 = (bf16[256,4096]{1,0:T(8,128)(2,1)S(1)}, bf16[256,4096]{1,0:T(8,128)(2,1)}, u32[]{:S(2)}) copy-start(bf16[256,4096]{1,0:T(8,128)(2,1)} %refs_4_.2) | copy-start | bytes 6291460
  9.5 0.9 copy-start.8
  10.4 3.1 %copy-start.10 = (f32[32,16]{0,1:T(8,128)S(1)}, f32[32,16]{0,1:T(8,128)}, u32[]{:S(2)}) copy-start(f32[32,16]{0,1:T(8,128)} %param.14) | copy-start | bytes 6148
  13.6 7.1 %copy-start.14 = (f32[32,16]{0,1:T(8,128)S(1)}, f32[32,16]{0,1:T(8,128)}, u32[]{:S(2)}) copy-start(f32[32,16]{0,1:T(8,128)} %param.15) | copy-start | bytes 6148
  18.1 0.8 copy-start.3
  18.9 0.7 copy-start.5
  19.6 14.7 %copy-start.4 = (bf16[256,1280]{1,0:T(8,128)(2,1)S(1)}, bf16[256,1280]{1,0:T(8,128)(2,1)}, u32[]{:S(2)}) copy-start(bf16[256,1280]{1,0:T(8,128)(2,1)} %copy-done.3) | copy-start | bytes 1966084
  19.7 7.5 %copy-start.6 = (f32[16,4096]{1,0:T(8,128)S(1)}, f32[16,4096]{1,0:T(8,128)}, u32[]{:S(2)}) copy-start(f32[16,4096]{1,0:T(8,128)} %copy-done.5) | copy-start | bytes 786436
  19.7 7.5 %collective-permute-start.1 = (f32[16,2048]{1,0:T(8,128)S(1)}, f32[16,2048]{1,0:T(8,128)S(1)}, u32[]{:S(2)}, u32[]{:S(2)}) collective-permute-start(f32[16,2048]{1,0:T(8,128)S(1)} %slice_select_fusion.2), channel_id=1, source_target_pairs={{0,2},{2,0},{4,6},{6,4},{8,10},{10,8},{12,14},{14,12},{16,18},{18,... | collective-permute-start | bytes 393224 | tf_op jit(solution)/shard_map/ppermute | solution.py:443
  27.2 3.5 %copy-start.12 = (f32[16,2048]{1,0:T(8,128)}, f32[16,2048]{1,0:T(8,128)S(1)}, u32[]{:S(2)}) copy-start(f32[16,2048]{1,0:T(8,128)S(1)} %collective-permute-done.1) | copy-start | bytes 393220
  27.3 11.5 %collective-permute-start.3 = (f32[16,2048]{1,0:T(8,128)S(1)}, f32[16,2048]{1,0:T(8,128)S(1)}, u32[]{:S(2)}, u32[]{:S(2)}) collective-permute-start(f32[16,2048]{1,0:T(8,128)S(1)} %get-tuple-element.69), channel_id=1, source_target_pairs={{0,4},{2,6},{4,8},{6,10},{8,12},{10,14},{12,16},{14,18},{16,20},{1... | collective-permute-start | bytes 393224 | tf_op jit(solution)/shard_map/ppermute | solution.py:465
  30.7 23.3 %copy-start.13 = (f32[16,2048]{1,0:T(8,128)S(1)}, f32[16,2048]{1,0:T(8,128)}, u32[]{:S(2)}) copy-start(f32[16,2048]{1,0:T(8,128)} %copy-done.12) | copy-start | bytes 393220
  30.7 12.2 %collective-permute-start.5 = (bf16[256,768]{1,0:T(8,128)(2,1)S(1)}, bf16[256,768]{1,0:T(8,128)(2,1)S(1)}, u32[]{:S(2)}, u32[]{:S(2)}) collective-permute-start(bf16[256,768]{1,0:T(8,128)(2,1)S(1)} %get-tuple-element.44.refs_3_.refs_7_), channel_id=1, source_target_pairs={{0,4},{2,6},{4,8},{6,10},{8,12},{10,14},{12,16},{14,18},{16,20},{1... | collective-permute-start | bytes 1179656 | tf_op jit(solution)/shard_map/ppermute | solution.py:463
  38.8 7.5 %collective-permute-start.4 = (f32[16,2048]{1,0:T(8,128)S(1)}, f32[16,2048]{1,0:T(8,128)S(1)}, u32[]{:S(2)}, u32[]{:S(2)}) collective-permute-start(f32[16,2048]{1,0:T(8,128)S(1)} %multiply_add_fusion.3), channel_id=1, source_target_pairs={{0,8},{2,10},{4,12},{6,14},{8,16},{10,18},{12,20},{14,22},{16,24},... | collective-permute-start | bytes 393224 | tf_op jit(solution)/shard_map/ppermute | solution.py:474
  42.3 23.6 %collective-permute-start.2 = (bf16[256,2048]{1,0:T(8,128)(2,1)S(1)}, bf16[256,2048]{1,0:T(8,128)(2,1)S(1)}, u32[]{:S(2)}, u32[]{:S(2)}) collective-permute-start(bf16[256,2048]{1,0:T(8,128)(2,1)S(1)} %get-tuple-element.38.refs_3_), channel_id=1, source_target_pairs={{0,2},{2,0},{4,6},{6,4},{8,10},{10,8},{12,14},{14,12},{16,18},{18,... | collective-permute-start | bytes 3145736 | tf_op jit(solution)/shard_map/ppermute | solution.py:464
  42.9 23.0 %collective-permute-start.6 = (bf16[256,1280]{1,0:T(8,128)(2,1)S(1)}, bf16[256,1280]{1,0:T(8,128)(2,1)S(1)}, u32[]{:S(2)}, u32[]{:S(2)}) collective-permute-start(bf16[256,1280]{1,0:T(8,128)(2,1)S(1)} %copy-done.4), channel_id=1, source_target_pairs={{0,4},{2,6},{4,8},{6,10},{8,12},{10,14},{12,16},{14,18},{16,20},{1... | collective-permute-start | bytes 1966088 | tf_op jit(solution)/shard_map/ppermute | solution.py:470
  46.4 7.6 %collective-permute-start.8 = (f32[16,2048]{1,0:T(8,128)S(1)}, f32[16,2048]{1,0:T(8,128)S(1)}, u32[]{:S(2)}, u32[]{:S(2)}) collective-permute-start(f32[16,2048]{1,0:T(8,128)S(1)} %multiply_add_fusion.2), channel_id=1, source_target_pairs={{0,16},{2,18},{4,20},{6,22},{8,24},{10,26},{12,28},{14,30},{1,17},... | collective-permute-start | bytes 393224 | tf_op jit(solution)/shard_map/ppermute | solution.py:474
  65.9 8.4 %copy-start.2 = (bf16[256,4096]{1,0:T(8,128)(2,1)S(1)}, bf16[256,4096]{1,0:T(8,128)(2,1)}, u32[]{:S(2)}) copy-start(bf16[256,4096]{1,0:T(8,128)(2,1)} %refs_4_.3) | copy-start | bytes 6291460
  65.9 8.4 %copy-start.9 = (f32[3,3,4096]{2,1,0:T(4,128)S(1)}, f32[3,3,4096]{2,1,0:T(4,128)}, u32[]{:S(2)}) copy-start(f32[3,3,4096]{2,1,0:T(4,128)} %refs_6_.4) | copy-start | bytes 442372
  68.6 31.3 %collective-permute-start.9 = (bf16[256,2048]{1,0:T(8,128)(2,1)S(1)}, bf16[256,2048]{1,0:T(8,128)(2,1)S(1)}, u32[]{:S(2)}, u32[]{:S(2)}) collective-permute-start(bf16[256,2048]{1,0:T(8,128)(2,1)S(1)} %get-tuple-element.56), channel_id=1, source_target_pairs={{0,2},{2,0},{4,6},{6,4},{8,10},{10,8},{12,14},{14,12},{16,18},{18,... | collective-permute-start | bytes 3145736 | tf_op jit(solution)/shard_map/ppermute | solution.py:495
  68.7 31.3 %collective-permute-start.7 = (bf16[256,2048]{1,0:T(8,128)(2,1)S(1)}, bf16[256,2048]{1,0:T(8,128)(2,1)S(1)}, u32[]{:S(2)}, u32[]{:S(2)}) collective-permute-start(bf16[256,2048]{1,0:T(8,128)(2,1)S(1)} %get-tuple-element.54), channel_id=1, source_target_pairs={{0,4},{2,6},{4,8},{6,10},{8,12},{10,14},{12,16},{14,18},{16,20},{1... | collective-permute-start | bytes 3145736 | tf_op jit(solution)/shard_map/ppermute | solution.py:496
  72.2 21.9 %collective-permute-start.10 = (f32[16,2048]{1,0:T(8,128)S(1)}, f32[16,2048]{1,0:T(8,128)S(1)}, u32[]{:S(2)}, u32[]{:S(2)}) collective-permute-start(f32[16,2048]{1,0:T(8,128)S(1)} %get-tuple-element.60), channel_id=1, source_target_pairs={{0,2},{2,0},{4,6},{6,4},{8,10},{10,8},{12,14},{14,12},{16,18},{18,... | collective-permute-start | bytes 393224 | tf_op jit(solution)/shard_map/ppermute | solution.py:492
  74.3 19.8 %copy-start.7 = (bf16[256,4096]{1,0:T(8,128)(2,1)S(1)}, bf16[256,4096]{1,0:T(8,128)(2,1)}, u32[]{:S(2)}) copy-start(bf16[256,4096]{1,0:T(8,128)(2,1)} %refs_6_.5) | copy-start | bytes 6291460
  99.9 6.8 %copy-start.11 = (f32[4096]{0:T(1024)S(1)}, f32[4096]{0:T(1024)}, u32[]{:S(2)}) copy-start(f32[4096]{0:T(1024)} %param.17) | copy-start | bytes 49156

commit v3 on v2

--- a/solution.py
+++ b/solution.py
@@ -102,6 +102,8 @@
 
 def head_kernel(sizes, *refs):
     k_ref, v_ref, tail_ref, sk_ref, rate_ref, *x_refs, f_ref = refs[len(sizes) :]
+    for source, x_ref in zip(refs, x_refs):
+        x_ref[...] = source[...]
     length = k_ref.shape[0]
 
     def make(start, x_ref):
@@ -188,12 +190,14 @@
 
 
 def merge_kernel(
-    first,
+    a_parts,
     b_parts,
     odd_ref,
     tb_ref,
-    near_ref,
-    own_ref,
+    near1_ref,
+    near2_ref,
+    own1_ref,
+    own2_ref,
     f_ref,
     far1_ref,
     far2_ref,
@@ -204,19 +208,27 @@
     keep_ref,
 ):
     odd = odd_ref[0]
+    edge = a_parts[0] * LANES
     middle = b_parts[0] * LANES
 
     @pl.when(odd == 1)
     def _():
-        send_a_ref[...] = own_ref[...]
+        send_a_ref[:, :edge] = own1_ref[...]
+        send_a_ref[:, edge:] = own2_ref[...]
         send_b_ref[:, :middle] = far1_ref[...]
         send_b_ref[:, middle:] = far2_ref[...]
 
-        def one(g):
-            lanes = at(g)
-            keep_ref[:, lanes] = f_ref[:, lanes] + dot(lag_one(tb_ref, g), near_ref[:, lanes])
-
-        each(first, one, 2)
+        def make(skip, near_ref):
+            def one(g):
+                wide = at(g + skip)
+                keep_ref[:, wide] = f_ref[:, wide] + dot(
+                    lag_one(tb_ref, g + skip), near_ref[:, at(g)]
+                )
+
+            return one
+
+        each(a_parts[0], make(0, near1_ref), 2)
+        each(a_parts[1], make(a_parts[0], near2_ref), 2)
 
     @pl.when(odd == 0)
     def _():
@@ -224,14 +236,17 @@
         send_b_ref[:, :middle] = xb1_ref[...]
         send_b_ref[:, middle:] = xb2_ref[...]
 
-        def one(g):
-            lanes = at(g)
-            send_a_ref[:, lanes] = (
-                dot(lag_one(tb_ref, g), near_ref[:, lanes])
-                + dot(lag_two(tb_ref, g), own_ref[:, lanes])
-            ).astype(BF16)
-
-        each(first, one, 2)
+        def make(skip, near_ref, own_ref):
+            def one(g):
+                send_a_ref[:, at(g + skip)] = (
+                    dot(lag_one(tb_ref, g + skip), near_ref[:, at(g)])
+                    + dot(lag_two(tb_ref, g + skip), own_ref[:, at(g)])
+                ).astype(BF16)
+
+            return one
+
+        each(a_parts[0], make(0, near1_ref, own1_ref), 2)
+        each(a_parts[1], make(a_parts[0], near2_ref, own2_ref), 2)
 
 
 def pre_kernel(
@@ -404,7 +419,8 @@
     first = groups // 2
     second = groups - first
     b_parts = ((second * 3) // 8, second - (second * 3) // 8)
-    sizes = (first, *b_parts)
+    a_parts = ((first * 3) // 8, first - (first * 3) // 8)
+    sizes = (*a_parts, *b_parts)
     wide_a = first * LANES
     wide_b = second * LANES
     odd = (lax.axis_index("ctx") % 2).astype(jnp.int32).reshape(1)
@@ -431,12 +447,11 @@
     mixed = call(
         lambda *refs: mix_kernel(sizes, *refs), blocks, "mix", key_proj, value_proj, short_kernel
     )
-    xa, xb1, xb2, window = call(
+    xa1, xa2, xb1, xb2, window = call(
         lambda *refs: head_kernel(sizes, *refs),
         [*blocks, shape((modes, channels), F32)],
         "head",
-        *mixed, key_proj, value_proj, after(tail, mixed[0]), short_kernel, rate_t,
-        alias={i: i for i in range(len(sizes))},
+        *mixed, key_proj, value_proj, tail, short_kernel, rate_t,
     )
     half = channels // 2
     mine = jnp.where(is_odd, window[:, half:], window[:, :half])
@@ -457,42 +472,45 @@
     wide_rate = jnp.where(is_odd, wide_rate[:, half:], wide_rate[:, :half])
     decay = lambda blocks: jnp.exp(-wide_rate * (length * blocks))
 
-    ta, part_a = tables(0, (first,), (xa,), source)
+    ta, part_a = tables(0, a_parts, (xa1, xa2), source)
     beside = after(beside, part_a)
     pair = decay(1.0) * jnp.where(is_odd, beside, mine) + jnp.where(is_odd, mine, beside)
     far1 = lax.ppermute(xb1, "ctx", shifted_pairs(devices, 2))
-    near_a = lax.ppermute(xa, "ctx", swap_pairs(devices))
+    near1 = lax.ppermute(xa1, "ctx", swap_pairs(devices))
     got = lax.ppermute(pair, "ctx", shifted_pairs(devices, 2))
     tb, part_b = tables(first, b_parts, (xb1, xb2), after(source, pair))
     before = after(got, part_b)
     pair = pair + decay(2.0) * before
-    far1 = after(far1, part_b)
-    far2 = lax.ppermute(after(xb2, far1, pair), "ctx", shifted_pairs(devices, 2))
-    near_a = after(near_a, part_b)
+    far1, near1 = after(far1, part_b), after(near1, part_b)
+    far2 = lax.ppermute(after(xb2, far1, near1, pair), "ctx", shifted_pairs(devices, 2))
+    near2 = lax.ppermute(after(xa2, far1, near1, pair), "ctx", swap_pairs(devices))
     hop = 4
     while hop < devices:
+        last = hop * 2 >= devices
+        if last:
+            far2, near2 = after(far2, pair), after(near2, pair)
         got = lax.ppermute(pair, "ctx", shifted_pairs(devices, hop))
+        if last:
+            send_a, send_b, keep_a = call(
+                lambda *refs: merge_kernel(a_parts, b_parts, *refs),
+                [
+                    shape((length, wide_a), BF16),
+                    shape((length, wide_b), BF16),
+                    shape((length, wide_a), F32),
+                ],
+                "merge",
+                odd, ta, near1, near2, xa1, xa2, part_a, far1, far2, xb1, xb2,
+                smem=1,
+            )
+            got = after(got, keep_a)
         before = before + decay(float(hop - 2)) * got
         pair = pair + decay(float(hop)) * got
         hop *= 2
-        if hop * 2 == devices:
-            far2, near_a = after(far2, pair), after(near_a, pair)
-    send_a, send_b, keep_a = call(
-        lambda *refs: merge_kernel(first, b_parts, *refs),
-        [
-            shape((length, wide_a), BF16),
-            shape((length, wide_b), BF16),
-            shape((length, wide_a), F32),
-        ],
-        "merge",
-        odd, ta, near_a, xa, part_a, far1, far2, xb1, xb2,
-        smem=1,
-    )
     onward = decay(1.0) * before + jnp.where(is_odd, beside, mine)
     other = lax.ppermute(
         after(jnp.where(is_odd, before, onward), keep_a), "ctx", swap_pairs(devices)
     )
-    near_b = lax.ppermute(after(send_b, onward), "ctx", swap_pairs(devices))
+    near_b = lax.ppermute(after(send_b, other), "ctx", swap_pairs(devices))
     got_a = lax.ppermute(send_a, "ctx", shifted_pairs(devices, 2))
     acc_b, query = call(
         lambda *refs: pre_kernel(first, *b_parts, *refs),
@@ -500,7 +518,6 @@
         "pre",
         tb, far1, far2, after(part_b, keep_a), query_proj, tail, short_kernel,
     )
-    other = after(other, query)
     state = jnp.where(
         is_odd,
         jnp.concatenate([other, onward], axis=1),

time: 109 us -> 98.4 us (0.903)
  waiting for transfers between devices: 29.7 us -> 17.8 us
  starting transfers between devices: 31.7 us -> 34.7 us
  local copies, waits for them, and re-layouts: 6.11 us -> 3.18 us
    ppermute x1, waiting for transfers between devices: 15.5 us -> 0.65 us  [body(): lax.ppermute(after(jnp.where(is_odd, before, onward), keep_a), 'ctx', swa...]
    ppermute x1, waiting for transfers between devices: 0.01 us -> 6.92 us  [body(): got_a = lax.ppermute(send_a, 'ctx', shifted_pairs(devices, 2))]
    ppermute x3 -> x4, starting transfers between devices: 4.12 us -> 7.14 us  [the longest x1 3.56 us: body(): lax.ppermute(after(xb2, far1, near1, pair), 'ctx', shifted_pairs(devices,...]
    ppermute x2, waiting for transfers between devices: 2.51 us -> 0.01 us  [body(): got = lax.ppermute(pair, 'ctx', shifted_pairs(devices, hop))]
    ppermute x1, starting transfers between devices: 3.5 us -> 5.52 us  [body(): got_a = lax.ppermute(send_a, 'ctx', shifted_pairs(devices, 2))]
    ppermute x1, starting transfers between devices: 2.07 us -> 0.11 us  [body(): lax.ppermute(after(jnp.where(is_odd, before, onward), keep_a), 'ctx', swa...]
    unnamed x31 -> x35, local copies, waits for them, and re-layouts: 4.26 us -> 2.62 us
    ppermute x3 -> x4, waiting for transfers between devices: 11.7 us -> 10.2 us  [the longest x1 4.41 us: body(): lax.ppermute(after(xa2, far1, near1, pair), 'ctx', swap_pairs(devices))]
  transfers between devices with their start and end apart: 11 -> 12, of which waited for: 3 -> 5; matrix products, arithmetic and copies ran while one was open for 2% -> 1% of each run, Pallas kernels for 20% -> 26%
where the time goes in v3:
time: 98.4 us; the launch traced here: 97.7 us
  Pallas kernels  38.2 us (39%)
  starting transfers between devices  34.7 us (35%)
  waiting for transfers between devices  17.8 us (18%)
  local copies, waits for them, and re-layouts  3.18 us (3%)
  blocking collectives  2.5 us (3%)
  between operations  1.02 us (1%)
    pallas_call x9, Pallas kernels, call(): pl.pallas_call(kernel, in_specs=specs, out_specs=outs, out_shape=out_shap...  36.4 us
    ppermute x2, starting transfers between devices, body(): got = lax.ppermute(pair, 'ctx', shifted_pairs(devices, hop))  8.7 us
    ppermute x1, waiting for transfers between devices, body(): got_a = lax.ppermute(send_a, 'ctx', shifted_pairs(devices, 2))  6.92 us
    ppermute x1, starting transfers between devices, body(): got_a = lax.ppermute(send_a, 'ctx', shifted_pairs(devices, 2))  5.52 us
    ppermute x1, starting transfers between devices, body(): tail = lax.ppermute(own_tail, 'ctx', shifted_pairs(devices, 1))  4.83 us
    ppermute x1, waiting for transfers between devices, body(): lax.ppermute(after(xa2, far1, near1, pair), 'ctx', swap_pairs(devices))  4.41 us
    ppermute x1, waiting for transfers between devices, body(): near_b = lax.ppermute(after(send_b, other), 'ctx', swap_pairs(devices))  3.62 us
    ppermute x1, starting transfers between devices, body(): lax.ppermute(after(xb2, far1, near1, pair), 'ctx', shifted_pairs(devices,...  3.56 us
  transfers between devices with their start and end apart: 12, of which 5 were waited for; matrix products, arithmetic and copies ran while one was open for 1% of the time, Pallas kernels for 26%

profile of v3, /device:TPU:0, one launch (start us, length us, event | category | flops | bytes accessed | tf_op | source)
XLA Modules:
  0.0 97.7 jit_solution(14237350234741525514)
XLA Ops:
  0.7 1.8 %tail.1 = bf16[8,4096]{1,0:T(8,128)(2,1)} custom-call(bf16[256,4096]{1,0:T(8,128)(2,1)} %refs_4_.3, bf16[256,4096]{1,0:T(8,128)(2,1)} %refs_4_.2, bf16[256,4096]{1,0:T(8,128)(2,1)} %refs_5_.1), custom_call_target="tpu_custom_call" | custom-call | tf_op jit(solution)/shard_map/tail/pallas_call | solution.py:431
  2.5 4.8 %collective-permute-start = (bf16[8,4096]{1,0:T(8,128)(2,1)}, bf16[8,4096]{1,0:T(8,128)(2,1)S(1)}, u32[]{:S(2)}, u32[]{:S(2)}) collective-permute-start(bf16[8,4096]{1,0:T(8,128)(2,1)} %tail.1), channel_id=1, source_target_pairs={{0,2},{2,4},{4,6},{6,8},{8,10},{10,12},{12,14},{14,16},{16,18},{18... | collective-permute-start | bytes 196616 | tf_op jit(solution)/shard_map/ppermute | solution.py:439
  7.4 1.6 %copy-done.1 = bf16[256,4096]{1,0:T(8,128)(2,1)S(1)} copy-done((bf16[256,4096]{1,0:T(8,128)(2,1)S(1)}, bf16[256,4096]{1,0:T(8,128)(2,1)}, u32[]{:S(2)}) %copy-start.1) | copy-done | bytes 2097176
  9.0 3.1 %mix.1 = (bf16[256,768]{1,0:T(8,128)(2,1)S(1)}, bf16[256,1280]{1,0:T(8,128)(2,1)S(1)}, bf16[256,768]{1,0:T(8,128)(2,1)S(1)}, bf16[256,1280]{1,0:T(8,128)(2,1)S(1)}) custom-call(bf16[256,4096]{1,0:T(8,128)(2,1)S(1)} %copy-done, bf16[256,4096]{1,0:T(8,128)(2,1)S(1)} %copy-done.1, f32[3,3,4096]{2,1,0:T(4,128)S(1)} %copy-done.6), custom_call_target="tpu_custom_call" | custom-call | bytes 20000 | tf_op jit(solution)/shard_map/mix/pallas_call | solution.py:391
  12.1 4.4 %head.1 = (bf16[256,768]{1,0:T(8,128)(2,1)}, bf16[256,1280]{1,0:T(8,128)(2,1)S(1)}, bf16[256,768]{1,0:T(8,128)(2,1)S(1)}, bf16[256,1280]{1,0:T(8,128)(2,1)S(1)}, f32[16,4096]{1,0:T(8,128)S(1)}) custom-call(bf16[256,768]{1,0:T(8,128)(2,1)S(1)} %get-tuple-element.36.refs_0_, bf16[256,1280]{1,0:T(8,128)(2,1)S(1)} %get-tuple-element.37.refs_1_, ...), custom_call_target="tpu_custom_call" | custom-call | bytes 20000 | tf_op jit(solution)/shard_map/head/pallas_call | solution.py:391
  16.5 0.7 copy-done.3
  17.2 0.1 copy-done.9
  17.3 1.5 %collective-permute-start.1 = (f32[16,2048]{1,0:T(8,128)S(1)}, f32[16,2048]{1,0:T(8,128)S(1)}, u32[]{:S(2)}, u32[]{:S(2)}) collective-permute-start(f32[16,2048]{1,0:T(8,128)S(1)} %slice_select_fusion.2), channel_id=1, source_target_pairs={{0,2},{2,0},{4,6},{6,4},{8,10},{10,8},{12,14},{14,12},{16,18},{18,... | collective-permute-start | bytes 393224 | tf_op jit(solution)/shard_map/ppermute | solution.py:458
  18.8 0.3 rev.4
  19.4 0.2 copy.13
  19.7 5.4 %table.2 = (bf16[16,128,512]{2,1,0:T(8,128)(2,1)S(1)}, f32[256,2048]{1,0:T(8,128)S(1)}) custom-call(f32[32,512]{1,0:T(8,128)S(1)} %pad_maximum_fusion.refs_0_, f32[16,32]{1,0:T(8,128)S(1)} %bitcast.11, f32[16,32]{1,0:T(8,128)S(1)} %multiply_bitcast_fusion.refs_2_.refs_4_, bf16[256,768]{1,0:T(8,128)(2,1)} %get-tuple-element.40.refs_3_.refs_4_, ...), custom_call_target="tpu_custom_call" | custom-call | bytes 20000 | tf_op jit(solution)/shard_map/table/pallas_call | solution.py:391
  25.2 3.4 %collective-permute-start.4 = (f32[16,2048]{1,0:T(8,128)S(1)}, f32[16,2048]{1,0:T(8,128)S(1)}, u32[]{:S(2)}, u32[]{:S(2)}) collective-permute-start(f32[16,2048]{1,0:T(8,128)S(1)} %get-tuple-element.73), channel_id=1, source_target_pairs={{0,4},{2,6},{4,8},{6,10},{8,12},{10,14},{12,16},{14,18},{16,20},{1... | collective-permute-start | bytes 393224 | tf_op jit(solution)/shard_map/ppermute | solution.py:480
  28.6 0.6 collective-permute-start.2
  29.2 3.5 %collective-permute-start.3 = (bf16[256,768]{1,0:T(8,128)(2,1)S(1)}, bf16[256,768]{1,0:T(8,128)(2,1)S(1)}, u32[]{:S(2)}, u32[]{:S(2)}) collective-permute-start(bf16[256,768]{1,0:T(8,128)(2,1)S(1)} %copy-done.10), channel_id=1, source_target_pairs={{0,4},{2,6},{4,8},{6,10},{8,12},{10,14},{12,16},{14,18},{16,20},{1... | collective-permute-start | bytes 1179656 | tf_op jit(solution)/shard_map/ppermute | solution.py:478
  32.7 4.4 %table.3 = (bf16[16,128,512]{2,1,0:T(8,128)(2,1)S(1)}, f32[256,2048]{1,0:T(8,128)S(1)}) custom-call(f32[32,512]{1,0:T(8,128)S(1)} %pad_maximum_fusion.refs_0_, f32[16,32]{1,0:T(8,128)S(1)} %bitcast.12, f32[16,32]{1,0:T(8,128)S(1)} %multiply_bitcast_fusion.refs_2_.refs_4_, bf16[256,768]{1,0:T(8,128)(2,1)S(1)} %copy-done.10, ...), custom_call_target="tpu_custom_call" | custom-call | bytes 20000 | tf_op jit(solution)/shard_map/table/pallas_call | solution.py:391
  37.2 3.4 %collective-permute-start.6 = (f32[16,2048]{1,0:T(8,128)S(1)}, f32[16,2048]{1,0:T(8,128)S(1)}, u32[]{:S(2)}, u32[]{:S(2)}) collective-permute-start(f32[16,2048]{1,0:T(8,128)S(1)} %multiply_add_fusion.3), channel_id=1, source_target_pairs={{0,8},{2,10},{4,12},{6,14},{8,16},{10,18},{12,20},{14,22},{16,24},... | collective-permute-start | bytes 393224 | tf_op jit(solution)/shard_map/ppermute | solution.py:492
  40.7 1.6 %collective-permute-start.5 = (bf16[256,1280]{1,0:T(8,128)(2,1)S(1)}, bf16[256,1280]{1,0:T(8,128)(2,1)S(1)}, u32[]{:S(2)}, u32[]{:S(2)}) collective-permute-start(bf16[256,1280]{1,0:T(8,128)(2,1)S(1)} %get-tuple-element.54.refs_4_.refs_5_), channel_id=1, source_target_pairs={{0,2},{2,0},{4,6},{6,4},{8,10},{10,8},{12,14},{14,12},{16,18},{18,... | collective-permute-start | bytes 1966088 | tf_op jit(solution)/shard_map/ppermute | solution.py:486
  42.2 3.6 %collective-permute-start.7 = (bf16[256,1280]{1,0:T(8,128)(2,1)S(1)}, bf16[256,1280]{1,0:T(8,128)(2,1)S(1)}, u32[]{:S(2)}, u32[]{:S(2)}) collective-permute-start(bf16[256,1280]{1,0:T(8,128)(2,1)S(1)} %get-tuple-element.56.refs_4_.refs_10_), channel_id=1, source_target_pairs={{0,4},{2,6},{4,8},{6,10},{8,12},{10,14},{12,16},{14,18},{16,20},{1... | collective-permute-start | bytes 1966088 | tf_op jit(solution)/shard_map/ppermute | solution.py:485
  45.8 5.3 %collective-permute-start.9 = (f32[16,2048]{1,0:T(8,128)S(1)}, f32[16,2048]{1,0:T(8,128)S(1)}, u32[]{:S(2)}, u32[]{:S(2)}) collective-permute-start(f32[16,2048]{1,0:T(8,128)S(1)} %multiply_add_fusion.2), channel_id=1, source_target_pairs={{0,16},{2,18},{4,20},{6,22},{8,24},{10,26},{12,28},{14,30},{1,17},... | collective-permute-start | bytes 393224 | tf_op jit(solution)/shard_map/ppermute | solution.py:492
  51.1 4.4 %collective-permute-done.5.refs_3_ = bf16[256,1280]{1,0:T(8,128)(2,1)S(1)} collective-permute-done((bf16[256,1280]{1,0:T(8,128)(2,1)S(1)}, bf16[256,1280]{1,0:T(8,128)(2,1)S(1)}, u32[]{:S(2)}, u32[]{:S(2)}) %collective-permute-start.5) | collective-permute-done | bytes 655392 | tf_op jit(solution)/shard_map/ppermute | solution.py:486
  55.5 2.1 %collective-permute-done.7.refs_8_.refs_2_ = bf16[256,1280]{1,0:T(8,128)(2,1)S(1)} collective-permute-done((bf16[256,1280]{1,0:T(8,128)(2,1)S(1)}, bf16[256,1280]{1,0:T(8,128)(2,1)S(1)}, u32[]{:S(2)}, u32[]{:S(2)}) %collective-permute-start.7) | collective-permute-done | bytes 655392 | tf_op jit(solution)/shard_map/ppermute | solution.py:485
  57.7 3.7 %merge.1 = (bf16[256,2048]{1,0:T(8,128)(2,1)S(1)}, bf16[256,2048]{1,0:T(8,128)(2,1)S(1)}, f32[256,2048]{1,0:T(8,128)S(1)}) custom-call(s32[1]{0:T(128)} %bitcast.refs_0_, bf16[16,128,512]{2,1,0:T(8,128)(2,1)S(1)} %get-tuple-element.42.refs_1_, bf16[256,768]{1,0:T(8,128)(2,1)S(1)} %collective-permute-done.2.refs_2_, ...), custom_call_target="tpu_custom_call" | custom-call | bytes 20000 | tf_op jit(solution)/shard_map/merge/pallas_call | solution.py:391
  61.6 5.5 %collective-permute-start.8 = (bf16[256,2048]{1,0:T(8,128)(2,1)S(1)}, bf16[256,2048]{1,0:T(8,128)(2,1)S(1)}, u32[]{:S(2)}, u32[]{:S(2)}) collective-permute-start(bf16[256,2048]{1,0:T(8,128)(2,1)S(1)} %get-tuple-element.58), channel_id=1, source_target_pairs={{0,4},{2,6},{4,8},{6,10},{8,12},{10,14},{12,16},{14,18},{16,20},{1... | collective-permute-start | bytes 3145736 | tf_op jit(solution)/shard_map/ppermute | solution.py:514
  67.1 0.7 collective-permute-done.10
  67.8 1.4 %collective-permute-start.11 = (bf16[256,2048]{1,0:T(8,128)(2,1)S(1)}, bf16[256,2048]{1,0:T(8,128)(2,1)S(1)}, u32[]{:S(2)}, u32[]{:S(2)}) collective-permute-start(bf16[256,2048]{1,0:T(8,128)(2,1)S(1)} %get-tuple-element.63), channel_id=1, source_target_pairs={{0,2},{2,0},{4,6},{6,4},{8,10},{10,8},{12,14},{14,12},{16,18},{18,... | collective-permute-start | bytes 3145736 | tf_op jit(solution)/shard_map/ppermute | solution.py:513
  69.2 3.3 %pre.1 = (f32[256,2048]{1,0:T(8,128)S(1)}, f32[256,4096]{1,0:T(8,128)S(1)}) custom-call(bf16[16,128,512]{2,1,0:T(8,128)(2,1)S(1)} %get-tuple-element.49.refs_0_.refs_2_, bf16[256,768]{1,0:T(8,128)(2,1)S(1)} %collective-permute-done.3.refs_7_.refs_1_, bf16[256,1280]{1,0:T(8,128)(2,1)S(1)} %collective-permute-done.7.refs_8_.refs_2_, ...), custom_call_target="tpu_custom_call" | custom-call | bytes 20000 | tf_op jit(solution)/shard_map/pre/pallas_call | solution.py:391
  72.5 5.8 %state.1.refs_5_ = f32[256,4096]{1,0:T(8,128)S(1)} custom-call(f32[256,2048]{1,0:T(8,128)S(1)} %get-tuple-element.60.refs_0_, f32[256,2048]{1,0:T(8,128)S(1)} %get-tuple-element.65.refs_1_, f32[16,4096]{1,0:T(8,128)S(1)} %maximum_select_fusion.refs_2_, f32[16,32]{1,0:T(8,128)S(1)} %bitcast.13, f32[16,32]{1,0:T(8,128)S(1)} %multiply_bitcast_fusion.refs_2_.refs_4_, ...), custom_call_target="tpu_custom_call" | custom-call | bytes 20000 | tf_op jit(solution)/shard_map/state/pallas_call | solution.py:391
  78.4 6.9 %collective-permute-done.8.refs_3_ = bf16[256,2048]{1,0:T(8,128)(2,1)S(1)} collective-permute-done((bf16[256,2048]{1,0:T(8,128)(2,1)S(1)}, bf16[256,2048]{1,0:T(8,128)(2,1)S(1)}, u32[]{:S(2)}, u32[]{:S(2)}) %collective-permute-start.8) | collective-permute-done | bytes 1048608 | tf_op jit(solution)/shard_map/ppermute | solution.py:514
  85.3 3.6 %collective-permute-done.11.refs_4_ = bf16[256,2048]{1,0:T(8,128)(2,1)S(1)} collective-permute-done((bf16[256,2048]{1,0:T(8,128)(2,1)S(1)}, bf16[256,2048]{1,0:T(8,128)(2,1)S(1)}, u32[]{:S(2)}, u32[]{:S(2)}) %collective-permute-start.11) | collective-permute-done | bytes 1048608 | tf_op jit(solution)/shard_map/ppermute | solution.py:513
  89.0 4.2 %late.1 = (bf16[256,4096]{1,0:T(8,128)(2,1)}, bf16[256,4096]{1,0:T(8,128)(2,1)S(1)}, f32[8,256]{1,0:T(8,128)S(1)}) custom-call(s32[1]{0:T(128)} %bitcast.refs_0_, bf16[16,128,512]{2,1,0:T(8,128)(2,1)S(1)} %get-tuple-element.42.refs_1_, bf16[16,128,512]{2,1,0:T(8,128)(2,1)S(1)} %get-tuple-element.49.refs_0_.refs_2_, ...), custom_call_target="tpu_custom_call" | custom-call | bytes 20000 | tf_op jit(solution)/shard_map/late/pallas_call | solution.py:391
  93.2 2.5 %psum.7.refs_0_ = f32[8,256]{1,0:T(8,128)S(1)} all-reduce(f32[8,256]{1,0:T(8,128)S(1)} %get-tuple-element.68), channel_id=1, replica_groups=mesh['ctx'=16,'width'=2] {'width'}, use_global_device_ids=true, to_apply=%region_0.1 | all-reduce | flops 2048 | bytes 16384 | tf_op jit(solution)/shard_map/psum | solution.py:545
  95.7 2.0 %norm.1 = bf16[256,4096]{1,0:T(8,128)(2,1)} custom-call(f32[8,256]{1,0:T(8,128)S(1)} %psum.7.refs_0_, f32[1,4096]{1,0:T(1,128)S(1)} %bitcast.14, bf16[256,4096]{1,0:T(8,128)(2,1)S(1)} %get-tuple-element.69.refs_2_), custom_call_target="tpu_custom_call" | custom-call | bytes 20000 | tf_op jit(solution)/shard_map/norm/pallas_call | solution.py:391
  (50 shorter events, 0.8 us)
Async XLA Ops:
  0.6 6.7 %copy-start = (bf16[256,4096]{1,0:T(8,128)(2,1)S(1)}, bf16[256,4096]{1,0:T(8,128)(2,1)}, u32[]{:S(2)}) copy-start(bf16[256,4096]{1,0:T(8,128)(2,1)} %refs_4_.2) | copy-start | bytes 6291460
  0.6 6.7 %copy-start.6 = (f32[3,3,4096]{2,1,0:T(4,128)S(1)}, f32[3,3,4096]{2,1,0:T(4,128)}, u32[]{:S(2)}) copy-start(f32[3,3,4096]{2,1,0:T(4,128)} %refs_6_.2) | copy-start | bytes 442372
  2.5 9.6 %collective-permute-start = (bf16[8,4096]{1,0:T(8,128)(2,1)}, bf16[8,4096]{1,0:T(8,128)(2,1)S(1)}, u32[]{:S(2)}, u32[]{:S(2)}) collective-permute-start(bf16[8,4096]{1,0:T(8,128)(2,1)} %tail.1), channel_id=1, source_target_pairs={{0,2},{2,4},{4,6},{6,8},{8,10},{10,12},{12,14},{14,16},{16,18},{18... | collective-permute-start | bytes 196616 | tf_op jit(solution)/shard_map/ppermute | solution.py:439
  7.4 1.6 %copy-start.1 = (bf16[256,4096]{1,0:T(8,128)(2,1)S(1)}, bf16[256,4096]{1,0:T(8,128)(2,1)}, u32[]{:S(2)}) copy-start(bf16[256,4096]{1,0:T(8,128)(2,1)} %refs_5_.1) | copy-start | bytes 6291460
  9.0 3.1 %copy-start.7 = (f32[3,3,4096]{2,1,0:T(4,128)S(1)}, f32[3,3,4096]{2,1,0:T(4,128)}, u32[]{:S(2)}) copy-start(f32[3,3,4096]{2,1,0:T(4,128)} %refs_6_.2) | copy-start | bytes 442372
  9.0 3.1 %copy-start.11 = (f32[32,16]{0,1:T(8,128)S(1)}, f32[32,16]{0,1:T(8,128)}, u32[]{:S(2)}) copy-start(f32[32,16]{0,1:T(8,128)} %param.14) | copy-start | bytes 6148
  12.1 6.7 %copy-start.16 = (f32[32,16]{0,1:T(8,128)S(1)}, f32[32,16]{0,1:T(8,128)}, u32[]{:S(2)}) copy-start(f32[32,16]{0,1:T(8,128)} %param.15) | copy-start | bytes 6148
  12.1 6.7 %copy-start.15 = (bf16[32,512]{1,0:T(8,128)(2,1)S(1)}, bf16[32,512]{1,0:T(8,128)(2,1)}, u32[]{:S(2)}) copy-start(bf16[32,512]{1,0:T(8,128)(2,1)} %param.13) | copy-start | bytes 98308
  16.5 0.7 copy-start.3
  16.5 0.8 copy-start.9
  17.3 7.8 %copy-start.4 = (f32[16,4096]{1,0:T(8,128)S(1)}, f32[16,4096]{1,0:T(8,128)}, u32[]{:S(2)}) copy-start(f32[16,4096]{1,0:T(8,128)} %copy-done.3) | copy-start | bytes 786436
  17.3 7.8 %collective-permute-start.1 = (f32[16,2048]{1,0:T(8,128)S(1)}, f32[16,2048]{1,0:T(8,128)S(1)}, u32[]{:S(2)}, u32[]{:S(2)}) collective-permute-start(f32[16,2048]{1,0:T(8,128)S(1)} %slice_select_fusion.2), channel_id=1, source_target_pairs={{0,2},{2,0},{4,6},{6,4},{8,10},{10,8},{12,14},{14,12},{16,18},{18,... | collective-permute-start | bytes 393224 | tf_op jit(solution)/shard_map/ppermute | solution.py:458
  18.8 10.4 %copy-start.10 = (bf16[256,768]{1,0:T(8,128)(2,1)S(1)}, bf16[256,768]{1,0:T(8,128)(2,1)}, u32[]{:S(2)}) copy-start(bf16[256,768]{1,0:T(8,128)(2,1)} %copy-done.9) | copy-start | bytes 1179652
  25.1 15.6 %copy-start.13 = (f32[16,2048]{1,0:T(8,128)}, f32[16,2048]{1,0:T(8,128)S(1)}, u32[]{:S(2)}) copy-start(f32[16,2048]{1,0:T(8,128)S(1)} %collective-permute-done.1) | copy-start | bytes 393220
  25.2 12.0 %collective-permute-start.4 = (f32[16,2048]{1,0:T(8,128)S(1)}, f32[16,2048]{1,0:T(8,128)S(1)}, u32[]{:S(2)}, u32[]{:S(2)}) collective-permute-start(f32[16,2048]{1,0:T(8,128)S(1)} %get-tuple-element.73), channel_id=1, source_target_pairs={{0,4},{2,6},{4,8},{6,10},{8,12},{10,14},{12,16},{14,18},{16,20},{1... | collective-permute-start | bytes 393224 | tf_op jit(solution)/shard_map/ppermute | solution.py:480
  28.6 12.1 %collective-permute-start.2 = (bf16[256,768]{1,0:T(8,128)(2,1)}, bf16[256,768]{1,0:T(8,128)(2,1)S(1)}, u32[]{:S(2)}, u32[]{:S(2)}) collective-permute-start(bf16[256,768]{1,0:T(8,128)(2,1)} %get-tuple-element.40.refs_3_.refs_4_), channel_id=1, source_target_pairs={{0,2},{2,0},{4,6},{6,4},{8,10},{10,8},{12,14},{14,12},{16,18},{18,... | collective-permute-start | bytes 1179656 | tf_op jit(solution)/shard_map/ppermute | solution.py:479
  29.2 11.4 %collective-permute-start.3 = (bf16[256,768]{1,0:T(8,128)(2,1)S(1)}, bf16[256,768]{1,0:T(8,128)(2,1)S(1)}, u32[]{:S(2)}, u32[]{:S(2)}) collective-permute-start(bf16[256,768]{1,0:T(8,128)(2,1)S(1)} %copy-done.10), channel_id=1, source_target_pairs={{0,4},{2,6},{4,8},{6,10},{8,12},{10,14},{12,16},{14,18},{16,20},{1... | collective-permute-start | bytes 1179656 | tf_op jit(solution)/shard_map/ppermute | solution.py:478
  37.2 8.6 %collective-permute-start.6 = (f32[16,2048]{1,0:T(8,128)S(1)}, f32[16,2048]{1,0:T(8,128)S(1)}, u32[]{:S(2)}, u32[]{:S(2)}) collective-permute-start(f32[16,2048]{1,0:T(8,128)S(1)} %multiply_add_fusion.3), channel_id=1, source_target_pairs={{0,8},{2,10},{4,12},{6,14},{8,16},{10,18},{12,20},{14,22},{16,24},... | collective-permute-start | bytes 393224 | tf_op jit(solution)/shard_map/ppermute | solution.py:492
  40.7 14.9 %collective-permute-start.5 = (bf16[256,1280]{1,0:T(8,128)(2,1)S(1)}, bf16[256,1280]{1,0:T(8,128)(2,1)S(1)}, u32[]{:S(2)}, u32[]{:S(2)}) collective-permute-start(bf16[256,1280]{1,0:T(8,128)(2,1)S(1)} %get-tuple-element.54.refs_4_.refs_5_), channel_id=1, source_target_pairs={{0,2},{2,0},{4,6},{6,4},{8,10},{10,8},{12,14},{14,12},{16,18},{18,... | collective-permute-start | bytes 1966088 | tf_op jit(solution)/shard_map/ppermute | solution.py:486
  42.2 15.4 %collective-permute-start.7 = (bf16[256,1280]{1,0:T(8,128)(2,1)S(1)}, bf16[256,1280]{1,0:T(8,128)(2,1)S(1)}, u32[]{:S(2)}, u32[]{:S(2)}) collective-permute-start(bf16[256,1280]{1,0:T(8,128)(2,1)S(1)} %get-tuple-element.56.refs_4_.refs_10_), channel_id=1, source_target_pairs={{0,4},{2,6},{4,8},{6,10},{8,12},{10,14},{12,16},{14,18},{16,20},{1... | collective-permute-start | bytes 1966088 | tf_op jit(solution)/shard_map/ppermute | solution.py:485
  45.8 15.5 %collective-permute-start.9 = (f32[16,2048]{1,0:T(8,128)S(1)}, f32[16,2048]{1,0:T(8,128)S(1)}, u32[]{:S(2)}, u32[]{:S(2)}) collective-permute-start(f32[16,2048]{1,0:T(8,128)S(1)} %multiply_add_fusion.2), channel_id=1, source_target_pairs={{0,16},{2,18},{4,20},{6,22},{8,24},{10,26},{12,28},{14,30},{1,17},... | collective-permute-start | bytes 393224 | tf_op jit(solution)/shard_map/ppermute | solution.py:492
  57.7 3.7 %copy-start.14 = (f32[16,2048]{1,0:T(8,128)S(1)}, f32[16,2048]{1,0:T(8,128)}, u32[]{:S(2)}) copy-start(f32[16,2048]{1,0:T(8,128)} %copy-done.13) | copy-start | bytes 393220
  57.7 11.5 %copy-start.2 = (bf16[256,4096]{1,0:T(8,128)(2,1)S(1)}, bf16[256,4096]{1,0:T(8,128)(2,1)}, u32[]{:S(2)}) copy-start(bf16[256,4096]{1,0:T(8,128)(2,1)} %refs_4_.3) | copy-start | bytes 6291460
  57.7 11.5 %copy-start.8 = (f32[3,3,4096]{2,1,0:T(4,128)S(1)}, f32[3,3,4096]{2,1,0:T(4,128)}, u32[]{:S(2)}) copy-start(f32[3,3,4096]{2,1,0:T(4,128)} %refs_6_.2) | copy-start | bytes 442372
  61.5 6.3 %collective-permute-start.10 = (f32[16,2048]{1,0:T(8,128)S(1)}, f32[16,2048]{1,0:T(8,128)S(1)}, u32[]{:S(2)}, u32[]{:S(2)}) collective-permute-start(f32[16,2048]{1,0:T(8,128)S(1)} %get-tuple-element.62), channel_id=1, source_target_pairs={{0,2},{2,0},{4,6},{6,4},{8,10},{10,8},{12,14},{14,12},{16,18},{18,... | collective-permute-start | bytes 393224 | tf_op jit(solution)/shard_map/ppermute | solution.py:510
  61.6 23.8 %collective-permute-start.8 = (bf16[256,2048]{1,0:T(8,128)(2,1)S(1)}, bf16[256,2048]{1,0:T(8,128)(2,1)S(1)}, u32[]{:S(2)}, u32[]{:S(2)}) collective-permute-start(bf16[256,2048]{1,0:T(8,128)(2,1)S(1)} %get-tuple-element.58), channel_id=1, source_target_pairs={{0,4},{2,6},{4,8},{6,10},{8,12},{10,14},{12,16},{14,18},{16,20},{1... | collective-permute-start | bytes 3145736 | tf_op jit(solution)/shard_map/ppermute | solution.py:514
  67.8 21.2 %collective-permute-start.11 = (bf16[256,2048]{1,0:T(8,128)(2,1)S(1)}, bf16[256,2048]{1,0:T(8,128)(2,1)S(1)}, u32[]{:S(2)}, u32[]{:S(2)}) collective-permute-start(bf16[256,2048]{1,0:T(8,128)(2,1)S(1)} %get-tuple-element.63), channel_id=1, source_target_pairs={{0,2},{2,0},{4,6},{6,4},{8,10},{10,8},{12,14},{14,12},{16,18},{18,... | collective-permute-start | bytes 3145736 | tf_op jit(solution)/shard_map/ppermute | solution.py:513
  69.2 3.4 %copy-start.5 = (bf16[256,4096]{1,0:T(8,128)(2,1)S(1)}, bf16[256,4096]{1,0:T(8,128)(2,1)}, u32[]{:S(2)}) copy-start(bf16[256,4096]{1,0:T(8,128)(2,1)} %refs_6_.3) | copy-start | bytes 6291460
  78.4 17.3 %copy-start.12 = (f32[4096]{0:T(1024)S(1)}, f32[4096]{0:T(1024)}, u32[]{:S(2)}) copy-start(f32[4096]{0:T(1024)} %param.17) | copy-start | bytes 49156

commit v4 on v3

--- a/solution.py
+++ b/solution.py
@@ -313,52 +313,54 @@
     return pltpu.make_async_copy(source_ref.at[:, span], target_ref.at[:, span], sems.at[index])
 
 
-def late_kernel(
+def finisher(start, base_ref, query_ref, out_ref, sum_ref):
+    def finish(g, term):
+        wide = at(g + start)
+        rounded = (base_ref[:, wide] + query_ref[:, wide] * term).astype(BF16)
+        out_ref[:, at(g)] = rounded
+        back = rounded.astype(F32)
+        sum_ref[...] += back * back
+
+    return finish
+
+
+def late_a_kernel(first, odd_ref, ta_ref, got_ref, base_ref, query_ref, out_ref, sum_ref):
+    odd = odd_ref[0]
+    sum_ref[...] = jnp.zeros_like(sum_ref)
+    finish = finisher(0, base_ref, query_ref, out_ref, sum_ref)
+
+    @pl.when(odd == 1)
+    def _():
+        each(first, lambda g: finish(g, dot(lag_two(ta_ref, g), got_ref[:, at(g)])), 2)
+
+    @pl.when(odd == 0)
+    def _():
+        each(first, lambda g: finish(g, got_ref[:, at(g)].astype(F32)), 2)
+
+
+def late_b_kernel(
     first,
     second,
-    odd_ref,
-    ta_ref,
     tb_ref,
-    got_ref,
     near_ref,
     base_ref,
     query_ref,
+    out_a_ref,
+    sum_a_ref,
     target_ref,
     out_ref,
     square_ref,
     sum_ref,
     sems,
 ):
-    odd = odd_ref[0]
-    sum_ref[...] = jnp.zeros_like(sum_ref)
-
-    def finish(wide, term):
-        rounded = (base_ref[:, wide] + query_ref[:, wide] * term).astype(BF16)
-        out_ref[:, wide] = rounded
-        back = rounded.astype(F32)
-        sum_ref[...] += back * back
-
-    def far(g):
-        finish(at(g), dot(lag_two(ta_ref, g), got_ref[:, at(g)]))
-
-    def merged(g):
-        finish(at(g), got_ref[:, at(g)].astype(F32))
-
-    def near(g):
-        finish(at(g + first), dot(lag_one(tb_ref, g), near_ref[:, at(g)]))
-
-    @pl.when(odd == 1)
-    def _():
-        each(first, far, 2)
-
-    @pl.when(odd == 0)
-    def _():
-        each(first, merged, 2)
-
-    copy_a = copy_out(out_ref, target_ref, sems, 0, 0, first)
+    wide_a = first * LANES
+    wide_b = second * LANES
+    copy_a = pltpu.make_async_copy(out_a_ref, target_ref.at[:, pl.ds(0, wide_a)], sems.at[0])
     copy_a.start()
-    each(second, near, 2)
-    copy_b = copy_out(out_ref, target_ref, sems, 1, first, first + second)
+    sum_ref[...] = sum_a_ref[...]
+    finish = finisher(first, base_ref, query_ref, out_ref, sum_ref)
+    each(second, lambda g: finish(g, dot(lag_one(tb_ref, g), near_ref[:, at(g)])), 2)
+    copy_b = pltpu.make_async_copy(out_ref, target_ref.at[:, pl.ds(wide_a, wide_b)], sems.at[1])
     copy_b.start()
     turned = jnp.transpose(sum_ref[...])
     square_ref[...] = jnp.broadcast_to(jnp.sum(turned, axis=0, keepdims=True), square_ref.shape)
@@ -366,14 +368,17 @@
     copy_b.wait()
 
 
-def norm_kernel(count, groups, total_ref, gain_ref, x_ref, target_ref, o_ref, sems):
+def norm_kernel(
+    count, first, second, total_ref, gain_ref, xa_ref, xb_ref, target_ref, o_ref, sems
+):
     scale = jnp.transpose(lax.rsqrt(total_ref[...] * (1.0 / count) + 1e-05))
     wide = jnp.broadcast_to(scale[:, 0:1], (scale.shape[0], LANES))
     copies = []
-    for index, (low, high) in enumerate(chunks_of(groups)):
+    for index, (low, high) in enumerate(chunks_of(first + second)):
         for g in range(low, high):
             lanes = at(g)
-            o_ref[:, lanes] = (x_ref[:, lanes].astype(F32) * wide * gain_ref[:, lanes]).astype(BF16)
+            x = xa_ref[:, at(g)] if g < first else xb_ref[:, at(g - first)]
+            o_ref[:, lanes] = (x.astype(F32) * wide * gain_ref[:, lanes]).astype(BF16)
         copy = copy_out(o_ref, target_ref, sems, index, low, high)
         copy.start()
         copies.append(copy)
@@ -418,8 +423,8 @@
     devices = lax.axis_size("ctx")
     first = groups // 2
     second = groups - first
-    b_parts = ((second * 3) // 8, second - (second * 3) // 8)
-    a_parts = ((first * 3) // 8, first - (first * 3) // 8)
+    b_parts = (second // 4, second - second // 4)
+    a_parts = (first // 4, first - first // 4)
     sizes = (*a_parts, *b_parts)
     wide_a = first * LANES
     wide_b = second * LANES
@@ -472,23 +477,21 @@
     wide_rate = jnp.where(is_odd, wide_rate[:, half:], wide_rate[:, :half])
     decay = lambda blocks: jnp.exp(-wide_rate * (length * blocks))
 
-    ta, part_a = tables(0, a_parts, (xa1, xa2), source)
-    beside = after(beside, part_a)
     pair = decay(1.0) * jnp.where(is_odd, beside, mine) + jnp.where(is_odd, mine, beside)
     far1 = lax.ppermute(xb1, "ctx", shifted_pairs(devices, 2))
     near1 = lax.ppermute(xa1, "ctx", swap_pairs(devices))
     got = lax.ppermute(pair, "ctx", shifted_pairs(devices, 2))
-    tb, part_b = tables(first, b_parts, (xb1, xb2), after(source, pair))
-    before = after(got, part_b)
+    before = got
     pair = pair + decay(2.0) * before
-    far1, near1 = after(far1, part_b), after(near1, part_b)
     far2 = lax.ppermute(after(xb2, far1, near1, pair), "ctx", shifted_pairs(devices, 2))
     near2 = lax.ppermute(after(xa2, far1, near1, pair), "ctx", swap_pairs(devices))
     hop = 4
     while hop < devices:
         last = hop * 2 >= devices
         if last:
-            far2, near2 = after(far2, pair), after(near2, pair)
+            ta, part_a = tables(0, a_parts, (xa1, xa2), after(source, pair))
+            tb, part_b = tables(first, b_parts, (xb1, xb2), after(source, part_a))
+            far2, near2 = after(far2, part_b), after(near2, part_b)
         got = lax.ppermute(pair, "ctx", shifted_pairs(devices, hop))
         if last:
             send_a, send_b, keep_a = call(
@@ -529,26 +532,32 @@
         "state",
         keep_a, acc_b, state, rate_t, weight_t, query, residual,
     )
-    block_out, again, squares = call(
-        lambda *refs: late_kernel(first, second, *refs),
+    out_a, sum_a = call(
+        lambda *refs: late_a_kernel(first, *refs),
+        [shape((length, wide_a), BF16), shape((length, LANES), F32)],
+        "late_a",
+        odd, ta, got_a, base, query,
+        smem=1,
+    )
+    block_out, out_b, squares = call(
+        lambda *refs: late_b_kernel(first, second, *refs),
         [
             shape((length, channels), BF16),
-            shape((length, channels), BF16),
+            shape((length, wide_b), BF16),
             shape((8, length), F32),
         ],
-        "late",
-        odd, ta, tb, got_a, near_b, base, query,
-        smem=1,
+        "late_b",
+        tb, near_b, base, query, out_a, sum_a,
         scratch=[pltpu.VMEM((length, LANES), F32), pltpu.SemaphoreType.DMA((2,))],
         loose=(0,),
     )
     total = lax.psum(squares, "width")
     count = float(channels * lax.axis_size("width"))
     (normed,) = call(
-        lambda *refs: norm_kernel(count, groups, *refs),
+        lambda *refs: norm_kernel(count, first, second, *refs),
         [shape((length, channels), BF16)],
         "norm",
-        total, norm_gain[None, :], again,
+        total, norm_gain[None, :], out_a, out_b,
         scratch=[pltpu.VMEM((length, channels), BF16), pltpu.SemaphoreType.DMA((8,))],
         loose=(0,),
     )

time: 98.4 us -> 97.3 us (0.989)
  waiting for transfers between devices: 17.8 us -> 12.9 us
  other arithmetic: 0.34 us -> 1.93 us
  local copies, waits for them, and re-layouts: 3.18 us -> 4.27 us
    ppermute x1, waiting for transfers between devices: 4.41 us -> 0.01 us  [body(): lax.ppermute(after(xa2, far1, near1, pair), 'ctx', swap_pairs(devices))]
    ppermute x1, waiting for transfers between devices: 0.01 us -> 3.18 us  [body(): lax.ppermute(jnp.where(is_odd, window[:, :half], window[:, half:]), 'ctx'...]
    ppermute x1, waiting for transfers between devices: 2.14 us -> 0.01 us  [body(): lax.ppermute(after(xb2, far1, near1, pair), 'ctx', shifted_pairs(devices,...]
    ppermute x1, waiting for transfers between devices: 6.92 us -> 5.46 us  [body(): got_a = lax.ppermute(send_a, 'ctx', shifted_pairs(devices, 2))]
    unnamed x35 -> x41, local copies, waits for them, and re-layouts: 2.62 us -> 3.72 us
    ppermute x1, waiting for transfers between devices: 3.62 us -> 2.58 us  [body(): near_b = lax.ppermute(after(send_b, other), 'ctx', swap_pairs(devices))]
    ppermute x1, starting transfers between devices: 3.56 us -> 4.59 us  [body(): lax.ppermute(after(xb2, far1, near1, pair), 'ctx', shifted_pairs(devices,...]
    pallas_call x9 -> x10, Pallas kernels: 36.4 us -> 37.1 us  [call(): pl.pallas_call(kernel, in_specs=specs, out_specs=outs, out_shape=out_shap...]
  transfers between devices with their start and end apart: 12 -> 12, of which waited for: 5 -> 5; matrix products, arithmetic and copies ran while one was open for 1% -> 2% of each run, Pallas kernels for 26% -> 28%
where the time goes in v4:
time: 97.3 us; the launch traced here: 96.8 us
  Pallas kernels  38.9 us (40%)
  starting transfers between devices  35.3 us (36%)
  waiting for transfers between devices  12.9 us (13%)
  local copies, waits for them, and re-layouts  4.27 us (4%)
  blocking collectives  2.5 us (3%)
  other arithmetic  1.93 us (2%)
  between operations  1.04 us (1%)
    pallas_call x10, Pallas kernels, call(): pl.pallas_call(kernel, in_specs=specs, out_specs=outs, out_shape=out_shap...  37.1 us
    ppermute x2, starting transfers between devices, body(): got = lax.ppermute(pair, 'ctx', shifted_pairs(devices, hop))  8.92 us
    ppermute x1, waiting for transfers between devices, body(): got_a = lax.ppermute(send_a, 'ctx', shifted_pairs(devices, 2))  5.46 us
    ppermute x1, starting transfers between devices, body(): tail = lax.ppermute(own_tail, 'ctx', shifted_pairs(devices, 1))  4.83 us
    ppermute x1, starting transfers between devices, body(): lax.ppermute(after(xb2, far1, near1, pair), 'ctx', shifted_pairs(devices,...  4.59 us
    ppermute x1, starting transfers between devices, body(): got_a = lax.ppermute(send_a, 'ctx', shifted_pairs(devices, 2))  4.55 us
    unnamed x41, local copies, waits for them, and re-layouts  3.72 us
    ppermute x1, starting transfers between devices, body(): got = lax.ppermute(pair, 'ctx', shifted_pairs(devices, 2))  3.43 us
  transfers between devices with their start and end apart: 12, of which 5 were waited for; matrix products, arithmetic and copies ran while one was open for 2% of the time, Pallas kernels for 28%

profile of v4, /device:TPU:0, one launch (start us, length us, event | category | flops | bytes accessed | tf_op | source)
XLA Modules:
  0.0 96.8 jit_solution(4124323059043244424)
XLA Ops:
  0.6 1.8 %tail.1 = bf16[8,4096]{1,0:T(8,128)(2,1)} custom-call(bf16[256,4096]{1,0:T(8,128)(2,1)} %refs_4_.3, bf16[256,4096]{1,0:T(8,128)(2,1)} %refs_4_.2, bf16[256,4096]{1,0:T(8,128)(2,1)} %refs_5_.1), custom_call_target="tpu_custom_call" | custom-call | tf_op jit(solution)/shard_map/tail/pallas_call | solution.py:436
  2.5 4.8 %collective-permute-start = (bf16[8,4096]{1,0:T(8,128)(2,1)}, bf16[8,4096]{1,0:T(8,128)(2,1)S(1)}, u32[]{:S(2)}, u32[]{:S(2)}) collective-permute-start(bf16[8,4096]{1,0:T(8,128)(2,1)} %tail.1), channel_id=1, source_target_pairs={{0,2},{2,4},{4,6},{6,8},{8,10},{10,12},{12,14},{14,16},{16,18},{18... | collective-permute-start | bytes 196616 | tf_op jit(solution)/shard_map/ppermute | solution.py:444
  7.4 1.6 %copy-done.1 = bf16[256,4096]{1,0:T(8,128)(2,1)S(1)} copy-done((bf16[256,4096]{1,0:T(8,128)(2,1)S(1)}, bf16[256,4096]{1,0:T(8,128)(2,1)}, u32[]{:S(2)}) %copy-start.1) | copy-done | bytes 2097176
  9.0 3.1 %mix.1 = (bf16[256,512]{1,0:T(8,128)(2,1)S(1)}, bf16[256,1536]{1,0:T(8,128)(2,1)S(1)}, bf16[256,512]{1,0:T(8,128)(2,1)S(1)}, bf16[256,1536]{1,0:T(8,128)(2,1)S(1)}) custom-call(bf16[256,4096]{1,0:T(8,128)(2,1)S(1)} %copy-done, bf16[256,4096]{1,0:T(8,128)(2,1)S(1)} %copy-done.1, f32[3,3,4096]{2,1,0:T(4,128)S(1)} %copy-done.4), custom_call_target="tpu_custom_call" | custom-call | bytes 20000 | tf_op jit(solution)/shard_map/mix/pallas_call | solution.py:396
  12.1 4.5 %head.1 = (bf16[256,512]{1,0:T(8,128)(2,1)S(1)}, bf16[256,1536]{1,0:T(8,128)(2,1)S(1)}, bf16[256,512]{1,0:T(8,128)(2,1)S(1)}, bf16[256,1536]{1,0:T(8,128)(2,1)}, f32[16,4096]{1,0:T(8,128)S(1)}) custom-call(bf16[256,512]{1,0:T(8,128)(2,1)S(1)} %get-tuple-element.35.refs_0_, bf16[256,1536]{1,0:T(8,128)(2,1)S(1)} %get-tuple-element.36.refs_1_, ...), custom_call_target="tpu_custom_call" | custom-call | bytes 20000 | tf_op jit(solution)/shard_map/head/pallas_call | solution.py:396
  16.6 1.6 %collective-permute-start.1 = (f32[16,2048]{1,0:T(8,128)S(1)}, f32[16,2048]{1,0:T(8,128)S(1)}, u32[]{:S(2)}, u32[]{:S(2)}) collective-permute-start(f32[16,2048]{1,0:T(8,128)S(1)} %slice_select_fusion.2), channel_id=1, source_target_pairs={{0,2},{2,0},{4,6},{6,4},{8,10},{10,8},{12,14},{14,12},{16,18},{18,... | collective-permute-start | bytes 393224 | tf_op jit(solution)/shard_map/ppermute | solution.py:463
  18.5 3.2 %collective-permute-done.1 = f32[16,2048]{1,0:T(8,128)S(1)} collective-permute-done((f32[16,2048]{1,0:T(8,128)S(1)}, f32[16,2048]{1,0:T(8,128)S(1)}, u32[]{:S(2)}, u32[]{:S(2)}) %collective-permute-start.1) | collective-permute-done | bytes 131104 | tf_op jit(solution)/shard_map/ppermute | solution.py:463
  21.7 3.4 %collective-permute-start.2 = (f32[16,2048]{1,0:T(8,128)S(1)}, f32[16,2048]{1,0:T(8,128)S(1)}, u32[]{:S(2)}, u32[]{:S(2)}) collective-permute-start(f32[16,2048]{1,0:T(8,128)S(1)} %get-tuple-element.71), channel_id=1, source_target_pairs={{0,4},{2,6},{4,8},{6,10},{8,12},{10,14},{12,16},{14,18},{16,20},{1... | collective-permute-start | bytes 393224 | tf_op jit(solution)/shard_map/ppermute | solution.py:483
  25.2 1.6 %collective-permute-start.4 = (bf16[256,512]{1,0:T(8,128)(2,1)S(1)}, bf16[256,512]{1,0:T(8,128)(2,1)S(1)}, u32[]{:S(2)}, u32[]{:S(2)}) collective-permute-start(bf16[256,512]{1,0:T(8,128)(2,1)S(1)} %get-tuple-element.41.refs_3_.refs_4_), channel_id=1, source_target_pairs={{0,2},{2,0},{4,6},{6,4},{8,10},{10,8},{12,14},{14,12},{16,18},{18,... | collective-permute-start | bytes 786440 | tf_op jit(solution)/shard_map/ppermute | solution.py:482
  26.7 3.4 %collective-permute-start.5 = (bf16[256,512]{1,0:T(8,128)(2,1)S(1)}, bf16[256,512]{1,0:T(8,128)(2,1)S(1)}, u32[]{:S(2)}, u32[]{:S(2)}) collective-permute-start(bf16[256,512]{1,0:T(8,128)(2,1)S(1)} %get-tuple-element.45.refs_3_.refs_9_), channel_id=1, source_target_pairs={{0,4},{2,6},{4,8},{6,10},{8,12},{10,14},{12,16},{14,18},{16,20},{1... | collective-permute-start | bytes 786440 | tf_op jit(solution)/shard_map/ppermute | solution.py:481
  30.2 3.5 %collective-permute-start.3 = (f32[16,2048]{1,0:T(8,128)S(1)}, f32[16,2048]{1,0:T(8,128)S(1)}, u32[]{:S(2)}, u32[]{:S(2)}) collective-permute-start(f32[16,2048]{1,0:T(8,128)S(1)} %multiply_add_fusion.3), channel_id=1, source_target_pairs={{0,8},{2,10},{4,12},{6,14},{8,16},{10,18},{12,20},{14,22},{16,24},... | collective-permute-start | bytes 393224 | tf_op jit(solution)/shard_map/ppermute | solution.py:495
  34.0 1.1 %collective-permute-start.6 = (bf16[256,1536]{1,0:T(8,128)(2,1)S(1)}, bf16[256,1536]{1,0:T(8,128)(2,1)}, u32[]{:S(2)}, u32[]{:S(2)}) collective-permute-start(bf16[256,1536]{1,0:T(8,128)(2,1)S(1)} %get-tuple-element.49.refs_4_.refs_5_), channel_id=1, source_target_pairs={{0,2},{2,0},{4,6},{6,4},{8,10},{10,8},{12,14},{14,12},{16,18},{18,... | collective-permute-start | bytes 2359304 | tf_op jit(solution)/shard_map/ppermute | solution.py:487
  35.2 4.6 %collective-permute-start.7 = (bf16[256,1536]{1,0:T(8,128)(2,1)}, bf16[256,1536]{1,0:T(8,128)(2,1)S(1)}, u32[]{:S(2)}, u32[]{:S(2)}) collective-permute-start(bf16[256,1536]{1,0:T(8,128)(2,1)} %get-tuple-element.52.refs_4_.refs_10_), channel_id=1, source_target_pairs={{0,4},{2,6},{4,8},{6,10},{8,12},{10,14},{12,16},{14,18},{16,20},{1... | collective-permute-start | bytes 2359304 | tf_op jit(solution)/shard_map/ppermute | solution.py:486
  39.8 0.7 multiply_add_fusion.2
  40.5 5.4 %collective-permute-start.8 = (f32[16,2048]{1,0:T(8,128)}, f32[16,2048]{1,0:T(8,128)}, u32[]{:S(2)}, u32[]{:S(2)}) collective-permute-start(f32[16,2048]{1,0:T(8,128)} %multiply_add_fusion.2), channel_id=1, source_target_pairs={{0,16},{2,18},{4,20},{6,22},{8,24},{10,26},{12,28},{14,30},{1,17},... | collective-permute-start | bytes 393224 | tf_op jit(solution)/shard_map/ppermute | solution.py:495
  46.5 1.0 copy-done.6
  47.4 4.4 %table.2 = (bf16[16,128,512]{2,1,0:T(8,128)(2,1)S(1)}, f32[256,2048]{1,0:T(8,128)S(1)}) custom-call(f32[32,512]{1,0:T(8,128)S(1)} %pad_maximum_fusion.refs_0_, f32[16,32]{1,0:T(8,128)S(1)} %bitcast.11, f32[16,32]{1,0:T(8,128)S(1)} %multiply_bitcast_fusion.refs_2_.refs_4_, bf16[256,512]{1,0:T(8,128)(2,1)S(1)} %copy-done.6, ...), custom_call_target="tpu_custom_call" | custom-call | bytes 20000 | tf_op jit(solution)/shard_map/table/pallas_call | solution.py:396
  51.9 5.6 %table.3 = (bf16[16,128,512]{2,1,0:T(8,128)(2,1)S(1)}, f32[256,2048]{1,0:T(8,128)S(1)}) custom-call(f32[32,512]{1,0:T(8,128)S(1)} %pad_maximum_fusion.refs_0_, f32[16,32]{1,0:T(8,128)S(1)} %bitcast.12, f32[16,32]{1,0:T(8,128)S(1)} %multiply_bitcast_fusion.refs_2_.refs_4_, bf16[256,512]{1,0:T(8,128)(2,1)S(1)} %copy-done.9, ...), custom_call_target="tpu_custom_call" | custom-call | bytes 20000 | tf_op jit(solution)/shard_map/table/pallas_call | solution.py:396
  57.5 4.0 %merge.1 = (bf16[256,2048]{1,0:T(8,128)(2,1)S(1)}, bf16[256,2048]{1,0:T(8,128)(2,1)S(1)}, f32[256,2048]{1,0:T(8,128)S(1)}) custom-call(s32[1]{0:T(128)} %bitcast.2.refs_0_, bf16[16,128,512]{2,1,0:T(8,128)(2,1)S(1)} %get-tuple-element.48.refs_1_, bf16[256,512]{1,0:T(8,128)(2,1)S(1)} %collective-permute-done.4.refs_2_, ...), custom_call_target="tpu_custom_call" | custom-call | bytes 20000 | tf_op jit(solution)/shard_map/merge/pallas_call | solution.py:396
  61.6 1.0 %broadcast_select_fusion = (f32[16,2048]{1,0:T(8,128)S(1)}, f32[16,2048]{1,0:T(8,128)S(1)}, f32[16,2048]{1,0:T(8,128)S(1)}) fusion(pred[]{:T(512)S(6)} %eq.5, f32[16,2048]{1,0:T(8,128)S(1)} %collective-permute-done.1, f32[16,4096]{1,0:T(8,128)S(1)} %get-tuple-element.39, f32[16,2048]{1,0:T(8,128)S(1)} %get-tuple-element.72, ...), kind=kLoop, calls=%fused_computation.14 | loop fusion | flops 393216 | bytes 1310721 | tf_op jit(solution)/shard_map/jit(_where)/select_n | solution.py:514
  63.2 4.5 %collective-permute-start.11 = (bf16[256,2048]{1,0:T(8,128)(2,1)S(1)}, bf16[256,2048]{1,0:T(8,128)(2,1)S(1)}, u32[]{:S(2)}, u32[]{:S(2)}) collective-permute-start(bf16[256,2048]{1,0:T(8,128)(2,1)S(1)} %get-tuple-element.62), channel_id=1, source_target_pairs={{0,4},{2,6},{4,8},{6,10},{8,12},{10,14},{12,16},{14,18},{16,20},{1... | collective-permute-start | bytes 3145736 | tf_op jit(solution)/shard_map/ppermute | solution.py:517
  67.8 1.3 %collective-permute-done.9 = f32[16,2048]{1,0:T(8,128)S(1)} collective-permute-done((f32[16,2048]{1,0:T(8,128)S(1)}, f32[16,2048]{1,0:T(8,128)S(1)}, u32[]{:S(2)}, u32[]{:S(2)}) %collective-permute-start.9) | collective-permute-done | bytes 131104 | tf_op jit(solution)/shard_map/ppermute | solution.py:513
  69.1 0.7 collective-permute-start.10
  69.8 0.9 copy-done.11
  70.8 3.3 %pre.1 = (f32[256,2048]{1,0:T(8,128)S(1)}, f32[256,4096]{1,0:T(8,128)S(1)}) custom-call(bf16[16,128,512]{2,1,0:T(8,128)(2,1)S(1)} %get-tuple-element.47.refs_0_, bf16[256,512]{1,0:T(8,128)(2,1)S(1)} %copy-done.11, bf16[256,1536]{1,0:T(8,128)(2,1)S(1)} %collective-permute-done.7.refs_8_.refs_2_, f32[256,2048]{1,0:T(8,128)S(1)} %get-tuple-element.59.refs_3_, ...), custom_call_target="tpu_custom_call" | custom-call | bytes 20000 | tf_op jit(solution)/shard_map/pre/pallas_call | solution.py:396
  74.1 5.8 %state.1.refs_3_.refs_2_ = f32[256,4096]{1,0:T(8,128)S(1)} custom-call(f32[256,2048]{1,0:T(8,128)S(1)} %get-tuple-element.55.refs_0_, f32[256,2048]{1,0:T(8,128)S(1)} %get-tuple-element.60.refs_1_, f32[16,4096]{1,0:T(8,128)S(1)} %maximum_select_fusion.refs_2_, f32[16,32]{1,0:T(8,128)S(1)} %bitcast.13, f32[16,32]{1,0:T(8,128)S(1)} %multiply_bitcast_fusion.refs_2_.refs_4_, ...), custom_call_target="tpu_custom_call" | custom-call | bytes 20000 | tf_op jit(solution)/shard_map/state/pallas_call | solution.py:396
  80.0 5.5 %collective-permute-done.11.refs_2_ = bf16[256,2048]{1,0:T(8,128)(2,1)S(1)} collective-permute-done((bf16[256,2048]{1,0:T(8,128)(2,1)S(1)}, bf16[256,2048]{1,0:T(8,128)(2,1)S(1)}, u32[]{:S(2)}, u32[]{:S(2)}) %collective-permute-start.11) | collective-permute-done | bytes 1048608 | tf_op jit(solution)/shard_map/ppermute | solution.py:517
  85.4 1.2 %late_a.1 = (bf16[256,2048]{1,0:T(8,128)(2,1)S(1)}, f32[256,128]{1,0:T(8,128)S(1)}) custom-call(s32[1]{0:T(128)} %bitcast.2.refs_0_, bf16[16,128,512]{2,1,0:T(8,128)(2,1)S(1)} %get-tuple-element.48.refs_1_, bf16[256,2048]{1,0:T(8,128)(2,1)S(1)} %collective-permute-done.11.refs_2_, f32[256,4096]{1,0:T(8,128)S(1)} %state.1.refs_3_.refs_2_, ...), custom_call_target="tpu_custom_call" | custom-call | bytes 20000 | tf_op jit(solution)/shard_map/late_a/pallas_call | solution.py:396
  86.6 2.6 %collective-permute-done.10.refs_1_ = bf16[256,2048]{1,0:T(8,128)(2,1)S(1)} collective-permute-done((bf16[256,2048]{1,0:T(8,128)(2,1)S(1)}, bf16[256,2048]{1,0:T(8,128)(2,1)S(1)}, u32[]{:S(2)}, u32[]{:S(2)}) %collective-permute-start.10) | collective-permute-done | bytes 1048608 | tf_op jit(solution)/shard_map/ppermute | solution.py:516
  89.2 3.1 %late_b.1 = (bf16[256,4096]{1,0:T(8,128)(2,1)}, bf16[256,2048]{1,0:T(8,128)(2,1)S(1)}, f32[8,256]{1,0:T(8,128)S(1)}) custom-call(bf16[16,128,512]{2,1,0:T(8,128)(2,1)S(1)} %get-tuple-element.47.refs_0_, bf16[256,2048]{1,0:T(8,128)(2,1)S(1)} %collective-permute-done.10.refs_1_, f32[256,4096]{1,0:T(8,128)S(1)} %state.1.refs_3_.refs_2_, ...), custom_call_target="tpu_custom_call" | custom-call | bytes 20000 | tf_op jit(solution)/shard_map/late_b/pallas_call | solution.py:396
  92.3 2.5 %psum.7.refs_0_ = f32[8,256]{1,0:T(8,128)S(1)} all-reduce(f32[8,256]{1,0:T(8,128)S(1)} %get-tuple-element.66), channel_id=1, replica_groups=mesh['ctx'=16,'width'=2] {'width'}, use_global_device_ids=true, to_apply=%region_0.1 | all-reduce | flops 2048 | bytes 16384 | tf_op jit(solution)/shard_map/psum | solution.py:554
  94.8 2.0 %norm.1 = bf16[256,4096]{1,0:T(8,128)(2,1)} custom-call(f32[8,256]{1,0:T(8,128)S(1)} %psum.7.refs_0_, f32[1,4096]{1,0:T(1,128)S(1)} %bitcast.14, bf16[256,2048]{1,0:T(8,128)(2,1)S(1)} %get-tuple-element.63.refs_4_.refs_2_, bf16[256,2048]{1,0:T(8,128)(2,1)S(1)} %get-tuple-element.67.refs_3_), custom_call_target="tpu_custom_call" | custom-call | bytes 20000 | tf_op jit(solution)/shard_map/norm/pallas_call | solution.py:396
  (57 shorter events, 1.9 us)
Async XLA Ops:
  0.6 6.7 %copy-start = (bf16[256,4096]{1,0:T(8,128)(2,1)S(1)}, bf16[256,4096]{1,0:T(8,128)(2,1)}, u32[]{:S(2)}) copy-start(bf16[256,4096]{1,0:T(8,128)(2,1)} %refs_4_.2) | copy-start | bytes 6291460
  0.6 6.7 %copy-start.4 = (f32[3,3,4096]{2,1,0:T(4,128)S(1)}, f32[3,3,4096]{2,1,0:T(4,128)}, u32[]{:S(2)}) copy-start(f32[3,3,4096]{2,1,0:T(4,128)} %refs_6_.2) | copy-start | bytes 442372
  2.5 9.6 %collective-permute-start = (bf16[8,4096]{1,0:T(8,128)(2,1)}, bf16[8,4096]{1,0:T(8,128)(2,1)S(1)}, u32[]{:S(2)}, u32[]{:S(2)}) collective-permute-start(bf16[8,4096]{1,0:T(8,128)(2,1)} %tail.1), channel_id=1, source_target_pairs={{0,2},{2,4},{4,6},{6,8},{8,10},{10,12},{12,14},{14,16},{16,18},{18... | collective-permute-start | bytes 196616 | tf_op jit(solution)/shard_map/ppermute | solution.py:444
  7.4 1.6 %copy-start.1 = (bf16[256,4096]{1,0:T(8,128)(2,1)S(1)}, bf16[256,4096]{1,0:T(8,128)(2,1)}, u32[]{:S(2)}) copy-start(bf16[256,4096]{1,0:T(8,128)(2,1)} %refs_5_.1) | copy-start | bytes 6291460
  9.0 3.1 %copy-start.12 = (f32[32,16]{0,1:T(8,128)S(1)}, f32[32,16]{0,1:T(8,128)}, u32[]{:S(2)}) copy-start(f32[32,16]{0,1:T(8,128)} %param.14) | copy-start | bytes 6148
  16.6 17.4 %copy-start.5 = (bf16[256,512]{1,0:T(8,128)(2,1)}, bf16[256,512]{1,0:T(8,128)(2,1)S(1)}, u32[]{:S(2)}) copy-start(bf16[256,512]{1,0:T(8,128)(2,1)S(1)} %get-tuple-element.41.refs_3_.refs_4_) | copy-start | bytes 786436
  16.6 18.6 %copy-start.8 = (bf16[256,512]{1,0:T(8,128)(2,1)}, bf16[256,512]{1,0:T(8,128)(2,1)S(1)}, u32[]{:S(2)}) copy-start(bf16[256,512]{1,0:T(8,128)(2,1)S(1)} %get-tuple-element.45.refs_3_.refs_9_) | copy-start | bytes 786436
  16.6 29.3 %copy-start.19 = (f32[32,16]{0,1:T(8,128)S(1)}, f32[32,16]{0,1:T(8,128)}, u32[]{:S(2)}) copy-start(f32[32,16]{0,1:T(8,128)} %param.15) | copy-start | bytes 6148
  16.6 29.3 %copy-start.18 = (bf16[32,512]{1,0:T(8,128)(2,1)S(1)}, bf16[32,512]{1,0:T(8,128)(2,1)}, u32[]{:S(2)}) copy-start(bf16[32,512]{1,0:T(8,128)(2,1)} %param.13) | copy-start | bytes 98308
  16.6 5.0 %collective-permute-start.1 = (f32[16,2048]{1,0:T(8,128)S(1)}, f32[16,2048]{1,0:T(8,128)S(1)}, u32[]{:S(2)}, u32[]{:S(2)}) collective-permute-start(f32[16,2048]{1,0:T(8,128)S(1)} %slice_select_fusion.2), channel_id=1, source_target_pairs={{0,2},{2,0},{4,6},{6,4},{8,10},{10,8},{12,14},{14,12},{16,18},{18,... | collective-permute-start | bytes 393224 | tf_op jit(solution)/shard_map/ppermute | solution.py:463
  21.7 8.4 %collective-permute-start.2 = (f32[16,2048]{1,0:T(8,128)S(1)}, f32[16,2048]{1,0:T(8,128)S(1)}, u32[]{:S(2)}, u32[]{:S(2)}) collective-permute-start(f32[16,2048]{1,0:T(8,128)S(1)} %get-tuple-element.71), channel_id=1, source_target_pairs={{0,4},{2,6},{4,8},{6,10},{8,12},{10,14},{12,16},{14,18},{16,20},{1... | collective-permute-start | bytes 393224 | tf_op jit(solution)/shard_map/ppermute | solution.py:483
  25.2 8.5 %collective-permute-start.4 = (bf16[256,512]{1,0:T(8,128)(2,1)S(1)}, bf16[256,512]{1,0:T(8,128)(2,1)S(1)}, u32[]{:S(2)}, u32[]{:S(2)}) collective-permute-start(bf16[256,512]{1,0:T(8,128)(2,1)S(1)} %get-tuple-element.41.refs_3_.refs_4_), channel_id=1, source_target_pairs={{0,2},{2,0},{4,6},{6,4},{8,10},{10,8},{12,14},{14,12},{16,18},{18,... | collective-permute-start | bytes 786440 | tf_op jit(solution)/shard_map/ppermute | solution.py:482
  26.7 7.3 %collective-permute-start.5 = (bf16[256,512]{1,0:T(8,128)(2,1)S(1)}, bf16[256,512]{1,0:T(8,128)(2,1)S(1)}, u32[]{:S(2)}, u32[]{:S(2)}) collective-permute-start(bf16[256,512]{1,0:T(8,128)(2,1)S(1)} %get-tuple-element.45.refs_3_.refs_9_), channel_id=1, source_target_pairs={{0,4},{2,6},{4,8},{6,10},{8,12},{10,14},{12,16},{14,18},{16,20},{1... | collective-permute-start | bytes 786440 | tf_op jit(solution)/shard_map/ppermute | solution.py:481
  30.2 10.3 %copy-start.14 = (f32[16,2048]{1,0:T(8,128)}, f32[16,2048]{1,0:T(8,128)S(1)}, u32[]{:S(2)}) copy-start(f32[16,2048]{1,0:T(8,128)S(1)} %collective-permute-done.2) | copy-start | bytes 393220
  30.2 9.5 %collective-permute-start.3 = (f32[16,2048]{1,0:T(8,128)S(1)}, f32[16,2048]{1,0:T(8,128)S(1)}, u32[]{:S(2)}, u32[]{:S(2)}) collective-permute-start(f32[16,2048]{1,0:T(8,128)S(1)} %multiply_add_fusion.3), channel_id=1, source_target_pairs={{0,8},{2,10},{4,12},{6,14},{8,16},{10,18},{12,20},{14,22},{16,24},... | collective-permute-start | bytes 393224 | tf_op jit(solution)/shard_map/ppermute | solution.py:495
  34.0 27.6 %copy-start.10 = (bf16[256,512]{1,0:T(8,128)(2,1)}, bf16[256,512]{1,0:T(8,128)(2,1)S(1)}, u32[]{:S(2)}) copy-start(bf16[256,512]{1,0:T(8,128)(2,1)S(1)} %collective-permute-done.5.refs_7_.refs_1_) | copy-start | bytes 786436
  34.0 23.5 %collective-permute-start.6 = (bf16[256,1536]{1,0:T(8,128)(2,1)S(1)}, bf16[256,1536]{1,0:T(8,128)(2,1)}, u32[]{:S(2)}, u32[]{:S(2)}) collective-permute-start(bf16[256,1536]{1,0:T(8,128)(2,1)S(1)} %get-tuple-element.49.refs_4_.refs_5_), channel_id=1, source_target_pairs={{0,2},{2,0},{4,6},{6,4},{8,10},{10,8},{12,14},{14,12},{16,18},{18,... | collective-permute-start | bytes 2359304 | tf_op jit(solution)/shard_map/ppermute | solution.py:487
  35.1 22.4 %copy-start.7 = (bf16[256,512]{1,0:T(8,128)(2,1)S(1)}, bf16[256,512]{1,0:T(8,128)(2,1)}, u32[]{:S(2)}) copy-start(bf16[256,512]{1,0:T(8,128)(2,1)} %copy-done.5) | copy-start | bytes 786436
  35.2 22.3 %collective-permute-start.7 = (bf16[256,1536]{1,0:T(8,128)(2,1)}, bf16[256,1536]{1,0:T(8,128)(2,1)S(1)}, u32[]{:S(2)}, u32[]{:S(2)}) collective-permute-start(bf16[256,1536]{1,0:T(8,128)(2,1)} %get-tuple-element.52.refs_4_.refs_10_), channel_id=1, source_target_pairs={{0,4},{2,6},{4,8},{6,10},{8,12},{10,14},{12,16},{14,18},{16,20},{1... | collective-permute-start | bytes 2359304 | tf_op jit(solution)/shard_map/ppermute | solution.py:486
  39.7 12.1 %copy-start.9 = (bf16[256,512]{1,0:T(8,128)(2,1)S(1)}, bf16[256,512]{1,0:T(8,128)(2,1)}, u32[]{:S(2)}) copy-start(bf16[256,512]{1,0:T(8,128)(2,1)} %copy-done.8) | copy-start | bytes 786436
  39.8 6.1 %copy-start.16 = (f32[16,2048]{1,0:T(8,128)}, f32[16,2048]{1,0:T(8,128)S(1)}, u32[]{:S(2)}) copy-start(f32[16,2048]{1,0:T(8,128)S(1)} %collective-permute-done.3) | copy-start | bytes 393220
  40.5 21.1 %collective-permute-start.8 = (f32[16,2048]{1,0:T(8,128)}, f32[16,2048]{1,0:T(8,128)}, u32[]{:S(2)}, u32[]{:S(2)}) collective-permute-start(f32[16,2048]{1,0:T(8,128)} %multiply_add_fusion.2), channel_id=1, source_target_pairs={{0,16},{2,18},{4,20},{6,22},{8,24},{10,26},{12,28},{14,30},{1,17},... | collective-permute-start | bytes 393224 | tf_op jit(solution)/shard_map/ppermute | solution.py:495
  46.5 1.0 copy-start.6
  57.5 4.1 %copy-start.15 = (f32[16,2048]{1,0:T(8,128)S(1)}, f32[16,2048]{1,0:T(8,128)}, u32[]{:S(2)}) copy-start(f32[16,2048]{1,0:T(8,128)} %copy-done.14) | copy-start | bytes 393220
  57.5 4.1 %copy-start.17 = (f32[16,2048]{1,0:T(8,128)S(1)}, f32[16,2048]{1,0:T(8,128)}, u32[]{:S(2)}) copy-start(f32[16,2048]{1,0:T(8,128)} %copy-done.16) | copy-start | bytes 393220
  57.5 12.3 %copy-start.2 = (bf16[256,4096]{1,0:T(8,128)(2,1)S(1)}, bf16[256,4096]{1,0:T(8,128)(2,1)}, u32[]{:S(2)}) copy-start(bf16[256,4096]{1,0:T(8,128)(2,1)} %refs_4_.3) | copy-start | bytes 6291460
  62.6 6.4 %collective-permute-start.9 = (f32[16,2048]{1,0:T(8,128)S(1)}, f32[16,2048]{1,0:T(8,128)S(1)}, u32[]{:S(2)}, u32[]{:S(2)}) collective-permute-start(f32[16,2048]{1,0:T(8,128)S(1)} %get-tuple-element.57), channel_id=1, source_target_pairs={{0,2},{2,0},{4,6},{6,4},{8,10},{10,8},{12,14},{14,12},{16,18},{18,... | collective-permute-start | bytes 393224 | tf_op jit(solution)/shard_map/ppermute | solution.py:513
  63.2 22.2 %collective-permute-start.11 = (bf16[256,2048]{1,0:T(8,128)(2,1)S(1)}, bf16[256,2048]{1,0:T(8,128)(2,1)S(1)}, u32[]{:S(2)}, u32[]{:S(2)}) collective-permute-start(bf16[256,2048]{1,0:T(8,128)(2,1)S(1)} %get-tuple-element.62), channel_id=1, source_target_pairs={{0,4},{2,6},{4,8},{6,10},{8,12},{10,14},{12,16},{14,18},{16,20},{1... | collective-permute-start | bytes 3145736 | tf_op jit(solution)/shard_map/ppermute | solution.py:517
  69.1 20.1 %collective-permute-start.10 = (bf16[256,2048]{1,0:T(8,128)(2,1)S(1)}, bf16[256,2048]{1,0:T(8,128)(2,1)S(1)}, u32[]{:S(2)}, u32[]{:S(2)}) collective-permute-start(bf16[256,2048]{1,0:T(8,128)(2,1)S(1)} %get-tuple-element.58), channel_id=1, source_target_pairs={{0,2},{2,0},{4,6},{6,4},{8,10},{10,8},{12,14},{14,12},{16,18},{18,... | collective-permute-start | bytes 3145736 | tf_op jit(solution)/shard_map/ppermute | solution.py:516
  69.8 1.0 copy-start.11
  70.8 3.4 %copy-start.3 = (bf16[256,4096]{1,0:T(8,128)(2,1)S(1)}, bf16[256,4096]{1,0:T(8,128)(2,1)}, u32[]{:S(2)}) copy-start(bf16[256,4096]{1,0:T(8,128)(2,1)} %refs_6_.3) | copy-start | bytes 6291460
  89.2 5.6 %copy-start.13 = (f32[4096]{0:T(1024)S(1)}, f32[4096]{0:T(1024)}, u32[]{:S(2)}) copy-start(f32[4096]{0:T(1024)} %param.17) | copy-start | bytes 49156

commit v5 on v4

--- a/solution.py
+++ b/solution.py
@@ -96,7 +96,7 @@
 
     start = 0
     for size, x_ref in zip(sizes, x_refs):
-        each(size, make(start, x_ref), 2)
+        each(size, make(start, x_ref), 8)
         start += size
 
 
@@ -132,7 +132,7 @@
 
     start = 0
     for size, x_ref in zip(sizes, x_refs):
-        each(size, make(start, x_ref), 2)
+        each(size, make(start, x_ref), 8)
         start += size
 
 
@@ -177,7 +177,7 @@
         both = dot(jnp.concatenate([hi, lo], axis=0), x_ref[:, lanes])
         f_ref[:, at(g + skip)] = both[: 2 * LANES] + both[2 * LANES :]
 
-    each(groups, one, 2)
+    each(groups, one, 4)
 
 
 def lag_one(tb_ref, g):
@@ -227,8 +227,8 @@
 
             return one
 
-        each(a_parts[0], make(0, near1_ref), 2)
-        each(a_parts[1], make(a_parts[0], near2_ref), 2)
+        each(a_parts[0], make(0, near1_ref), 8)
+        each(a_parts[1], make(a_parts[0], near2_ref), 8)
 
     @pl.when(odd == 0)
     def _():
@@ -245,8 +245,8 @@
 
             return one
 
-        each(a_parts[0], make(0, near1_ref, own1_ref), 2)
-        each(a_parts[1], make(a_parts[0], near2_ref, own2_ref), 2)
+        each(a_parts[0], make(0, near1_ref, own1_ref), 8)
+        each(a_parts[1], make(a_parts[0], near2_ref, own2_ref), 8)
 
 
 def pre_kernel(
@@ -258,7 +258,7 @@
         query_ref[:, lanes] = short_filter(q_ref, kern, lanes)
         query_ref[0:16, lanes] = short_filter_top(q_ref, tails_of(tail_ref, 0, lanes), kern, lanes)
 
-    each(start, filtered, 2)
+    each(start, filtered, 8)
 
     def make(skip, far_ref):
         def added(g):
@@ -268,8 +268,8 @@
 
         return added
 
-    each(one, make(0, far1_ref), 2)
-    each(two, make(one, far2_ref), 2)
+    each(one, make(0, far1_ref), 8)
+    each(two, make(one, far2_ref), 8)
 
 
 def state_kernel(
@@ -300,8 +300,8 @@
 
         return one
 
-    each(first, make(0, fa_ref), 2)
-    each(second, make(first, fb_ref), 2)
+    each(first, make(0, fa_ref), 8)
+    each(second, make(first, fb_ref), 8)
 
 
 def chunks_of(groups):
@@ -331,11 +331,11 @@
 
     @pl.when(odd == 1)
     def _():
-        each(first, lambda g: finish(g, dot(lag_two(ta_ref, g), got_ref[:, at(g)])), 2)
+        each(first, lambda g: finish(g, dot(lag_two(ta_ref, g), got_ref[:, at(g)])), 8)
 
     @pl.when(odd == 0)
     def _():
-        each(first, lambda g: finish(g, got_ref[:, at(g)].astype(F32)), 2)
+        each(first, lambda g: finish(g, got_ref[:, at(g)].astype(F32)), 8)
 
 
 def late_b_kernel(
@@ -359,7 +359,7 @@
     copy_a.start()
     sum_ref[...] = sum_a_ref[...]
     finish = finisher(first, base_ref, query_ref, out_ref, sum_ref)
-    each(second, lambda g: finish(g, dot(lag_one(tb_ref, g), near_ref[:, at(g)])), 2)
+    each(second, lambda g: finish(g, dot(lag_one(tb_ref, g), near_ref[:, at(g)])), 8)
     copy_b = pltpu.make_async_copy(out_ref, target_ref.at[:, pl.ds(wide_a, wide_b)], sems.at[1])
     copy_b.start()
     turned = jnp.transpose(sum_ref[...])

time: 97.3 us -> 90.3 us (0.928)
  Pallas kernels: 38.9 us -> 27.4 us
  waiting for transfers between devices: 12.9 us -> 16.7 us
    pallas_call x10, Pallas kernels: 37.1 us -> 25.6 us  [call(): pl.pallas_call(kernel, in_specs=specs, out_specs=outs, out_shape=out_shap...]
    ppermute x1, waiting for transfers between devices: 5.46 us -> 9.39 us  [body(): got_a = lax.ppermute(send_a, 'ctx', shifted_pairs(devices, 2))]
  transfers between devices with their start and end apart: 12 -> 12, of which waited for: 5 -> 5; matrix products, arithmetic and copies ran while one was open for 2% -> 2% of each run, Pallas kernels for 28% -> 22%
where the time goes in v5:
time: 90.3 us; the launch traced here: 89.8 us
  starting transfers between devices  35.7 us (40%)
  Pallas kernels  27.4 us (30%)
  waiting for transfers between devices  16.7 us (18%)
  local copies, waits for them, and re-layouts  4.27 us (5%)
  blocking collectives  2.5 us (3%)
  other arithmetic  1.93 us (2%)
  between operations  1.19 us (1%)
    pallas_call x10, Pallas kernels, call(): pl.pallas_call(kernel, in_specs=specs, out_specs=outs, out_shape=out_shap...  25.6 us
    ppermute x1, waiting for transfers between devices, body(): got_a = lax.ppermute(send_a, 'ctx', shifted_pairs(devices, 2))  9.39 us
    ppermute x2, starting transfers between devices, body(): got = lax.ppermute(pair, 'ctx', shifted_pairs(devices, hop))  8.92 us
    ppermute x1, starting transfers between devices, body(): got_a = lax.ppermute(send_a, 'ctx', shifted_pairs(devices, 2))  4.85 us
    ppermute x1, starting transfers between devices, body(): tail = lax.ppermute(own_tail, 'ctx', shifted_pairs(devices, 1))  4.83 us
    ppermute x1, starting transfers between devices, body(): lax.ppermute(after(xb2, far1, near1, pair), 'ctx', shifted_pairs(devices,...  4.6 us
    unnamed x41, local copies, waits for them, and re-layouts  3.72 us
    ppermute x1, starting transfers between devices, body(): got = lax.ppermute(pair, 'ctx', shifted_pairs(devices, 2))  3.43 us
  transfers between devices with their start and end apart: 12, of which 5 were waited for; matrix products, arithmetic and copies ran while one was open for 2% of the time, Pallas kernels for 22%

profile of v5, /device:TPU:0, one launch (start us, length us, event | category | flops | bytes accessed | tf_op | source)
XLA Modules:
  0.0 89.8 jit_solution(11441940301950009395)
XLA Ops:
  0.6 1.8 %tail.1 = bf16[8,4096]{1,0:T(8,128)(2,1)} custom-call(bf16[256,4096]{1,0:T(8,128)(2,1)} %refs_4_.3, bf16[256,4096]{1,0:T(8,128)(2,1)} %refs_4_.2, bf16[256,4096]{1,0:T(8,128)(2,1)} %refs_5_.1), custom_call_target="tpu_custom_call" | custom-call | tf_op jit(solution)/shard_map/tail/pallas_call | solution.py:436
  2.5 4.8 %collective-permute-start = (bf16[8,4096]{1,0:T(8,128)(2,1)}, bf16[8,4096]{1,0:T(8,128)(2,1)S(1)}, u32[]{:S(2)}, u32[]{:S(2)}) collective-permute-start(bf16[8,4096]{1,0:T(8,128)(2,1)} %tail.1), channel_id=1, source_target_pairs={{0,2},{2,4},{4,6},{6,8},{8,10},{10,12},{12,14},{14,16},{16,18},{18... | collective-permute-start | bytes 196616 | tf_op jit(solution)/shard_map/ppermute | solution.py:444
  7.4 1.6 %copy-done.1 = bf16[256,4096]{1,0:T(8,128)(2,1)S(1)} copy-done((bf16[256,4096]{1,0:T(8,128)(2,1)S(1)}, bf16[256,4096]{1,0:T(8,128)(2,1)}, u32[]{:S(2)}) %copy-start.1) | copy-done | bytes 2097176
  9.0 3.0 %mix.1 = (bf16[256,512]{1,0:T(8,128)(2,1)S(1)}, bf16[256,1536]{1,0:T(8,128)(2,1)S(1)}, bf16[256,512]{1,0:T(8,128)(2,1)S(1)}, bf16[256,1536]{1,0:T(8,128)(2,1)S(1)}) custom-call(bf16[256,4096]{1,0:T(8,128)(2,1)S(1)} %copy-done, bf16[256,4096]{1,0:T(8,128)(2,1)S(1)} %copy-done.1, f32[3,3,4096]{2,1,0:T(4,128)S(1)} %copy-done.4), custom_call_target="tpu_custom_call" | custom-call | bytes 20000 | tf_op jit(solution)/shard_map/mix/pallas_call | solution.py:396
  12.0 1.5 %head.1 = (bf16[256,512]{1,0:T(8,128)(2,1)S(1)}, bf16[256,1536]{1,0:T(8,128)(2,1)S(1)}, bf16[256,512]{1,0:T(8,128)(2,1)S(1)}, bf16[256,1536]{1,0:T(8,128)(2,1)}, f32[16,4096]{1,0:T(8,128)S(1)}) custom-call(bf16[256,512]{1,0:T(8,128)(2,1)S(1)} %get-tuple-element.35.refs_0_, bf16[256,1536]{1,0:T(8,128)(2,1)S(1)} %get-tuple-element.36.refs_1_, ...), custom_call_target="tpu_custom_call" | custom-call | bytes 20000 | tf_op jit(solution)/shard_map/head/pallas_call | solution.py:396
  13.5 1.6 %collective-permute-start.1 = (f32[16,2048]{1,0:T(8,128)S(1)}, f32[16,2048]{1,0:T(8,128)S(1)}, u32[]{:S(2)}, u32[]{:S(2)}) collective-permute-start(f32[16,2048]{1,0:T(8,128)S(1)} %slice_select_fusion.2), channel_id=1, source_target_pairs={{0,2},{2,0},{4,6},{6,4},{8,10},{10,8},{12,14},{14,12},{16,18},{18,... | collective-permute-start | bytes 393224 | tf_op jit(solution)/shard_map/ppermute | solution.py:463
  15.3 3.2 %collective-permute-done.1 = f32[16,2048]{1,0:T(8,128)S(1)} collective-permute-done((f32[16,2048]{1,0:T(8,128)S(1)}, f32[16,2048]{1,0:T(8,128)S(1)}, u32[]{:S(2)}, u32[]{:S(2)}) %collective-permute-start.1) | collective-permute-done | bytes 131104 | tf_op jit(solution)/shard_map/ppermute | solution.py:463
  18.6 3.4 %collective-permute-start.2 = (f32[16,2048]{1,0:T(8,128)S(1)}, f32[16,2048]{1,0:T(8,128)S(1)}, u32[]{:S(2)}, u32[]{:S(2)}) collective-permute-start(f32[16,2048]{1,0:T(8,128)S(1)} %get-tuple-element.71), channel_id=1, source_target_pairs={{0,4},{2,6},{4,8},{6,10},{8,12},{10,14},{12,16},{14,18},{16,20},{1... | collective-permute-start | bytes 393224 | tf_op jit(solution)/shard_map/ppermute | solution.py:483
  22.0 1.6 %collective-permute-start.4 = (bf16[256,512]{1,0:T(8,128)(2,1)S(1)}, bf16[256,512]{1,0:T(8,128)(2,1)S(1)}, u32[]{:S(2)}, u32[]{:S(2)}) collective-permute-start(bf16[256,512]{1,0:T(8,128)(2,1)S(1)} %get-tuple-element.41.refs_3_.refs_4_), channel_id=1, source_target_pairs={{0,2},{2,0},{4,6},{6,4},{8,10},{10,8},{12,14},{14,12},{16,18},{18,... | collective-permute-start | bytes 786440 | tf_op jit(solution)/shard_map/ppermute | solution.py:482
  23.6 3.4 %collective-permute-start.5 = (bf16[256,512]{1,0:T(8,128)(2,1)S(1)}, bf16[256,512]{1,0:T(8,128)(2,1)S(1)}, u32[]{:S(2)}, u32[]{:S(2)}) collective-permute-start(bf16[256,512]{1,0:T(8,128)(2,1)S(1)} %get-tuple-element.45.refs_3_.refs_9_), channel_id=1, source_target_pairs={{0,4},{2,6},{4,8},{6,10},{8,12},{10,14},{12,16},{14,18},{16,20},{1... | collective-permute-start | bytes 786440 | tf_op jit(solution)/shard_map/ppermute | solution.py:481
  27.1 3.5 %collective-permute-start.3 = (f32[16,2048]{1,0:T(8,128)S(1)}, f32[16,2048]{1,0:T(8,128)S(1)}, u32[]{:S(2)}, u32[]{:S(2)}) collective-permute-start(f32[16,2048]{1,0:T(8,128)S(1)} %multiply_add_fusion.3), channel_id=1, source_target_pairs={{0,8},{2,10},{4,12},{6,14},{8,16},{10,18},{12,20},{14,22},{16,24},... | collective-permute-start | bytes 393224 | tf_op jit(solution)/shard_map/ppermute | solution.py:495
  30.9 1.1 %collective-permute-start.6 = (bf16[256,1536]{1,0:T(8,128)(2,1)S(1)}, bf16[256,1536]{1,0:T(8,128)(2,1)}, u32[]{:S(2)}, u32[]{:S(2)}) collective-permute-start(bf16[256,1536]{1,0:T(8,128)(2,1)S(1)} %get-tuple-element.49.refs_4_.refs_5_), channel_id=1, source_target_pairs={{0,2},{2,0},{4,6},{6,4},{8,10},{10,8},{12,14},{14,12},{16,18},{18,... | collective-permute-start | bytes 2359304 | tf_op jit(solution)/shard_map/ppermute | solution.py:487
  32.0 4.6 %collective-permute-start.7 = (bf16[256,1536]{1,0:T(8,128)(2,1)}, bf16[256,1536]{1,0:T(8,128)(2,1)S(1)}, u32[]{:S(2)}, u32[]{:S(2)}) collective-permute-start(bf16[256,1536]{1,0:T(8,128)(2,1)} %get-tuple-element.52.refs_4_.refs_10_), channel_id=1, source_target_pairs={{0,4},{2,6},{4,8},{6,10},{8,12},{10,14},{12,16},{14,18},{16,20},{1... | collective-permute-start | bytes 2359304 | tf_op jit(solution)/shard_map/ppermute | solution.py:486
  36.6 0.7 multiply_add_fusion.2
  37.3 5.4 %collective-permute-start.8 = (f32[16,2048]{1,0:T(8,128)}, f32[16,2048]{1,0:T(8,128)}, u32[]{:S(2)}, u32[]{:S(2)}) collective-permute-start(f32[16,2048]{1,0:T(8,128)} %multiply_add_fusion.2), channel_id=1, source_target_pairs={{0,16},{2,18},{4,20},{6,22},{8,24},{10,26},{12,28},{14,30},{1,17},... | collective-permute-start | bytes 393224 | tf_op jit(solution)/shard_map/ppermute | solution.py:495
  43.3 1.0 %copy-done.6 = bf16[256,512]{1,0:T(8,128)(2,1)S(1)} copy-done((bf16[256,512]{1,0:T(8,128)(2,1)S(1)}, bf16[256,512]{1,0:T(8,128)(2,1)}, u32[]{:S(2)}) %copy-start.6) | copy-done | bytes 262168
  44.3 3.3 %table.2 = (bf16[16,128,512]{2,1,0:T(8,128)(2,1)S(1)}, f32[256,2048]{1,0:T(8,128)S(1)}) custom-call(f32[32,512]{1,0:T(8,128)S(1)} %pad_maximum_fusion.refs_0_, f32[16,32]{1,0:T(8,128)S(1)} %bitcast.11, f32[16,32]{1,0:T(8,128)S(1)} %multiply_bitcast_fusion.refs_2_.refs_4_, bf16[256,512]{1,0:T(8,128)(2,1)S(1)} %copy-done.6, ...), custom_call_target="tpu_custom_call" | custom-call | bytes 20000 | tf_op jit(solution)/shard_map/table/pallas_call | solution.py:396
  47.6 4.4 %table.3 = (bf16[16,128,512]{2,1,0:T(8,128)(2,1)S(1)}, f32[256,2048]{1,0:T(8,128)S(1)}) custom-call(f32[32,512]{1,0:T(8,128)S(1)} %pad_maximum_fusion.refs_0_, f32[16,32]{1,0:T(8,128)S(1)} %bitcast.12, f32[16,32]{1,0:T(8,128)S(1)} %multiply_bitcast_fusion.refs_2_.refs_4_, bf16[256,512]{1,0:T(8,128)(2,1)S(1)} %copy-done.9, ...), custom_call_target="tpu_custom_call" | custom-call | bytes 20000 | tf_op jit(solution)/shard_map/table/pallas_call | solution.py:396
  52.1 3.0 %merge.1 = (bf16[256,2048]{1,0:T(8,128)(2,1)S(1)}, bf16[256,2048]{1,0:T(8,128)(2,1)S(1)}, f32[256,2048]{1,0:T(8,128)S(1)}) custom-call(s32[1]{0:T(128)} %bitcast.2.refs_0_, bf16[16,128,512]{2,1,0:T(8,128)(2,1)S(1)} %get-tuple-element.48.refs_1_, bf16[256,512]{1,0:T(8,128)(2,1)S(1)} %collective-permute-done.4.refs_2_, ...), custom_call_target="tpu_custom_call" | custom-call | bytes 20000 | tf_op jit(solution)/shard_map/merge/pallas_call | solution.py:396
  55.1 1.0 %broadcast_select_fusion = (f32[16,2048]{1,0:T(8,128)S(1)}, f32[16,2048]{1,0:T(8,128)S(1)}, f32[16,2048]{1,0:T(8,128)S(1)}) fusion(pred[]{:T(512)S(6)} %eq.5, f32[16,2048]{1,0:T(8,128)S(1)} %collective-permute-done.1, f32[16,4096]{1,0:T(8,128)S(1)} %get-tuple-element.39, f32[16,2048]{1,0:T(8,128)S(1)} %get-tuple-element.72, ...), kind=kLoop, calls=%fused_computation.14 | loop fusion | flops 393216 | bytes 1310721 | tf_op jit(solution)/shard_map/jit(_where)/select_n | solution.py:514
  56.5 4.8 %collective-permute-start.11 = (bf16[256,2048]{1,0:T(8,128)(2,1)S(1)}, bf16[256,2048]{1,0:T(8,128)(2,1)S(1)}, u32[]{:S(2)}, u32[]{:S(2)}) collective-permute-start(bf16[256,2048]{1,0:T(8,128)(2,1)S(1)} %get-tuple-element.62), channel_id=1, source_target_pairs={{0,4},{2,6},{4,8},{6,10},{8,12},{10,14},{12,16},{14,18},{16,20},{1... | collective-permute-start | bytes 3145736 | tf_op jit(solution)/shard_map/ppermute | solution.py:517
  61.4 1.1 %collective-permute-done.9 = f32[16,2048]{1,0:T(8,128)S(1)} collective-permute-done((f32[16,2048]{1,0:T(8,128)S(1)}, f32[16,2048]{1,0:T(8,128)S(1)}, u32[]{:S(2)}, u32[]{:S(2)}) %collective-permute-start.9) | collective-permute-done | bytes 131104 | tf_op jit(solution)/shard_map/ppermute | solution.py:513
  62.5 1.0 %collective-permute-start.10 = (bf16[256,2048]{1,0:T(8,128)(2,1)S(1)}, bf16[256,2048]{1,0:T(8,128)(2,1)S(1)}, u32[]{:S(2)}, u32[]{:S(2)}) collective-permute-start(bf16[256,2048]{1,0:T(8,128)(2,1)S(1)} %get-tuple-element.58), channel_id=1, source_target_pairs={{0,2},{2,0},{4,6},{6,4},{8,10},{10,8},{12,14},{14,12},{16,18},{18,... | collective-permute-start | bytes 3145736 | tf_op jit(solution)/shard_map/ppermute | solution.py:516
  63.4 0.9 %copy-done.11 = bf16[256,512]{1,0:T(8,128)(2,1)S(1)} copy-done((bf16[256,512]{1,0:T(8,128)(2,1)S(1)}, bf16[256,512]{1,0:T(8,128)(2,1)}, u32[]{:S(2)}) %copy-start.11) | copy-done | bytes 262168
  64.4 2.3 %pre.1 = (f32[256,2048]{1,0:T(8,128)S(1)}, f32[256,4096]{1,0:T(8,128)S(1)}) custom-call(bf16[16,128,512]{2,1,0:T(8,128)(2,1)S(1)} %get-tuple-element.47.refs_0_, bf16[256,512]{1,0:T(8,128)(2,1)S(1)} %copy-done.11, bf16[256,1536]{1,0:T(8,128)(2,1)S(1)} %collective-permute-done.7.refs_8_.refs_2_, f32[256,2048]{1,0:T(8,128)S(1)} %get-tuple-element.59.refs_3_, ...), custom_call_target="tpu_custom_call" | custom-call | bytes 20000 | tf_op jit(solution)/shard_map/pre/pallas_call | solution.py:396
  66.7 2.9 %state.1.refs_3_.refs_2_ = f32[256,4096]{1,0:T(8,128)S(1)} custom-call(f32[256,2048]{1,0:T(8,128)S(1)} %get-tuple-element.55.refs_0_, f32[256,2048]{1,0:T(8,128)S(1)} %get-tuple-element.60.refs_1_, f32[16,4096]{1,0:T(8,128)S(1)} %maximum_select_fusion.refs_2_, f32[16,32]{1,0:T(8,128)S(1)} %bitcast.13, f32[16,32]{1,0:T(8,128)S(1)} %multiply_bitcast_fusion.refs_2_.refs_4_, ...), custom_call_target="tpu_custom_call" | custom-call | bytes 20000 | tf_op jit(solution)/shard_map/state/pallas_call | solution.py:396
  69.6 9.4 %collective-permute-done.11.refs_2_ = bf16[256,2048]{1,0:T(8,128)(2,1)S(1)} collective-permute-done((bf16[256,2048]{1,0:T(8,128)(2,1)S(1)}, bf16[256,2048]{1,0:T(8,128)(2,1)S(1)}, u32[]{:S(2)}, u32[]{:S(2)}) %collective-permute-start.11) | collective-permute-done | bytes 1048608 | tf_op jit(solution)/shard_map/ppermute | solution.py:517
  79.0 1.2 %late_a.1 = (bf16[256,2048]{1,0:T(8,128)(2,1)S(1)}, f32[256,128]{1,0:T(8,128)S(1)}) custom-call(s32[1]{0:T(128)} %bitcast.2.refs_0_, bf16[16,128,512]{2,1,0:T(8,128)(2,1)S(1)} %get-tuple-element.48.refs_1_, bf16[256,2048]{1,0:T(8,128)(2,1)S(1)} %collective-permute-done.11.refs_2_, f32[256,4096]{1,0:T(8,128)S(1)} %state.1.refs_3_.refs_2_, ...), custom_call_target="tpu_custom_call" | custom-call | bytes 20000 | tf_op jit(solution)/shard_map/late_a/pallas_call | solution.py:396
  80.2 2.8 %collective-permute-done.10.refs_1_ = bf16[256,2048]{1,0:T(8,128)(2,1)S(1)} collective-permute-done((bf16[256,2048]{1,0:T(8,128)(2,1)S(1)}, bf16[256,2048]{1,0:T(8,128)(2,1)S(1)}, u32[]{:S(2)}, u32[]{:S(2)}) %collective-permute-start.10) | collective-permute-done | bytes 1048608 | tf_op jit(solution)/shard_map/ppermute | solution.py:516
  82.9 2.2 %late_b.1 = (bf16[256,4096]{1,0:T(8,128)(2,1)}, bf16[256,2048]{1,0:T(8,128)(2,1)S(1)}, f32[8,256]{1,0:T(8,128)S(1)}) custom-call(bf16[16,128,512]{2,1,0:T(8,128)(2,1)S(1)} %get-tuple-element.47.refs_0_, bf16[256,2048]{1,0:T(8,128)(2,1)S(1)} %collective-permute-done.10.refs_1_, f32[256,4096]{1,0:T(8,128)S(1)} %state.1.refs_3_.refs_2_, ...), custom_call_target="tpu_custom_call" | custom-call | bytes 20000 | tf_op jit(solution)/shard_map/late_b/pallas_call | solution.py:396
  85.1 2.5 %psum.7.refs_0_ = f32[8,256]{1,0:T(8,128)S(1)} all-reduce(f32[8,256]{1,0:T(8,128)S(1)} %get-tuple-element.66), channel_id=1, replica_groups=mesh['ctx'=16,'width'=2] {'width'}, use_global_device_ids=true, to_apply=%region_0.1 | all-reduce | flops 2048 | bytes 16384 | tf_op jit(solution)/shard_map/psum | solution.py:554
  87.6 2.0 %norm.1 = bf16[256,4096]{1,0:T(8,128)(2,1)} custom-call(f32[8,256]{1,0:T(8,128)S(1)} %psum.7.refs_0_, f32[1,4096]{1,0:T(1,128)S(1)} %bitcast.14, bf16[256,2048]{1,0:T(8,128)(2,1)S(1)} %get-tuple-element.63.refs_4_.refs_2_, bf16[256,2048]{1,0:T(8,128)(2,1)S(1)} %get-tuple-element.67.refs_3_), custom_call_target="tpu_custom_call" | custom-call | bytes 20000 | tf_op jit(solution)/shard_map/norm/pallas_call | solution.py:396
  (57 shorter events, 1.8 us)
Async XLA Ops:
  0.6 6.7 %copy-start = (bf16[256,4096]{1,0:T(8,128)(2,1)S(1)}, bf16[256,4096]{1,0:T(8,128)(2,1)}, u32[]{:S(2)}) copy-start(bf16[256,4096]{1,0:T(8,128)(2,1)} %refs_4_.2) | copy-start | bytes 6291460
  0.6 6.7 %copy-start.4 = (f32[3,3,4096]{2,1,0:T(4,128)S(1)}, f32[3,3,4096]{2,1,0:T(4,128)}, u32[]{:S(2)}) copy-start(f32[3,3,4096]{2,1,0:T(4,128)} %refs_6_.2) | copy-start | bytes 442372
  2.5 9.4 %collective-permute-start = (bf16[8,4096]{1,0:T(8,128)(2,1)}, bf16[8,4096]{1,0:T(8,128)(2,1)S(1)}, u32[]{:S(2)}, u32[]{:S(2)}) collective-permute-start(bf16[8,4096]{1,0:T(8,128)(2,1)} %tail.1), channel_id=1, source_target_pairs={{0,2},{2,4},{4,6},{6,8},{8,10},{10,12},{12,14},{14,16},{16,18},{18... | collective-permute-start | bytes 196616 | tf_op jit(solution)/shard_map/ppermute | solution.py:444
  7.4 1.6 %copy-start.1 = (bf16[256,4096]{1,0:T(8,128)(2,1)S(1)}, bf16[256,4096]{1,0:T(8,128)(2,1)}, u32[]{:S(2)}) copy-start(bf16[256,4096]{1,0:T(8,128)(2,1)} %refs_5_.1) | copy-start | bytes 6291460
  9.0 3.0 %copy-start.12 = (f32[32,16]{0,1:T(8,128)S(1)}, f32[32,16]{0,1:T(8,128)}, u32[]{:S(2)}) copy-start(f32[32,16]{0,1:T(8,128)} %param.14) | copy-start | bytes 6148
  13.4 17.4 %copy-start.5 = (bf16[256,512]{1,0:T(8,128)(2,1)}, bf16[256,512]{1,0:T(8,128)(2,1)S(1)}, u32[]{:S(2)}) copy-start(bf16[256,512]{1,0:T(8,128)(2,1)S(1)} %get-tuple-element.41.refs_3_.refs_4_) | copy-start | bytes 786436
  13.4 18.6 %copy-start.8 = (bf16[256,512]{1,0:T(8,128)(2,1)}, bf16[256,512]{1,0:T(8,128)(2,1)S(1)}, u32[]{:S(2)}) copy-start(bf16[256,512]{1,0:T(8,128)(2,1)S(1)} %get-tuple-element.45.refs_3_.refs_9_) | copy-start | bytes 786436
  13.4 29.3 %copy-start.19 = (f32[32,16]{0,1:T(8,128)S(1)}, f32[32,16]{0,1:T(8,128)}, u32[]{:S(2)}) copy-start(f32[32,16]{0,1:T(8,128)} %param.15) | copy-start | bytes 6148
  13.4 29.3 %copy-start.18 = (bf16[32,512]{1,0:T(8,128)(2,1)S(1)}, bf16[32,512]{1,0:T(8,128)(2,1)}, u32[]{:S(2)}) copy-start(bf16[32,512]{1,0:T(8,128)(2,1)} %param.13) | copy-start | bytes 98308
  13.5 5.0 %collective-permute-start.1 = (f32[16,2048]{1,0:T(8,128)S(1)}, f32[16,2048]{1,0:T(8,128)S(1)}, u32[]{:S(2)}, u32[]{:S(2)}) collective-permute-start(f32[16,2048]{1,0:T(8,128)S(1)} %slice_select_fusion.2), channel_id=1, source_target_pairs={{0,2},{2,0},{4,6},{6,4},{8,10},{10,8},{12,14},{14,12},{16,18},{18,... | collective-permute-start | bytes 393224 | tf_op jit(solution)/shard_map/ppermute | solution.py:463
  18.6 8.4 %collective-permute-start.2 = (f32[16,2048]{1,0:T(8,128)S(1)}, f32[16,2048]{1,0:T(8,128)S(1)}, u32[]{:S(2)}, u32[]{:S(2)}) collective-permute-start(f32[16,2048]{1,0:T(8,128)S(1)} %get-tuple-element.71), channel_id=1, source_target_pairs={{0,4},{2,6},{4,8},{6,10},{8,12},{10,14},{12,16},{14,18},{16,20},{1... | collective-permute-start | bytes 393224 | tf_op jit(solution)/shard_map/ppermute | solution.py:483
  22.0 8.5 %collective-permute-start.4 = (bf16[256,512]{1,0:T(8,128)(2,1)S(1)}, bf16[256,512]{1,0:T(8,128)(2,1)S(1)}, u32[]{:S(2)}, u32[]{:S(2)}) collective-permute-start(bf16[256,512]{1,0:T(8,128)(2,1)S(1)} %get-tuple-element.41.refs_3_.refs_4_), channel_id=1, source_target_pairs={{0,2},{2,0},{4,6},{6,4},{8,10},{10,8},{12,14},{14,12},{16,18},{18,... | collective-permute-start | bytes 786440 | tf_op jit(solution)/shard_map/ppermute | solution.py:482
  23.6 7.3 %collective-permute-start.5 = (bf16[256,512]{1,0:T(8,128)(2,1)S(1)}, bf16[256,512]{1,0:T(8,128)(2,1)S(1)}, u32[]{:S(2)}, u32[]{:S(2)}) collective-permute-start(bf16[256,512]{1,0:T(8,128)(2,1)S(1)} %get-tuple-element.45.refs_3_.refs_9_), channel_id=1, source_target_pairs={{0,4},{2,6},{4,8},{6,10},{8,12},{10,14},{12,16},{14,18},{16,20},{1... | collective-permute-start | bytes 786440 | tf_op jit(solution)/shard_map/ppermute | solution.py:481
  27.0 10.3 %copy-start.14 = (f32[16,2048]{1,0:T(8,128)}, f32[16,2048]{1,0:T(8,128)S(1)}, u32[]{:S(2)}) copy-start(f32[16,2048]{1,0:T(8,128)S(1)} %collective-permute-done.2) | copy-start | bytes 393220
  27.1 9.5 %collective-permute-start.3 = (f32[16,2048]{1,0:T(8,128)S(1)}, f32[16,2048]{1,0:T(8,128)S(1)}, u32[]{:S(2)}, u32[]{:S(2)}) collective-permute-start(f32[16,2048]{1,0:T(8,128)S(1)} %multiply_add_fusion.3), channel_id=1, source_target_pairs={{0,8},{2,10},{4,12},{6,14},{8,16},{10,18},{12,20},{14,22},{16,24},... | collective-permute-start | bytes 393224 | tf_op jit(solution)/shard_map/ppermute | solution.py:495
  30.9 24.2 %copy-start.10 = (bf16[256,512]{1,0:T(8,128)(2,1)}, bf16[256,512]{1,0:T(8,128)(2,1)S(1)}, u32[]{:S(2)}) copy-start(bf16[256,512]{1,0:T(8,128)(2,1)S(1)} %collective-permute-done.5.refs_7_.refs_1_) | copy-start | bytes 786436
  30.9 21.1 %collective-permute-start.6 = (bf16[256,1536]{1,0:T(8,128)(2,1)S(1)}, bf16[256,1536]{1,0:T(8,128)(2,1)}, u32[]{:S(2)}, u32[]{:S(2)}) collective-permute-start(bf16[256,1536]{1,0:T(8,128)(2,1)S(1)} %get-tuple-element.49.refs_4_.refs_5_), channel_id=1, source_target_pairs={{0,2},{2,0},{4,6},{6,4},{8,10},{10,8},{12,14},{14,12},{16,18},{18,... | collective-permute-start | bytes 2359304 | tf_op jit(solution)/shard_map/ppermute | solution.py:487
  32.0 20.0 %copy-start.7 = (bf16[256,512]{1,0:T(8,128)(2,1)S(1)}, bf16[256,512]{1,0:T(8,128)(2,1)}, u32[]{:S(2)}) copy-start(bf16[256,512]{1,0:T(8,128)(2,1)} %copy-done.5) | copy-start | bytes 786436
  32.0 20.0 %collective-permute-start.7 = (bf16[256,1536]{1,0:T(8,128)(2,1)}, bf16[256,1536]{1,0:T(8,128)(2,1)S(1)}, u32[]{:S(2)}, u32[]{:S(2)}) collective-permute-start(bf16[256,1536]{1,0:T(8,128)(2,1)} %get-tuple-element.52.refs_4_.refs_10_), channel_id=1, source_target_pairs={{0,4},{2,6},{4,8},{6,10},{8,12},{10,14},{12,16},{14,18},{16,20},{1... | collective-permute-start | bytes 2359304 | tf_op jit(solution)/shard_map/ppermute | solution.py:486
  36.6 11.0 %copy-start.9 = (bf16[256,512]{1,0:T(8,128)(2,1)S(1)}, bf16[256,512]{1,0:T(8,128)(2,1)}, u32[]{:S(2)}) copy-start(bf16[256,512]{1,0:T(8,128)(2,1)} %copy-done.8) | copy-start | bytes 786436
  36.6 6.1 %copy-start.16 = (f32[16,2048]{1,0:T(8,128)}, f32[16,2048]{1,0:T(8,128)S(1)}, u32[]{:S(2)}) copy-start(f32[16,2048]{1,0:T(8,128)S(1)} %collective-permute-done.3) | copy-start | bytes 393220
  37.3 17.7 %collective-permute-start.8 = (f32[16,2048]{1,0:T(8,128)}, f32[16,2048]{1,0:T(8,128)}, u32[]{:S(2)}, u32[]{:S(2)}) collective-permute-start(f32[16,2048]{1,0:T(8,128)} %multiply_add_fusion.2), channel_id=1, source_target_pairs={{0,16},{2,18},{4,20},{6,22},{8,24},{10,26},{12,28},{14,30},{1,17},... | collective-permute-start | bytes 393224 | tf_op jit(solution)/shard_map/ppermute | solution.py:495
  43.3 1.0 %copy-start.6 = (bf16[256,512]{1,0:T(8,128)(2,1)S(1)}, bf16[256,512]{1,0:T(8,128)(2,1)}, u32[]{:S(2)}) copy-start(bf16[256,512]{1,0:T(8,128)(2,1)} %copy-done.5) | copy-start | bytes 786436
  52.0 3.0 %copy-start.15 = (f32[16,2048]{1,0:T(8,128)S(1)}, f32[16,2048]{1,0:T(8,128)}, u32[]{:S(2)}) copy-start(f32[16,2048]{1,0:T(8,128)} %copy-done.14) | copy-start | bytes 393220
  52.0 3.0 %copy-start.17 = (f32[16,2048]{1,0:T(8,128)S(1)}, f32[16,2048]{1,0:T(8,128)}, u32[]{:S(2)}) copy-start(f32[16,2048]{1,0:T(8,128)} %copy-done.16) | copy-start | bytes 393220
  52.1 11.4 %copy-start.2 = (bf16[256,4096]{1,0:T(8,128)(2,1)S(1)}, bf16[256,4096]{1,0:T(8,128)(2,1)}, u32[]{:S(2)}) copy-start(bf16[256,4096]{1,0:T(8,128)(2,1)} %refs_4_.3) | copy-start | bytes 6291460
  56.1 6.4 %collective-permute-start.9 = (f32[16,2048]{1,0:T(8,128)S(1)}, f32[16,2048]{1,0:T(8,128)S(1)}, u32[]{:S(2)}, u32[]{:S(2)}) collective-permute-start(f32[16,2048]{1,0:T(8,128)S(1)} %get-tuple-element.57), channel_id=1, source_target_pairs={{0,2},{2,0},{4,6},{6,4},{8,10},{10,8},{12,14},{14,12},{16,18},{18,... | collective-permute-start | bytes 393224 | tf_op jit(solution)/shard_map/ppermute | solution.py:513
  56.5 22.5 %collective-permute-start.11 = (bf16[256,2048]{1,0:T(8,128)(2,1)S(1)}, bf16[256,2048]{1,0:T(8,128)(2,1)S(1)}, u32[]{:S(2)}, u32[]{:S(2)}) collective-permute-start(bf16[256,2048]{1,0:T(8,128)(2,1)S(1)} %get-tuple-element.62), channel_id=1, source_target_pairs={{0,4},{2,6},{4,8},{6,10},{8,12},{10,14},{12,16},{14,18},{16,20},{1... | collective-permute-start | bytes 3145736 | tf_op jit(solution)/shard_map/ppermute | solution.py:517
  62.5 20.5 %collective-permute-start.10 = (bf16[256,2048]{1,0:T(8,128)(2,1)S(1)}, bf16[256,2048]{1,0:T(8,128)(2,1)S(1)}, u32[]{:S(2)}, u32[]{:S(2)}) collective-permute-start(bf16[256,2048]{1,0:T(8,128)(2,1)S(1)} %get-tuple-element.58), channel_id=1, source_target_pairs={{0,2},{2,0},{4,6},{6,4},{8,10},{10,8},{12,14},{14,12},{16,18},{18,... | collective-permute-start | bytes 3145736 | tf_op jit(solution)/shard_map/ppermute | solution.py:516
  63.4 1.0 %copy-start.11 = (bf16[256,512]{1,0:T(8,128)(2,1)S(1)}, bf16[256,512]{1,0:T(8,128)(2,1)}, u32[]{:S(2)}) copy-start(bf16[256,512]{1,0:T(8,128)(2,1)} %copy-done.10) | copy-start | bytes 786436
  64.4 2.3 %copy-start.3 = (bf16[256,4096]{1,0:T(8,128)(2,1)S(1)}, bf16[256,4096]{1,0:T(8,128)(2,1)}, u32[]{:S(2)}) copy-start(bf16[256,4096]{1,0:T(8,128)(2,1)} %refs_6_.3) | copy-start | bytes 6291460
  82.9 4.7 %copy-start.13 = (f32[4096]{0:T(1024)S(1)}, f32[4096]{0:T(1024)}, u32[]{:S(2)}) copy-start(f32[4096]{0:T(1024)} %param.17) | copy-start | bytes 49156

commit v6 on v5

--- a/solution.py
+++ b/solution.py
@@ -483,8 +483,8 @@
     got = lax.ppermute(pair, "ctx", shifted_pairs(devices, 2))
     before = got
     pair = pair + decay(2.0) * before
-    far2 = lax.ppermute(after(xb2, far1, near1, pair), "ctx", shifted_pairs(devices, 2))
-    near2 = lax.ppermute(after(xa2, far1, near1, pair), "ctx", swap_pairs(devices))
+    far2 = lax.ppermute(after(xb2, far1, pair), "ctx", shifted_pairs(devices, 2))
+    near2 = lax.ppermute(after(xa2, near1, pair), "ctx", swap_pairs(devices))
     hop = 4
     while hop < devices:
         last = hop * 2 >= devices

time: 90.3 us -> 90.2 us (level)
  no operation moved by 1% of the time
where the time goes in v6:
time: 90.2 us; the launch traced here: 89.7 us
  starting transfers between devices  35.6 us (39%)
  Pallas kernels  27.4 us (30%)
  waiting for transfers between devices  16.7 us (19%)
  local copies, waits for them, and re-layouts  4.27 us (5%)
  blocking collectives  2.5 us (3%)
  other arithmetic  1.93 us (2%)
  between operations  1.19 us (1%)
    pallas_call x10, Pallas kernels, call(): pl.pallas_call(kernel, in_specs=specs, out_specs=outs, out_shape=out_shap...  25.6 us
    ppermute x1, waiting for transfers between devices, body(): got_a = lax.ppermute(send_a, 'ctx', shifted_pairs(devices, 2))  9.39 us
    ppermute x2, starting transfers between devices, body(): got = lax.ppermute(pair, 'ctx', shifted_pairs(devices, hop))  8.92 us
    ppermute x1, starting transfers between devices, body(): lax.ppermute(after(xb2, far1, pair), 'ctx', shifted_pairs(devices, 2))  4.87 us
    ppermute x1, starting transfers between devices, body(): got_a = lax.ppermute(send_a, 'ctx', shifted_pairs(devices, 2))  4.84 us
    ppermute x1, starting transfers between devices, body(): tail = lax.ppermute(own_tail, 'ctx', shifted_pairs(devices, 1))  4.83 us
    unnamed x41, local copies, waits for them, and re-layouts  3.72 us
    ppermute x1, starting transfers between devices, body(): got = lax.ppermute(pair, 'ctx', shifted_pairs(devices, 2))  3.43 us
  transfers between devices with their start and end apart: 12, of which 5 were waited for; matrix products, arithmetic and copies ran while one was open for 2% of the time, Pallas kernels for 22%

profile of v6, /device:TPU:0, one launch (start us, length us, event | category | flops | bytes accessed | tf_op | source)
XLA Modules:
  0.0 89.7 jit_solution(14752244995219811388)
XLA Ops:
  0.6 1.8 %tail.1 = bf16[8,4096]{1,0:T(8,128)(2,1)} custom-call(bf16[256,4096]{1,0:T(8,128)(2,1)} %refs_4_.3, bf16[256,4096]{1,0:T(8,128)(2,1)} %refs_4_.2, bf16[256,4096]{1,0:T(8,128)(2,1)} %refs_5_.1), custom_call_target="tpu_custom_call" | custom-call | tf_op jit(solution)/shard_map/tail/pallas_call | solution.py:436
  2.5 4.8 %collective-permute-start = (bf16[8,4096]{1,0:T(8,128)(2,1)}, bf16[8,4096]{1,0:T(8,128)(2,1)S(1)}, u32[]{:S(2)}, u32[]{:S(2)}) collective-permute-start(bf16[8,4096]{1,0:T(8,128)(2,1)} %tail.1), channel_id=1, source_target_pairs={{0,2},{2,4},{4,6},{6,8},{8,10},{10,12},{12,14},{14,16},{16,18},{18... | collective-permute-start | bytes 196616 | tf_op jit(solution)/shard_map/ppermute | solution.py:444
  7.4 1.6 %copy-done.1 = bf16[256,4096]{1,0:T(8,128)(2,1)S(1)} copy-done((bf16[256,4096]{1,0:T(8,128)(2,1)S(1)}, bf16[256,4096]{1,0:T(8,128)(2,1)}, u32[]{:S(2)}) %copy-start.1) | copy-done | bytes 2097176
  9.0 3.0 %mix.1 = (bf16[256,512]{1,0:T(8,128)(2,1)S(1)}, bf16[256,1536]{1,0:T(8,128)(2,1)S(1)}, bf16[256,512]{1,0:T(8,128)(2,1)S(1)}, bf16[256,1536]{1,0:T(8,128)(2,1)S(1)}) custom-call(bf16[256,4096]{1,0:T(8,128)(2,1)S(1)} %copy-done, bf16[256,4096]{1,0:T(8,128)(2,1)S(1)} %copy-done.1, f32[3,3,4096]{2,1,0:T(4,128)S(1)} %copy-done.4), custom_call_target="tpu_custom_call" | custom-call | bytes 20000 | tf_op jit(solution)/shard_map/mix/pallas_call | solution.py:396
  12.0 1.5 %head.1 = (bf16[256,512]{1,0:T(8,128)(2,1)S(1)}, bf16[256,1536]{1,0:T(8,128)(2,1)S(1)}, bf16[256,512]{1,0:T(8,128)(2,1)S(1)}, bf16[256,1536]{1,0:T(8,128)(2,1)}, f32[16,4096]{1,0:T(8,128)S(1)}) custom-call(bf16[256,512]{1,0:T(8,128)(2,1)S(1)} %get-tuple-element.35.refs_0_, bf16[256,1536]{1,0:T(8,128)(2,1)S(1)} %get-tuple-element.36.refs_1_, ...), custom_call_target="tpu_custom_call" | custom-call | bytes 20000 | tf_op jit(solution)/shard_map/head/pallas_call | solution.py:396
  13.5 1.6 %collective-permute-start.1 = (f32[16,2048]{1,0:T(8,128)S(1)}, f32[16,2048]{1,0:T(8,128)S(1)}, u32[]{:S(2)}, u32[]{:S(2)}) collective-permute-start(f32[16,2048]{1,0:T(8,128)S(1)} %slice_select_fusion.2), channel_id=1, source_target_pairs={{0,2},{2,0},{4,6},{6,4},{8,10},{10,8},{12,14},{14,12},{16,18},{18,... | collective-permute-start | bytes 393224 | tf_op jit(solution)/shard_map/ppermute | solution.py:463
  15.3 3.2 %collective-permute-done.1 = f32[16,2048]{1,0:T(8,128)S(1)} collective-permute-done((f32[16,2048]{1,0:T(8,128)S(1)}, f32[16,2048]{1,0:T(8,128)S(1)}, u32[]{:S(2)}, u32[]{:S(2)}) %collective-permute-start.1) | collective-permute-done | bytes 131104 | tf_op jit(solution)/shard_map/ppermute | solution.py:463
  18.6 3.4 %collective-permute-start.2 = (f32[16,2048]{1,0:T(8,128)S(1)}, f32[16,2048]{1,0:T(8,128)S(1)}, u32[]{:S(2)}, u32[]{:S(2)}) collective-permute-start(f32[16,2048]{1,0:T(8,128)S(1)} %get-tuple-element.71), channel_id=1, source_target_pairs={{0,4},{2,6},{4,8},{6,10},{8,12},{10,14},{12,16},{14,18},{16,20},{1... | collective-permute-start | bytes 393224 | tf_op jit(solution)/shard_map/ppermute | solution.py:483
  22.0 1.6 %collective-permute-start.4 = (bf16[256,512]{1,0:T(8,128)(2,1)S(1)}, bf16[256,512]{1,0:T(8,128)(2,1)S(1)}, u32[]{:S(2)}, u32[]{:S(2)}) collective-permute-start(bf16[256,512]{1,0:T(8,128)(2,1)S(1)} %get-tuple-element.41.refs_3_.refs_4_), channel_id=1, source_target_pairs={{0,2},{2,0},{4,6},{6,4},{8,10},{10,8},{12,14},{14,12},{16,18},{18,... | collective-permute-start | bytes 786440 | tf_op jit(solution)/shard_map/ppermute | solution.py:482
  23.6 3.4 %collective-permute-start.6 = (bf16[256,512]{1,0:T(8,128)(2,1)S(1)}, bf16[256,512]{1,0:T(8,128)(2,1)S(1)}, u32[]{:S(2)}, u32[]{:S(2)}) collective-permute-start(bf16[256,512]{1,0:T(8,128)(2,1)S(1)} %get-tuple-element.45.refs_3_.refs_9_), channel_id=1, source_target_pairs={{0,4},{2,6},{4,8},{6,10},{8,12},{10,14},{12,16},{14,18},{16,20},{1... | collective-permute-start | bytes 786440 | tf_op jit(solution)/shard_map/ppermute | solution.py:481
  27.1 3.5 %collective-permute-start.3 = (f32[16,2048]{1,0:T(8,128)S(1)}, f32[16,2048]{1,0:T(8,128)S(1)}, u32[]{:S(2)}, u32[]{:S(2)}) collective-permute-start(f32[16,2048]{1,0:T(8,128)S(1)} %multiply_add_fusion.3), channel_id=1, source_target_pairs={{0,8},{2,10},{4,12},{6,14},{8,16},{10,18},{12,20},{14,22},{16,24},... | collective-permute-start | bytes 393224 | tf_op jit(solution)/shard_map/ppermute | solution.py:495
  30.9 4.9 %collective-permute-start.7 = (bf16[256,1536]{1,0:T(8,128)(2,1)}, bf16[256,1536]{1,0:T(8,128)(2,1)S(1)}, u32[]{:S(2)}, u32[]{:S(2)}) collective-permute-start(bf16[256,1536]{1,0:T(8,128)(2,1)} %get-tuple-element.52.refs_4_.refs_10_), channel_id=1, source_target_pairs={{0,4},{2,6},{4,8},{6,10},{8,12},{10,14},{12,16},{14,18},{16,20},{1... | collective-permute-start | bytes 2359304 | tf_op jit(solution)/shard_map/ppermute | solution.py:486
  35.8 0.8 collective-permute-start.5
  36.6 0.7 multiply_add_fusion.2
  37.2 5.4 %collective-permute-start.8 = (f32[16,2048]{1,0:T(8,128)}, f32[16,2048]{1,0:T(8,128)}, u32[]{:S(2)}, u32[]{:S(2)}) collective-permute-start(f32[16,2048]{1,0:T(8,128)} %multiply_add_fusion.2), channel_id=1, source_target_pairs={{0,16},{2,18},{4,20},{6,22},{8,24},{10,26},{12,28},{14,30},{1,17},... | collective-permute-start | bytes 393224 | tf_op jit(solution)/shard_map/ppermute | solution.py:495
  43.3 1.0 %copy-done.6 = bf16[256,512]{1,0:T(8,128)(2,1)S(1)} copy-done((bf16[256,512]{1,0:T(8,128)(2,1)S(1)}, bf16[256,512]{1,0:T(8,128)(2,1)}, u32[]{:S(2)}) %copy-start.6) | copy-done | bytes 262168
  44.2 3.3 %table.2 = (bf16[16,128,512]{2,1,0:T(8,128)(2,1)S(1)}, f32[256,2048]{1,0:T(8,128)S(1)}) custom-call(f32[32,512]{1,0:T(8,128)S(1)} %pad_maximum_fusion.refs_0_, f32[16,32]{1,0:T(8,128)S(1)} %bitcast.11, f32[16,32]{1,0:T(8,128)S(1)} %multiply_bitcast_fusion.refs_2_.refs_4_, bf16[256,512]{1,0:T(8,128)(2,1)S(1)} %copy-done.6, ...), custom_call_target="tpu_custom_call" | custom-call | bytes 20000 | tf_op jit(solution)/shard_map/table/pallas_call | solution.py:396
  47.5 4.4 %table.3 = (bf16[16,128,512]{2,1,0:T(8,128)(2,1)S(1)}, f32[256,2048]{1,0:T(8,128)S(1)}) custom-call(f32[32,512]{1,0:T(8,128)S(1)} %pad_maximum_fusion.refs_0_, f32[16,32]{1,0:T(8,128)S(1)} %bitcast.12, f32[16,32]{1,0:T(8,128)S(1)} %multiply_bitcast_fusion.refs_2_.refs_4_, bf16[256,512]{1,0:T(8,128)(2,1)S(1)} %copy-done.9, ...), custom_call_target="tpu_custom_call" | custom-call | bytes 20000 | tf_op jit(solution)/shard_map/table/pallas_call | solution.py:396
  52.0 3.0 %merge.1 = (bf16[256,2048]{1,0:T(8,128)(2,1)S(1)}, bf16[256,2048]{1,0:T(8,128)(2,1)S(1)}, f32[256,2048]{1,0:T(8,128)S(1)}) custom-call(s32[1]{0:T(128)} %bitcast.2.refs_0_, bf16[16,128,512]{2,1,0:T(8,128)(2,1)S(1)} %get-tuple-element.48.refs_1_, bf16[256,512]{1,0:T(8,128)(2,1)S(1)} %collective-permute-done.4.refs_2_, ...), custom_call_target="tpu_custom_call" | custom-call | bytes 20000 | tf_op jit(solution)/shard_map/merge/pallas_call | solution.py:396
  55.0 1.0 %broadcast_select_fusion = (f32[16,2048]{1,0:T(8,128)S(1)}, f32[16,2048]{1,0:T(8,128)S(1)}, f32[16,2048]{1,0:T(8,128)S(1)}) fusion(pred[]{:T(512)S(6)} %eq.5, f32[16,2048]{1,0:T(8,128)S(1)} %collective-permute-done.1, f32[16,4096]{1,0:T(8,128)S(1)} %get-tuple-element.39, f32[16,2048]{1,0:T(8,128)S(1)} %get-tuple-element.72, ...), kind=kLoop, calls=%fused_computation.14 | loop fusion | flops 393216 | bytes 1310721 | tf_op jit(solution)/shard_map/jit(_where)/select_n | solution.py:514
  56.4 4.8 %collective-permute-start.11 = (bf16[256,2048]{1,0:T(8,128)(2,1)S(1)}, bf16[256,2048]{1,0:T(8,128)(2,1)S(1)}, u32[]{:S(2)}, u32[]{:S(2)}) collective-permute-start(bf16[256,2048]{1,0:T(8,128)(2,1)S(1)} %get-tuple-element.62), channel_id=1, source_target_pairs={{0,4},{2,6},{4,8},{6,10},{8,12},{10,14},{12,16},{14,18},{16,20},{1... | collective-permute-start | bytes 3145736 | tf_op jit(solution)/shard_map/ppermute | solution.py:517
  61.3 1.1 %collective-permute-done.9 = f32[16,2048]{1,0:T(8,128)S(1)} collective-permute-done((f32[16,2048]{1,0:T(8,128)S(1)}, f32[16,2048]{1,0:T(8,128)S(1)}, u32[]{:S(2)}, u32[]{:S(2)}) %collective-permute-start.9) | collective-permute-done | bytes 131104 | tf_op jit(solution)/shard_map/ppermute | solution.py:513
  62.4 1.0 %collective-permute-start.10 = (bf16[256,2048]{1,0:T(8,128)(2,1)S(1)}, bf16[256,2048]{1,0:T(8,128)(2,1)S(1)}, u32[]{:S(2)}, u32[]{:S(2)}) collective-permute-start(bf16[256,2048]{1,0:T(8,128)(2,1)S(1)} %get-tuple-element.58), channel_id=1, source_target_pairs={{0,2},{2,0},{4,6},{6,4},{8,10},{10,8},{12,14},{14,12},{16,18},{18,... | collective-permute-start | bytes 3145736 | tf_op jit(solution)/shard_map/ppermute | solution.py:516
  63.3 0.9 %copy-done.11 = bf16[256,512]{1,0:T(8,128)(2,1)S(1)} copy-done((bf16[256,512]{1,0:T(8,128)(2,1)S(1)}, bf16[256,512]{1,0:T(8,128)(2,1)}, u32[]{:S(2)}) %copy-start.11) | copy-done | bytes 262168
  64.3 2.3 %pre.1 = (f32[256,2048]{1,0:T(8,128)S(1)}, f32[256,4096]{1,0:T(8,128)S(1)}) custom-call(bf16[16,128,512]{2,1,0:T(8,128)(2,1)S(1)} %get-tuple-element.47.refs_0_, bf16[256,512]{1,0:T(8,128)(2,1)S(1)} %copy-done.11, bf16[256,1536]{1,0:T(8,128)(2,1)S(1)} %collective-permute-done.7.refs_8_.refs_2_, f32[256,2048]{1,0:T(8,128)S(1)} %get-tuple-element.59.refs_3_, ...), custom_call_target="tpu_custom_call" | custom-call | bytes 20000 | tf_op jit(solution)/shard_map/pre/pallas_call | solution.py:396
  66.7 2.9 %state.1.refs_3_.refs_2_ = f32[256,4096]{1,0:T(8,128)S(1)} custom-call(f32[256,2048]{1,0:T(8,128)S(1)} %get-tuple-element.55.refs_0_, f32[256,2048]{1,0:T(8,128)S(1)} %get-tuple-element.60.refs_1_, f32[16,4096]{1,0:T(8,128)S(1)} %maximum_select_fusion.refs_2_, f32[16,32]{1,0:T(8,128)S(1)} %bitcast.13, f32[16,32]{1,0:T(8,128)S(1)} %multiply_bitcast_fusion.refs_2_.refs_4_, ...), custom_call_target="tpu_custom_call" | custom-call | bytes 20000 | tf_op jit(solution)/shard_map/state/pallas_call | solution.py:396
  69.5 9.4 %collective-permute-done.11.refs_2_ = bf16[256,2048]{1,0:T(8,128)(2,1)S(1)} collective-permute-done((bf16[256,2048]{1,0:T(8,128)(2,1)S(1)}, bf16[256,2048]{1,0:T(8,128)(2,1)S(1)}, u32[]{:S(2)}, u32[]{:S(2)}) %collective-permute-start.11) | collective-permute-done | bytes 1048608 | tf_op jit(solution)/shard_map/ppermute | solution.py:517
  78.9 1.2 %late_a.1 = (bf16[256,2048]{1,0:T(8,128)(2,1)S(1)}, f32[256,128]{1,0:T(8,128)S(1)}) custom-call(s32[1]{0:T(128)} %bitcast.2.refs_0_, bf16[16,128,512]{2,1,0:T(8,128)(2,1)S(1)} %get-tuple-element.48.refs_1_, bf16[256,2048]{1,0:T(8,128)(2,1)S(1)} %collective-permute-done.11.refs_2_, f32[256,4096]{1,0:T(8,128)S(1)} %state.1.refs_3_.refs_2_, ...), custom_call_target="tpu_custom_call" | custom-call | bytes 20000 | tf_op jit(solution)/shard_map/late_a/pallas_call | solution.py:396
  80.1 2.8 %collective-permute-done.10.refs_1_ = bf16[256,2048]{1,0:T(8,128)(2,1)S(1)} collective-permute-done((bf16[256,2048]{1,0:T(8,128)(2,1)S(1)}, bf16[256,2048]{1,0:T(8,128)(2,1)S(1)}, u32[]{:S(2)}, u32[]{:S(2)}) %collective-permute-start.10) | collective-permute-done | bytes 1048608 | tf_op jit(solution)/shard_map/ppermute | solution.py:516
  82.9 2.2 %late_b.1 = (bf16[256,4096]{1,0:T(8,128)(2,1)}, bf16[256,2048]{1,0:T(8,128)(2,1)S(1)}, f32[8,256]{1,0:T(8,128)S(1)}) custom-call(bf16[16,128,512]{2,1,0:T(8,128)(2,1)S(1)} %get-tuple-element.47.refs_0_, bf16[256,2048]{1,0:T(8,128)(2,1)S(1)} %collective-permute-done.10.refs_1_, f32[256,4096]{1,0:T(8,128)S(1)} %state.1.refs_3_.refs_2_, ...), custom_call_target="tpu_custom_call" | custom-call | bytes 20000 | tf_op jit(solution)/shard_map/late_b/pallas_call | solution.py:396
  85.0 2.5 %psum.7.refs_0_ = f32[8,256]{1,0:T(8,128)S(1)} all-reduce(f32[8,256]{1,0:T(8,128)S(1)} %get-tuple-element.66), channel_id=1, replica_groups=mesh['ctx'=16,'width'=2] {'width'}, use_global_device_ids=true, to_apply=%region_0.1 | all-reduce | flops 2048 | bytes 16384 | tf_op jit(solution)/shard_map/psum | solution.py:554
  87.6 2.0 %norm.1 = bf16[256,4096]{1,0:T(8,128)(2,1)} custom-call(f32[8,256]{1,0:T(8,128)S(1)} %psum.7.refs_0_, f32[1,4096]{1,0:T(1,128)S(1)} %bitcast.14, bf16[256,2048]{1,0:T(8,128)(2,1)S(1)} %get-tuple-element.63.refs_4_.refs_2_, bf16[256,2048]{1,0:T(8,128)(2,1)S(1)} %get-tuple-element.67.refs_3_), custom_call_target="tpu_custom_call" | custom-call | bytes 20000 | tf_op jit(solution)/shard_map/norm/pallas_call | solution.py:396
  (57 shorter events, 1.8 us)
Async XLA Ops:
  0.6 6.7 %copy-start = (bf16[256,4096]{1,0:T(8,128)(2,1)S(1)}, bf16[256,4096]{1,0:T(8,128)(2,1)}, u32[]{:S(2)}) copy-start(bf16[256,4096]{1,0:T(8,128)(2,1)} %refs_4_.2) | copy-start | bytes 6291460
  0.6 6.7 %copy-start.4 = (f32[3,3,4096]{2,1,0:T(4,128)S(1)}, f32[3,3,4096]{2,1,0:T(4,128)}, u32[]{:S(2)}) copy-start(f32[3,3,4096]{2,1,0:T(4,128)} %refs_6_.2) | copy-start | bytes 442372
  2.5 9.4 %collective-permute-start = (bf16[8,4096]{1,0:T(8,128)(2,1)}, bf16[8,4096]{1,0:T(8,128)(2,1)S(1)}, u32[]{:S(2)}, u32[]{:S(2)}) collective-permute-start(bf16[8,4096]{1,0:T(8,128)(2,1)} %tail.1), channel_id=1, source_target_pairs={{0,2},{2,4},{4,6},{6,8},{8,10},{10,12},{12,14},{14,16},{16,18},{18... | collective-permute-start | bytes 196616 | tf_op jit(solution)/shard_map/ppermute | solution.py:444
  7.4 1.6 %copy-start.1 = (bf16[256,4096]{1,0:T(8,128)(2,1)S(1)}, bf16[256,4096]{1,0:T(8,128)(2,1)}, u32[]{:S(2)}) copy-start(bf16[256,4096]{1,0:T(8,128)(2,1)} %refs_5_.1) | copy-start | bytes 6291460
  9.0 3.0 %copy-start.12 = (f32[32,16]{0,1:T(8,128)S(1)}, f32[32,16]{0,1:T(8,128)}, u32[]{:S(2)}) copy-start(f32[32,16]{0,1:T(8,128)} %param.14) | copy-start | bytes 6148
  13.4 17.4 %copy-start.5 = (bf16[256,512]{1,0:T(8,128)(2,1)}, bf16[256,512]{1,0:T(8,128)(2,1)S(1)}, u32[]{:S(2)}) copy-start(bf16[256,512]{1,0:T(8,128)(2,1)S(1)} %get-tuple-element.41.refs_3_.refs_4_) | copy-start | bytes 786436
  13.4 22.3 %copy-start.8 = (bf16[256,512]{1,0:T(8,128)(2,1)}, bf16[256,512]{1,0:T(8,128)(2,1)S(1)}, u32[]{:S(2)}) copy-start(bf16[256,512]{1,0:T(8,128)(2,1)S(1)} %get-tuple-element.45.refs_3_.refs_9_) | copy-start | bytes 786436
  13.4 29.2 %copy-start.19 = (f32[32,16]{0,1:T(8,128)S(1)}, f32[32,16]{0,1:T(8,128)}, u32[]{:S(2)}) copy-start(f32[32,16]{0,1:T(8,128)} %param.15) | copy-start | bytes 6148
  13.4 29.3 %copy-start.18 = (bf16[32,512]{1,0:T(8,128)(2,1)S(1)}, bf16[32,512]{1,0:T(8,128)(2,1)}, u32[]{:S(2)}) copy-start(bf16[32,512]{1,0:T(8,128)(2,1)} %param.13) | copy-start | bytes 98308
  13.5 5.0 %collective-permute-start.1 = (f32[16,2048]{1,0:T(8,128)S(1)}, f32[16,2048]{1,0:T(8,128)S(1)}, u32[]{:S(2)}, u32[]{:S(2)}) collective-permute-start(f32[16,2048]{1,0:T(8,128)S(1)} %slice_select_fusion.2), channel_id=1, source_target_pairs={{0,2},{2,0},{4,6},{6,4},{8,10},{10,8},{12,14},{14,12},{16,18},{18,... | collective-permute-start | bytes 393224 | tf_op jit(solution)/shard_map/ppermute | solution.py:463
  18.6 8.4 %collective-permute-start.2 = (f32[16,2048]{1,0:T(8,128)S(1)}, f32[16,2048]{1,0:T(8,128)S(1)}, u32[]{:S(2)}, u32[]{:S(2)}) collective-permute-start(f32[16,2048]{1,0:T(8,128)S(1)} %get-tuple-element.71), channel_id=1, source_target_pairs={{0,4},{2,6},{4,8},{6,10},{8,12},{10,14},{12,16},{14,18},{16,20},{1... | collective-permute-start | bytes 393224 | tf_op jit(solution)/shard_map/ppermute | solution.py:483
  22.0 8.5 %collective-permute-start.4 = (bf16[256,512]{1,0:T(8,128)(2,1)S(1)}, bf16[256,512]{1,0:T(8,128)(2,1)S(1)}, u32[]{:S(2)}, u32[]{:S(2)}) collective-permute-start(bf16[256,512]{1,0:T(8,128)(2,1)S(1)} %get-tuple-element.41.refs_3_.refs_4_), channel_id=1, source_target_pairs={{0,2},{2,0},{4,6},{6,4},{8,10},{10,8},{12,14},{14,12},{16,18},{18,... | collective-permute-start | bytes 786440 | tf_op jit(solution)/shard_map/ppermute | solution.py:482
  23.6 7.3 %collective-permute-start.6 = (bf16[256,512]{1,0:T(8,128)(2,1)S(1)}, bf16[256,512]{1,0:T(8,128)(2,1)S(1)}, u32[]{:S(2)}, u32[]{:S(2)}) collective-permute-start(bf16[256,512]{1,0:T(8,128)(2,1)S(1)} %get-tuple-element.45.refs_3_.refs_9_), channel_id=1, source_target_pairs={{0,4},{2,6},{4,8},{6,10},{8,12},{10,14},{12,16},{14,18},{16,20},{1... | collective-permute-start | bytes 786440 | tf_op jit(solution)/shard_map/ppermute | solution.py:481
  27.0 10.2 %copy-start.14 = (f32[16,2048]{1,0:T(8,128)}, f32[16,2048]{1,0:T(8,128)S(1)}, u32[]{:S(2)}) copy-start(f32[16,2048]{1,0:T(8,128)S(1)} %collective-permute-done.2) | copy-start | bytes 393220
  27.1 9.5 %collective-permute-start.3 = (f32[16,2048]{1,0:T(8,128)S(1)}, f32[16,2048]{1,0:T(8,128)S(1)}, u32[]{:S(2)}, u32[]{:S(2)}) collective-permute-start(f32[16,2048]{1,0:T(8,128)S(1)} %multiply_add_fusion.3), channel_id=1, source_target_pairs={{0,8},{2,10},{4,12},{6,14},{8,16},{10,18},{12,20},{14,22},{16,24},... | collective-permute-start | bytes 393224 | tf_op jit(solution)/shard_map/ppermute | solution.py:495
  30.9 24.1 %copy-start.10 = (bf16[256,512]{1,0:T(8,128)(2,1)}, bf16[256,512]{1,0:T(8,128)(2,1)S(1)}, u32[]{:S(2)}) copy-start(bf16[256,512]{1,0:T(8,128)(2,1)S(1)} %collective-permute-done.6.refs_7_.refs_1_) | copy-start | bytes 786436
  30.9 21.1 %collective-permute-start.7 = (bf16[256,1536]{1,0:T(8,128)(2,1)}, bf16[256,1536]{1,0:T(8,128)(2,1)S(1)}, u32[]{:S(2)}, u32[]{:S(2)}) collective-permute-start(bf16[256,1536]{1,0:T(8,128)(2,1)} %get-tuple-element.52.refs_4_.refs_10_), channel_id=1, source_target_pairs={{0,4},{2,6},{4,8},{6,10},{8,12},{10,14},{12,16},{14,18},{16,20},{1... | collective-permute-start | bytes 2359304 | tf_op jit(solution)/shard_map/ppermute | solution.py:486
  35.8 16.2 %copy-start.7 = (bf16[256,512]{1,0:T(8,128)(2,1)S(1)}, bf16[256,512]{1,0:T(8,128)(2,1)}, u32[]{:S(2)}) copy-start(bf16[256,512]{1,0:T(8,128)(2,1)} %copy-done.5) | copy-start | bytes 786436
  35.8 16.2 %collective-permute-start.5 = (bf16[256,1536]{1,0:T(8,128)(2,1)S(1)}, bf16[256,1536]{1,0:T(8,128)(2,1)}, u32[]{:S(2)}, u32[]{:S(2)}) collective-permute-start(bf16[256,1536]{1,0:T(8,128)(2,1)S(1)} %get-tuple-element.49.refs_4_.refs_5_), channel_id=1, source_target_pairs={{0,2},{2,0},{4,6},{6,4},{8,10},{10,8},{12,14},{14,12},{16,18},{18,... | collective-permute-start | bytes 2359304 | tf_op jit(solution)/shard_map/ppermute | solution.py:487
  36.6 10.9 %copy-start.9 = (bf16[256,512]{1,0:T(8,128)(2,1)S(1)}, bf16[256,512]{1,0:T(8,128)(2,1)}, u32[]{:S(2)}) copy-start(bf16[256,512]{1,0:T(8,128)(2,1)} %copy-done.8) | copy-start | bytes 786436
  36.6 6.1 %copy-start.16 = (f32[16,2048]{1,0:T(8,128)}, f32[16,2048]{1,0:T(8,128)S(1)}, u32[]{:S(2)}) copy-start(f32[16,2048]{1,0:T(8,128)S(1)} %collective-permute-done.3) | copy-start | bytes 393220
  37.2 17.7 %collective-permute-start.8 = (f32[16,2048]{1,0:T(8,128)}, f32[16,2048]{1,0:T(8,128)}, u32[]{:S(2)}, u32[]{:S(2)}) collective-permute-start(f32[16,2048]{1,0:T(8,128)} %multiply_add_fusion.2), channel_id=1, source_target_pairs={{0,16},{2,18},{4,20},{6,22},{8,24},{10,26},{12,28},{14,30},{1,17},... | collective-permute-start | bytes 393224 | tf_op jit(solution)/shard_map/ppermute | solution.py:495
  43.2 1.0 %copy-start.6 = (bf16[256,512]{1,0:T(8,128)(2,1)S(1)}, bf16[256,512]{1,0:T(8,128)(2,1)}, u32[]{:S(2)}) copy-start(bf16[256,512]{1,0:T(8,128)(2,1)} %copy-done.5) | copy-start | bytes 786436
  51.9 3.0 %copy-start.15 = (f32[16,2048]{1,0:T(8,128)S(1)}, f32[16,2048]{1,0:T(8,128)}, u32[]{:S(2)}) copy-start(f32[16,2048]{1,0:T(8,128)} %copy-done.14) | copy-start | bytes 393220
  52.0 3.0 %copy-start.17 = (f32[16,2048]{1,0:T(8,128)S(1)}, f32[16,2048]{1,0:T(8,128)}, u32[]{:S(2)}) copy-start(f32[16,2048]{1,0:T(8,128)} %copy-done.16) | copy-start | bytes 393220
  52.0 11.4 %copy-start.2 = (bf16[256,4096]{1,0:T(8,128)(2,1)S(1)}, bf16[256,4096]{1,0:T(8,128)(2,1)}, u32[]{:S(2)}) copy-start(bf16[256,4096]{1,0:T(8,128)(2,1)} %refs_4_.3) | copy-start | bytes 6291460
  56.0 6.4 %collective-permute-start.9 = (f32[16,2048]{1,0:T(8,128)S(1)}, f32[16,2048]{1,0:T(8,128)S(1)}, u32[]{:S(2)}, u32[]{:S(2)}) collective-permute-start(f32[16,2048]{1,0:T(8,128)S(1)} %get-tuple-element.57), channel_id=1, source_target_pairs={{0,2},{2,0},{4,6},{6,4},{8,10},{10,8},{12,14},{14,12},{16,18},{18,... | collective-permute-start | bytes 393224 | tf_op jit(solution)/shard_map/ppermute | solution.py:513
  56.4 22.5 %collective-permute-start.11 = (bf16[256,2048]{1,0:T(8,128)(2,1)S(1)}, bf16[256,2048]{1,0:T(8,128)(2,1)S(1)}, u32[]{:S(2)}, u32[]{:S(2)}) collective-permute-start(bf16[256,2048]{1,0:T(8,128)(2,1)S(1)} %get-tuple-element.62), channel_id=1, source_target_pairs={{0,4},{2,6},{4,8},{6,10},{8,12},{10,14},{12,16},{14,18},{16,20},{1... | collective-permute-start | bytes 3145736 | tf_op jit(solution)/shard_map/ppermute | solution.py:517
  62.4 20.5 %collective-permute-start.10 = (bf16[256,2048]{1,0:T(8,128)(2,1)S(1)}, bf16[256,2048]{1,0:T(8,128)(2,1)S(1)}, u32[]{:S(2)}, u32[]{:S(2)}) collective-permute-start(bf16[256,2048]{1,0:T(8,128)(2,1)S(1)} %get-tuple-element.58), channel_id=1, source_target_pairs={{0,2},{2,0},{4,6},{6,4},{8,10},{10,8},{12,14},{14,12},{16,18},{18,... | collective-permute-start | bytes 3145736 | tf_op jit(solution)/shard_map/ppermute | solution.py:516
  63.3 1.0 %copy-start.11 = (bf16[256,512]{1,0:T(8,128)(2,1)S(1)}, bf16[256,512]{1,0:T(8,128)(2,1)}, u32[]{:S(2)}) copy-start(bf16[256,512]{1,0:T(8,128)(2,1)} %copy-done.10) | copy-start | bytes 786436
  64.3 2.4 %copy-start.3 = (bf16[256,4096]{1,0:T(8,128)(2,1)S(1)}, bf16[256,4096]{1,0:T(8,128)(2,1)}, u32[]{:S(2)}) copy-start(bf16[256,4096]{1,0:T(8,128)(2,1)} %refs_6_.3) | copy-start | bytes 6291460
  82.9 4.7 %copy-start.13 = (f32[4096]{0:T(1024)S(1)}, f32[4096]{0:T(1024)}, u32[]{:S(2)}) copy-start(f32[4096]{0:T(1024)} %param.17) | copy-start | bytes 49156
